TPU v7x, 256 devices: a whole 4x4x8 slice. The times are simulated.
256 devices in a mesh: gx: 8 (over z), gy: 4 (over y), gz: 8 (over x, core).
Axes of the slice: x: 4, y: 4, z: 8, core: 2. Of those that a mesh axis runs over, the one named last changes fastest.
Arguments:
- distribution: bfloat16 [16, 32, 64, 12, 512], P('gx', 'gy', 'gz'), may hold values from 0.019897461 to 1
- block_ids: int32 [16, 32, 64, 12], P('gx', 'gy', 'gz'), may hold values from 0 to 215, as said below
- cell_counts: int32 [16, 32, 64], P('gx', 'gy', 'gz'), may hold values from 6 to 12
- owner: int32 [16, 32, 64], P('gx', 'gy', 'gz'), may hold values from 0 to 63, as said below
- restitution: bfloat16 [16, 32, 64], P('gx', 'gy', 'gz'), may hold values from 0.5 to 0.94921875
Outputs:
- moved_distribution: bfloat16 [4, 8192, 12, 512], P('gy', ('gx', 'gz'))
- moved_ids: int32 [4, 8192, 12], P('gy', ('gx', 'gz'))
- moved_counts: int32 [4, 8192], P('gy', ('gx', 'gz'))
Inputs may be any that keep to these rules, and one draw needn't show every extreme that they name: `block_ids`: the 12 numbers of one cell are distinct block numbers. `owner`: owner g means the device of the cell's gy row with gx index g // 8 and gz index g % 8. Each device sends exactly 2 of its cells to each of the 64 devices of its gy row (itself included), and each device owns exactly 128 cells afterwards.
All inputs are finite; a program needn't handle non-finite values.
Results may differ from a plain program's by a relative error of at most 0.001.
The roundings to bfloat16 on the way count: a program that leaves them out, or rounds other values in their place, can miss the bound.
Values may be sent and summed in bfloat16 or wider, within the bound.
No kernel may reach another device: no remote copies, remote signals or barrier semaphores. Data moves between devices by JAX's collectives and lax.ppermute only.
A program may use at most 64 MiB of HBM per device.

v0:
```python
import math

import jax
import jax.numpy as jnp
from jax import lax
from jax.sharding import PartitionSpec as P

NV1 = 48
BLK = 8
MAXB = 12


STEP_COEFF = 0.6
IMPACT_KIND = 0.02


def extended(value, sides, width):
    for axis, dim in sides:
        peers, length = (lax.axis_size(axis), value.shape[dim])
        up = [(i, (i + 1) % peers) for i in range(peers)]
        down = [(j, i) for i, j in up]
        last = lax.slice_in_dim(value, length - width, length, axis=dim)
        first = lax.slice_in_dim(value, 0, width, axis=dim)
        before = lax.ppermute(last, axis, up)
        after = lax.ppermute(first, axis, down)
        value = jnp.concatenate([before, value, after], axis=dim)
    return value


def inner_offsets():
    velocity_index = jnp.arange(BLK**3, dtype=jnp.int32)
    coords = jnp.stack(
        [velocity_index // (BLK * BLK), velocity_index // BLK % BLK, velocity_index % BLK]
    )
    return coords.astype(jnp.float32) - (BLK - 1) / 2.0


def block_centers(ids):
    blocks_edge = NV1 // BLK
    coords = jnp.stack(
        [ids // (blocks_edge * blocks_edge), ids // blocks_edge % blocks_edge, ids % blocks_edge]
    )
    return coords.astype(jnp.float32) * BLK + (BLK - 1) / 2.0 - (NV1 - 1) / 2.0


def neighbor_values(own_ids, other_ids, other_values):
    matches = (
        (own_ids[..., :, None] == other_ids[..., None, :]) & (own_ids[..., :, None] >= 0)
    ).astype(jnp.bfloat16)
    return jnp.einsum(
        "abcst,abctj->abcsj", matches, other_values, preferred_element_type=jnp.float32
    )


def relax(read, raw_ids, live_mask, coefficient):
    inner_offset = inner_offsets()
    centers = block_centers(raw_ids)
    tile_span = inner_offset.shape[1]
    squares = jnp.sum(inner_offset * inner_offset, axis=0)
    weights_table = jnp.concatenate(
        [jnp.ones((1, tile_span), jnp.float32), inner_offset, squares[None]], axis=0
    ).T.astype(jnp.bfloat16)
    leading = read.shape[:-1]
    block_sums = jnp.dot(
        read.reshape(-1, tile_span), weights_table, preferred_element_type=jnp.float32
    ).reshape(leading + (5,))
    block_mass = block_sums[..., 0]
    particle_count_field = jnp.sum(block_mass, axis=-1)
    momentum = [
        jnp.sum(block_mass * centers[k] + block_sums[..., 1 + k], axis=-1) for k in range(3)
    ]
    center_sq = centers[0] * centers[0] + centers[1] * centers[1] + centers[2] * centers[2]
    cross = (
        centers[0] * block_sums[..., 1]
        + centers[1] * block_sums[..., 2]
        + centers[2] * block_sums[..., 3]
    )
    motion_work_sum = jnp.sum(block_mass * center_sq + 2.0 * cross + block_sums[..., 4], axis=-1)
    average_drift = [momentum[k] / particle_count_field for k in range(3)]
    thermal_spread = (
        motion_work_sum / particle_count_field
        - (
            average_drift[0] * average_drift[0]
            + average_drift[1] * average_drift[1]
            + average_drift[2] * average_drift[2]
        )
    ) / 3.0
    return_parcels_home = coefficient.astype(jnp.float32)
    destination_holder = (
        thermal_spread * (1.0 + return_parcels_home) * (1.0 + return_parcels_home) / 4.0
    )
    equilibration_frequency = 1.0 - jnp.exp(
        -IMPACT_KIND * (particle_count_field / tile_span) * jnp.sqrt(thermal_spread)
    )
    distance = jnp.zeros(read.shape, jnp.float32)
    for k in range(3):
        offset_k = centers[k][..., None] + inner_offset[k] - average_drift[k][..., None, None]
        distance = distance + offset_k * offset_k
    scale = particle_count_field / (2.0 * math.pi * destination_holder) ** 1.5
    maxwellian = scale[..., None, None] * jnp.exp(
        -distance / (2.0 * destination_holder[..., None, None])
    )
    stream_vals = read.astype(jnp.float32)
    relaxed = (
        stream_vals + equilibration_frequency[..., None, None] * (maxwellian - stream_vals)
    ) * live_mask[..., None]
    return relaxed.astype(jnp.bfloat16)


def carry_cells(outgoing, metadata):
    return (
        lax.all_to_all(outgoing, ("gx", "gz"), split_axis=0, concat_axis=0, tiled=True),
        lax.all_to_all(metadata, ("gx", "gz"), split_axis=0, concat_axis=0, tiled=True),
    )


def on_device(distribution, block_ids, cell_counts, owner, restitution):
    size_x, size_y, size_z = cell_counts.shape
    slot_index = jnp.arange(MAXB, dtype=jnp.int32)
    live = slot_index < cell_counts[..., None]
    listed = jnp.where(live, block_ids, -1)
    padded = extended(distribution, (("gx", 0), ("gy", 1), ("gz", 2)), 1)
    padded_ids = extended(listed, (("gx", 0), ("gy", 1), ("gz", 2)), 1)
    neighbours = [
        (
            padded[:-2, 1:-1, 1:-1],
            padded_ids[:-2, 1:-1, 1:-1],
            padded[2:, 1:-1, 1:-1],
            padded_ids[2:, 1:-1, 1:-1],
        ),
        (
            padded[1:-1, :-2, 1:-1],
            padded_ids[1:-1, :-2, 1:-1],
            padded[1:-1, 2:, 1:-1],
            padded_ids[1:-1, 2:, 1:-1],
        ),
        (
            padded[1:-1, 1:-1, :-2],
            padded_ids[1:-1, 1:-1, :-2],
            padded[1:-1, 1:-1, 2:],
            padded_ids[1:-1, 1:-1, 2:],
        ),
    ]
    inner_offset = inner_offsets()
    centers = block_centers(block_ids)
    center_value = distribution.astype(jnp.float32)
    flux_sum = jnp.zeros(center_value.shape, jnp.float32)
    lam = STEP_COEFF / (NV1 - 1)
    for direction in range(3):
        lower_vals, lower_ids, upper_vals, upper_ids = neighbours[direction]
        velocity = centers[direction][..., None] + inner_offset[direction]
        from_lower = neighbor_values(listed, lower_ids, lower_vals)
        from_upper = neighbor_values(listed, upper_ids, upper_vals)
        flux_sum = (
            flux_sum
            + jnp.maximum(velocity, 0.0) * (center_value - from_lower)
            + jnp.minimum(velocity, 0.0) * (from_upper - center_value)
        )
    live_mask = live.astype(jnp.float32)
    read = ((center_value - lam * flux_sum) * live_mask[..., None]).astype(jnp.bfloat16)
    cell_total = size_x * size_y * size_z
    count_x = lax.axis_size("gx")
    count_z = lax.axis_size("gz")
    group_size = count_x * count_z
    capacity = cell_total // group_size
    id_columns = block_ids.reshape(cell_total, MAXB).astype(jnp.bfloat16)
    count_column = cell_counts.reshape(cell_total, 1).astype(jnp.bfloat16)
    payload = relax(read, block_ids, live_mask, restitution)
    metadata = jnp.concatenate([id_columns, count_column], axis=1)
    payload_rows = payload.reshape(cell_total, -1)
    row_width = payload_rows.shape[1]
    owners = owner.reshape(cell_total)
    onehot = (owners[:, None] == jnp.arange(group_size, dtype=jnp.int32)[None, :]).astype(jnp.int32)
    rank_within = jnp.sum((jnp.cumsum(onehot, axis=0) - onehot) * onehot, axis=1)
    positions = owners * capacity + rank_within
    outgoing = (
        jnp.zeros((group_size * capacity, row_width), jnp.bfloat16).at[positions].set(payload_rows)
    )
    outgoing_meta = (
        jnp.zeros((group_size * capacity, metadata.shape[1]), jnp.bfloat16)
        .at[positions]
        .set(metadata)
    )
    received, received_meta = carry_cells(outgoing, outgoing_meta)
    valid_slot = received_meta[:, MAXB] > 0
    targets = jnp.where(valid_slot, jnp.cumsum(valid_slot.astype(jnp.int32)) - 1, cell_total)
    placed = jnp.zeros((cell_total, row_width), jnp.bfloat16).at[targets].set(received, mode="drop")
    placed_meta = (
        jnp.zeros((cell_total, received_meta.shape[1]), jnp.bfloat16)
        .at[targets]
        .set(received_meta, mode="drop")
    )
    moved_ids = placed_meta[:, :MAXB].astype(jnp.int32)
    moved_counts = placed_meta[:, MAXB].astype(jnp.int32)
    placed_cells = placed.reshape(cell_total, MAXB, -1)
    return (
        placed_cells.reshape(1, cell_total, MAXB, -1),
        moved_ids.reshape(1, cell_total, MAXB),
        moved_counts.reshape(1, cell_total),
    )


def solution(mesh):
    placed = (
        P("gx", "gy", "gz", None, None),
        P("gx", "gy", "gz", None),
        P("gx", "gy", "gz"),
        P("gx", "gy", "gz"),
        P("gx", "gy", "gz"),
    )
    return jax.shard_map(
        on_device,
        mesh=mesh,
        in_specs=placed,
        out_specs=(
            P("gy", ("gx", "gz"), None, None),
            P("gy", ("gx", "gz"), None),
            P("gy", ("gx", "gz")),
        ),
        check_vma=False,
    )
```

profile of v0, /device:TPU:1, one launch (start us, length us, event | category | flops | bytes accessed | tf_op | source)
XLA Modules:
  0.0 149.9 jit_solution(6939328425389893196)
XLA Ops:
  1.6 2.5 %collective-permute-start = (s32[1,8,8,12]{3,2,1,0:T(8,128)S(1)}, s32[1,8,8,12]{3,2,1,0:T(8,128)S(1)}, u32[]{:S(2)}, u32[]{:S(2)}) collective-permute-start(s32[1,8,8,12]{3,2,1,0:T(8,128)S(1)} %get-tuple-element.57), channel_id=1, source_target_pairs={{0,32},{32,64},{64,96},{96,128},{128,160},{160,192},{192,224},{224... | collective-permute-start | bytes 9224 | tf_op jit(solution)/shard_map/ppermute | solution.py:24
  4.1 4.0 %collective-permute-start.2 = (s32[1,8,8,12]{3,2,1,0:T(8,128)S(1)}, s32[1,8,8,12]{3,2,1,0:T(8,128)S(1)}, u32[]{:S(2)}, u32[]{:S(2)}) collective-permute-start(s32[1,8,8,12]{3,2,1,0:T(8,128)S(1)} %get-tuple-element.58), channel_id=1, source_target_pairs={{32,0},{64,32},{96,64},{128,96},{160,128},{192,160},{224,192},{0,2... | collective-permute-start | bytes 9224 | tf_op jit(solution)/shard_map/ppermute | solution.py:25
  12.5 1.4 scatter_custom_fusion
  13.9 9.7 %all-to-all-start = ((bf16[64,2,13]{2,1,0:T(2,128)(2,1)}), bf16[64,2,13]{2,1,0:T(2,128)(2,1)S(1)}, u32[]{:S(2)}, u32[]{:S(2)}) async-start(bf16[64,2,13]{2,1,0:T(2,128)(2,1)} %bitcast.2), calls=%async_computation | async-start | bytes 65536 | tf_op jit(solution)/shard_map/all_to_all | solution.py:113
  23.7 1.5 fusion.106
  25.1 2.9 %collective-permute-start.3 = (bf16[1,8,8,12,512]{4,2,3,1,0:T(8,128)(2,1)S(1)}, bf16[1,8,8,12,512]{4,2,3,1,0:T(8,128)(2,1)S(1)}, u32[]{:S(2)}, u32[]{:S(2)}) collective-permute-start(bf16[1,8,8,12,512]{4,2,3,1,0:T(8,128)(2,1)S(1)} %get-tuple-element.29), channel_id=1, source_target_pairs={{32,0},{64,32},{96,64},{128,96},{160,128},{192,160},{224,192},{0,2... | collective-permute-start | bytes 2359304 | tf_op jit(solution)/shard_map/ppermute | solution.py:25
  28.2 1.4 collective-permute-start.4
  29.6 1.5 %collective-permute-start.6 = (s32[4,1,8,12]{3,2,1,0:T(8,128)S(1)}, s32[4,1,8,12]{3,2,1,0:T(8,128)S(1)}, u32[]{:S(2)}, u32[]{:S(2)}) collective-permute-start(s32[4,1,8,12]{3,2,1,0:T(8,128)S(1)} %get-tuple-element.49), channel_id=1, source_target_pairs={{8,0},{16,8},{24,16},{0,24},{9,1},{17,9},{25,17},{1,25},{10,2},{18... | collective-permute-start | bytes 4616 | tf_op jit(solution)/shard_map/ppermute | solution.py:25
  31.1 1.3 collective-permute-done.4
  32.5 1.8 %collective-permute-start.10 = (s32[4,10,1,12]{3,2,1,0:T(1,128)S(1)}, s32[4,10,1,12]{3,2,1,0:T(1,128)S(1)}, u32[]{:S(2)}, u32[]{:S(2)}) collective-permute-start(s32[4,10,1,12]{3,2,1,0:T(1,128)S(1)} %get-tuple-element.45), channel_id=1, source_target_pairs={{1,0},{2,1},{3,2},{4,3},{5,4},{6,5},{7,6},{0,7},{9,8},{10,9},{11,1... | collective-permute-start | bytes 5768 | tf_op jit(solution)/shard_map/ppermute | solution.py:25
  35.4 1.7 %collective-permute-done.10 = s32[4,10,1,12]{3,2,1,0:T(1,128)S(1)} collective-permute-done((s32[4,10,1,12]{3,2,1,0:T(1,128)S(1)}, s32[4,10,1,12]{3,2,1,0:T(1,128)S(1)}, u32[]{:S(2)}, u32[]{:S(2)}) %collective-permute-start.10) | collective-permute-done | bytes 1952 | tf_op jit(solution)/shard_map/ppermute | solution.py:25
  37.2 10.5 %collective-permute-done.1 = bf16[1,8,8,12,512]{4,2,3,1,0:T(8,128)(2,1)S(1)} collective-permute-done((bf16[1,8,8,12,512]{4,2,3,1,0:T(8,128)(2,1)S(1)}, bf16[1,8,8,12,512]{4,2,3,1,0:T(8,128)(2,1)S(1)}, u32[]{:S(2)}, u32[]{:S(2)}) %collective-permute-start.1) | collective-permute-done | bytes 786464 | tf_op jit(solution)/shard_map/ppermute | solution.py:24
  49.2 1.4 collective-permute-start.5
  50.6 1.7 %collective-permute-start.7 = (bf16[4,1,8,12,512]{4,3,2,1,0:T(8,128)(2,1)S(1)}, bf16[4,1,8,12,512]{4,3,2,1,0:T(8,128)(2,1)S(1)}, u32[]{:S(2)}, u32[]{:S(2)}) collective-permute-start(bf16[4,1,8,12,512]{4,3,2,1,0:T(8,128)(2,1)S(1)} %get-tuple-element.26), channel_id=1, source_target_pairs={{8,0},{16,8},{24,16},{0,24},{9,1},{17,9},{25,17},{1,25},{10,2},{18... | collective-permute-start | bytes 1179656 | tf_op jit(solution)/shard_map/ppermute | solution.py:25
  52.3 2.3 %fusion.31 = f32[2,8,8,12,512]{4,3,2,1,0:T(8,128)S(1)} fusion(bf16[1,8,8,12,512]{4,3,2,1,0:T(8,128)(2,1)S(1)} %get-tuple-element.33, bf16[2,8,8,12,512]{4,3,2,1,0:T(8,128)(2,1)S(1)} %get-tuple-element.27, s32[2,8,8,12]{3,2,1,0:T(8,128)S(1)} %get-tuple-element.51, s32[2,8,8,12]{3,2,1,0:T(8,128)S(1)} %get-tuple-element.22, ...), kind=kOutput, calls=%fused_computation.63 | convolution fusion | flops 19697664 | bytes 5518848 | tf_op jit(solution)/shard_map/abcst,abctj->abcsj/dot_general | solution.py:50
  54.6 2.3 %fusion.33 = f32[2,8,8,12,512]{4,3,2,1,0:T(8,128)S(1)} fusion(bf16[2,8,8,12,512]{4,3,2,1,0:T(8,128)(2,1)S(1)} %get-tuple-element.27, bf16[1,8,8,12,512]{4,3,2,1,0:T(8,128)(2,1)S(1)} %get-tuple-element.31, s32[2,8,8,12]{3,2,1,0:T(8,128)S(1)} %get-tuple-element.50, s32[2,8,8,12]{3,2,1,0:T(8,128)S(1)} %get-tuple-element.22, ...), kind=kOutput, calls=%fused_computation.66 | convolution fusion | flops 19697664 | bytes 5518848 | tf_op jit(solution)/shard_map/abcst,abctj->abcsj/dot_general | solution.py:50
  56.8 5.7 %collective-permute-done.5 = bf16[4,1,8,12,512]{4,3,2,1,0:T(8,128)(2,1)S(1)} collective-permute-done((bf16[4,1,8,12,512]{4,3,2,1,0:T(8,128)(2,1)S(1)}, bf16[4,1,8,12,512]{4,3,2,1,0:T(8,128)(2,1)S(1)}, u32[]{:S(2)}, u32[]{:S(2)}) %collective-permute-start.5) | collective-permute-done | bytes 393248 | tf_op jit(solution)/shard_map/ppermute | solution.py:24
  63.6 3.4 %collective-permute-start.9 = (bf16[4,10,1,12,512]{4,0,3,2,1:T(4,128)(2,1)S(1)}, bf16[4,10,1,12,512]{4,0,3,2,1:T(4,128)(2,1)S(1)}, u32[]{:S(2)}, u32[]{:S(2)}) collective-permute-start(bf16[4,10,1,12,512]{4,0,3,2,1:T(4,128)(2,1)S(1)} %copy.67), channel_id=1, source_target_pairs={{0,1},{1,2},{2,3},{3,4},{4,5},{5,6},{6,7},{7,0},{8,9},{9,10},{10,1... | collective-permute-start | bytes 1474568 | tf_op jit(solution)/shard_map/ppermute | solution.py:24
  67.0 2.3 %fusion.27 = f32[2,8,8,12,512]{4,3,2,1,0:T(8,128)S(1)} fusion(bf16[4,1,8,12,512]{4,3,2,1,0:T(8,128)(2,1)S(1)} %collective-permute-done.7, bf16[4,8,8,12,512]{4,3,2,1,0:T(8,128)(2,1)S(1)} %get-tuple-element.34, s32[2,8,8,12]{3,2,1,0:T(8,128)S(1)} %get-tuple-element.52, s32[2,8,8,12]{3,2,1,0:T(8,128)S(1)} %get-tuple-element.22, ...), kind=kOutput, calls=%fused_computation.57 | convolution fusion | flops 19697664 | bytes 6698496 | tf_op jit(solution)/shard_map/abcst,abctj->abcsj/dot_general | solution.py:50
  69.3 2.3 %fusion.29 = f32[2,8,8,12,512]{4,3,2,1,0:T(8,128)S(1)} fusion(bf16[4,8,8,12,512]{4,3,2,1,0:T(8,128)(2,1)S(1)} %get-tuple-element.34, bf16[4,1,8,12,512]{4,3,2,1,0:T(8,128)(2,1)S(1)} %collective-permute-done.5, s32[2,8,8,12]{3,2,1,0:T(8,128)S(1)} %get-tuple-element.47, s32[2,8,8,12]{3,2,1,0:T(8,128)S(1)} %get-tuple-element.22, ...), kind=kOutput, calls=%fused_computation.60 | convolution fusion | flops 19697664 | bytes 6698496 | tf_op jit(solution)/shard_map/abcst,abctj->abcsj/dot_general | solution.py:50
  71.6 1.2 collective-permute-done.9
  72.9 2.4 %collective-permute-done.11 = bf16[4,10,1,12,512]{4,0,3,2,1:T(4,128)(2,1)S(1)} collective-permute-done((bf16[4,10,1,12,512]{4,0,3,2,1:T(4,128)(2,1)S(1)}, bf16[4,10,1,12,512]{4,0,3,2,1:T(4,128)(2,1)S(1)}, u32[]{:S(2)}, u32[]{:S(2)}) %collective-permute-start.11) | collective-permute-done | bytes 491552 | tf_op jit(solution)/shard_map/ppermute | solution.py:25
  75.4 1.5 %fusion.25 = f32[2,8,8,12,512]{4,3,2,1,0:T(8,128)S(1)} fusion(bf16[4,10,1,12,512]{4,3,2,1,0:T(8,128)(2,1)S(1)} %copy.68, bf16[4,1,8,12,512]{4,3,2,1,0:T(8,128)(2,1)S(1)} %collective-permute-done.7, bf16[4,8,8,12,512]{4,3,2,1,0:T(8,128)(2,1)S(1)} %get-tuple-element.34, bf16[4,1,8,12,512]{4,3,2,1,0:T(8,128)(2,1)S(1)} %collective-permute-done.5, ...), kind=kOutput, calls=%fused_computation.52 | convolution fusion | flops 21270528 | bytes 7583232 | tf_op jit(solution)/shard_map/abcst,abctj->abcsj/dot_general | solution.py:50
  77.0 7.1 %multiply_convert_fusion = bf16[2,8,8,12,512]{4,3,2,1,0:T(8,128)(2,1)S(1)} fusion(f32[2,8,8,12,512]{4,3,2,1,0:T(8,128)S(1)} %fusion.25, f32[2,8,8,12,512]{4,3,2,1,0:T(8,128)S(1)} %fusion.27, f32[2,8,8,12,512]{4,3,2,1,0:T(8,128)S(1)} %fusion.29, f32[2,8,8,12,512]{4,3,2,1,0:T(8,128)S(1)} %fusion.31, f32[2,8,8,12,512]{4,3,2,1,0:T(8,128)S(1)} %fusion.33, ...), kind=kOutput, calls=%fused_computation.46 | convolution fusion | flops 45649920 | bytes 23342592 | tf_op jit(solution)/shard_map/abcst,abctj->abcsj/dot_general | solution.py:50
  84.1 2.6 %fusion.87 = f32[2,8,8,12,5]{3,4,2,1,0:T(8,128)S(1)} fusion(bf16[2,8,8,12,512]{4,3,2,1,0:T(8,128)(2,1)S(1)} %multiply_convert_fusion, bf16[1,512]{1,0:T(2,128)(2,1)S(1)} %broadcast_in_dim.9, bf16[3,512]{1,0:T(4,128)(2,1)S(1)} %get-tuple-element.65, bf16[5]{0:T(256)(128)(2,1)S(1)} %pad.clone), kind=kOutput, calls=%fused_computation.181 | convolution fusion | flops 7879680 | bytes 1607690 | tf_op jit(solution)/shard_map/dot_general | solution.py:64
  87.2 3.9 %fusion.2 = bf16[2,8,8,12,512]{4,3,2,1,0:T(8,128)(2,1)S(1)} fusion(bf16[2,8,8,12,512]{4,3,2,1,0:T(8,128)(2,1)S(1)} %multiply_convert_fusion, f32[2,8,8]{2,1,0:T(8,128)S(1)} %get-tuple-element.60, f32[2,8,8]{2,1,0:T(8,128)S(1)} %get-tuple-element.20, f32[2,8,8]{2,1,0:T(8,128)S(1)} %get-tuple-element.19, f32[2,8,8]{2,1,0:T(8,128)S(1)} %get-tuple-element.18, ...), kind=kLoop, calls=%fused_computation.24 | loop fusion | flops 15728640 | bytes 3179520 | tf_op jit(solution)/shard_map/convert_element_type | solution.py:107
  92.2 3.1 %scatter_custom_fusion.1 = bf16[128,6144]{1,0:T(8,128)(2,1)S(1)} fusion(s32[128]{0:T(128)S(1)} %fusion.75, bf16[128,6144]{1,0:T(8,128)(2,1)S(1)} %bitcast.67, bf16[]{:T(256)} %constant.132.clone.1), kind=kCustom, calls=%fused_computation.82 | custom fusion | bytes 1572866 | tf_op jit(solution)/shard_map/scatter | solution.py:177
  95.3 1.9 %all_to_all.19 = bf16[64,2,6144]{2,1,0:T(2,128)(2,1)} reshape(bf16[128,6144]{1,0:T(8,128)(2,1)S(1)} %scatter_custom_fusion.1) | data formatting | bytes 3145728 | tf_op jit(solution)/shard_map/all_to_all | solution.py:112
  97.2 7.4 %all-to-all-start.1 = ((bf16[64,2,6144]{2,1,0:T(2,128)(2,1)}), bf16[64,2,6144]{2,1,0:T(2,128)(2,1)S(1)}, u32[]{:S(2)}, u32[]{:S(2)}) async-start(bf16[64,2,6144]{2,1,0:T(2,128)(2,1)} %all_to_all.19), calls=%async_computation.1 | async-start | bytes 3145728 | tf_op jit(solution)/shard_map/all_to_all | solution.py:112
  107.6 36.1 %all-to-all-done.1 = bf16[64,2,6144]{2,1,0:T(2,128)(2,1)S(1)} async-done(((bf16[64,2,6144]{2,1,0:T(2,128)(2,1)}), bf16[64,2,6144]{2,1,0:T(2,128)(2,1)S(1)}, u32[]{:S(2)}, u32[]{:S(2)}) %all-to-all-start.1) | async-done | bytes 1572896 | tf_op jit(solution)/shard_map/all_to_all | solution.py:112
  144.3 3.1 %scatter_custom_fusion.2 = bf16[128,6144]{1,0:T(8,128)(2,1)S(1)} fusion(s32[128]{0:T(128)S(1)} %fusion.76, bf16[128,6144]{1,0:T(8,128)(2,1)S(1)} %reshape.285, bf16[]{:T(256)} %constant.132.clone.1), kind=kCustom, calls=%fused_computation.80 | custom fusion | bytes 1572866 | tf_op jit(solution)/shard_map/scatter | solution.py:187
  148.3 1.6 %copy.76 = bf16[1,128,12,512]{3,1,2,0:T(8,128)(2,1)} copy(bf16[1,128,12,512]{1,3,2,0:T(8,128)(2,1)S(1)} %bitcast.66) | data formatting | bytes 3145728
  (68 shorter events, 15.3 us)
Async XLA Ops:
  1.6 26.6 %collective-permute-start = (s32[1,8,8,12]{3,2,1,0:T(8,128)S(1)}, s32[1,8,8,12]{3,2,1,0:T(8,128)S(1)}, u32[]{:S(2)}, u32[]{:S(2)}) collective-permute-start(s32[1,8,8,12]{3,2,1,0:T(8,128)S(1)} %get-tuple-element.57), channel_id=1, source_target_pairs={{0,32},{32,64},{64,96},{96,128},{128,160},{160,192},{192,224},{224... | collective-permute-start | bytes 9224 | tf_op jit(solution)/shard_map/ppermute | solution.py:24
  4.1 24.1 %collective-permute-start.2 = (s32[1,8,8,12]{3,2,1,0:T(8,128)S(1)}, s32[1,8,8,12]{3,2,1,0:T(8,128)S(1)}, u32[]{:S(2)}, u32[]{:S(2)}) collective-permute-start(s32[1,8,8,12]{3,2,1,0:T(8,128)S(1)} %get-tuple-element.58), channel_id=1, source_target_pairs={{32,0},{64,32},{96,64},{128,96},{160,128},{192,160},{224,192},{0,2... | collective-permute-start | bytes 9224 | tf_op jit(solution)/shard_map/ppermute | solution.py:25
  12.0 36.0 %copy-start = (bf16[2,8,8,12,512]{4,2,3,1,0:T(8,128)(2,1)S(1)}, bf16[2,8,8,12,512]{4,2,3,1,0:T(8,128)(2,1)}, u32[]{:S(2)}) copy-start(bf16[2,8,8,12,512]{4,2,3,1,0:T(8,128)(2,1)} %param.5) | copy-start | bytes 4718596
  13.9 83.3 %all-to-all-start = ((bf16[64,2,13]{2,1,0:T(2,128)(2,1)}), bf16[64,2,13]{2,1,0:T(2,128)(2,1)S(1)}, u32[]{:S(2)}, u32[]{:S(2)}) async-start(bf16[64,2,13]{2,1,0:T(2,128)(2,1)} %bitcast.2), calls=%async_computation | async-start | bytes 65536 | tf_op jit(solution)/shard_map/all_to_all | solution.py:113
  25.1 23.6 %collective-permute-start.3 = (bf16[1,8,8,12,512]{4,2,3,1,0:T(8,128)(2,1)S(1)}, bf16[1,8,8,12,512]{4,2,3,1,0:T(8,128)(2,1)S(1)}, u32[]{:S(2)}, u32[]{:S(2)}) collective-permute-start(bf16[1,8,8,12,512]{4,2,3,1,0:T(8,128)(2,1)S(1)} %get-tuple-element.29), channel_id=1, source_target_pairs={{32,0},{64,32},{96,64},{128,96},{160,128},{192,160},{224,192},{0,2... | collective-permute-start | bytes 2359304 | tf_op jit(solution)/shard_map/ppermute | solution.py:25
  28.0 19.6 %collective-permute-start.1 = (bf16[1,8,8,12,512]{4,2,3,1,0:T(8,128)(2,1)S(1)}, bf16[1,8,8,12,512]{4,2,3,1,0:T(8,128)(2,1)S(1)}, u32[]{:S(2)}, u32[]{:S(2)}) collective-permute-start(bf16[1,8,8,12,512]{4,2,3,1,0:T(8,128)(2,1)S(1)} %get-tuple-element.30), channel_id=1, source_target_pairs={{0,32},{32,64},{64,96},{96,128},{128,160},{160,192},{192,224},{224... | collective-permute-start | bytes 2359304 | tf_op jit(solution)/shard_map/ppermute | solution.py:24
  28.2 4.2 %collective-permute-start.4 = (s32[4,1,8,12]{3,2,1,0:T(8,128)S(1)}, s32[4,1,8,12]{3,2,1,0:T(8,128)S(1)}, u32[]{:S(2)}, u32[]{:S(2)}) collective-permute-start(s32[4,1,8,12]{3,2,1,0:T(8,128)S(1)} %get-tuple-element.48), channel_id=1, source_target_pairs={{0,8},{8,16},{16,24},{24,0},{1,9},{9,17},{17,25},{25,1},{2,10},{10... | collective-permute-start | bytes 4616 | tf_op jit(solution)/shard_map/ppermute | solution.py:24
  29.6 2.9 %collective-permute-start.6 = (s32[4,1,8,12]{3,2,1,0:T(8,128)S(1)}, s32[4,1,8,12]{3,2,1,0:T(8,128)S(1)}, u32[]{:S(2)}, u32[]{:S(2)}) collective-permute-start(s32[4,1,8,12]{3,2,1,0:T(8,128)S(1)} %get-tuple-element.49), channel_id=1, source_target_pairs={{8,0},{16,8},{24,16},{0,24},{9,1},{17,9},{25,17},{1,25},{10,2},{18... | collective-permute-start | bytes 4616 | tf_op jit(solution)/shard_map/ppermute | solution.py:25
  32.5 4.7 %collective-permute-start.10 = (s32[4,10,1,12]{3,2,1,0:T(1,128)S(1)}, s32[4,10,1,12]{3,2,1,0:T(1,128)S(1)}, u32[]{:S(2)}, u32[]{:S(2)}) collective-permute-start(s32[4,10,1,12]{3,2,1,0:T(1,128)S(1)} %get-tuple-element.45), channel_id=1, source_target_pairs={{1,0},{2,1},{3,2},{4,3},{5,4},{6,5},{7,6},{0,7},{9,8},{10,9},{11,1... | collective-permute-start | bytes 5768 | tf_op jit(solution)/shard_map/ppermute | solution.py:25
  34.3 2.8 %collective-permute-start.8 = (s32[4,10,1,12]{3,2,1,0:T(1,128)S(1)}, s32[4,10,1,12]{3,2,1,0:T(1,128)S(1)}, u32[]{:S(2)}, u32[]{:S(2)}) collective-permute-start(s32[4,10,1,12]{3,2,1,0:T(1,128)S(1)} %get-tuple-element.46), channel_id=1, source_target_pairs={{0,1},{1,2},{2,3},{3,4},{4,5},{5,6},{6,7},{7,0},{8,9},{9,10},{10,1... | collective-permute-start | bytes 5768 | tf_op jit(solution)/shard_map/ppermute | solution.py:24
  49.2 13.4 %collective-permute-start.5 = (bf16[4,1,8,12,512]{4,3,2,1,0:T(8,128)(2,1)S(1)}, bf16[4,1,8,12,512]{4,3,2,1,0:T(8,128)(2,1)S(1)}, u32[]{:S(2)}, u32[]{:S(2)}) collective-permute-start(bf16[4,1,8,12,512]{4,3,2,1,0:T(8,128)(2,1)S(1)} %get-tuple-element.25), channel_id=1, source_target_pairs={{0,8},{8,16},{16,24},{24,0},{1,9},{9,17},{17,25},{25,1},{2,10},{10... | collective-permute-start | bytes 1179656 | tf_op jit(solution)/shard_map/ppermute | solution.py:24
  50.6 12.0 %collective-permute-start.7 = (bf16[4,1,8,12,512]{4,3,2,1,0:T(8,128)(2,1)S(1)}, bf16[4,1,8,12,512]{4,3,2,1,0:T(8,128)(2,1)S(1)}, u32[]{:S(2)}, u32[]{:S(2)}) collective-permute-start(bf16[4,1,8,12,512]{4,3,2,1,0:T(8,128)(2,1)S(1)} %get-tuple-element.26), channel_id=1, source_target_pairs={{8,0},{16,8},{24,16},{0,24},{9,1},{17,9},{25,17},{1,25},{10,2},{18... | collective-permute-start | bytes 1179656 | tf_op jit(solution)/shard_map/ppermute | solution.py:25
  63.6 9.2 %collective-permute-start.9 = (bf16[4,10,1,12,512]{4,0,3,2,1:T(4,128)(2,1)S(1)}, bf16[4,10,1,12,512]{4,0,3,2,1:T(4,128)(2,1)S(1)}, u32[]{:S(2)}, u32[]{:S(2)}) collective-permute-start(bf16[4,10,1,12,512]{4,0,3,2,1:T(4,128)(2,1)S(1)} %copy.67), channel_id=1, source_target_pairs={{0,1},{1,2},{2,3},{3,4},{4,5},{5,6},{6,7},{7,0},{8,9},{9,10},{10,1... | collective-permute-start | bytes 1474568 | tf_op jit(solution)/shard_map/ppermute | solution.py:24
  67.0 8.3 %collective-permute-start.11 = (bf16[4,10,1,12,512]{4,0,3,2,1:T(4,128)(2,1)S(1)}, bf16[4,10,1,12,512]{4,0,3,2,1:T(4,128)(2,1)S(1)}, u32[]{:S(2)}, u32[]{:S(2)}) collective-permute-start(bf16[4,10,1,12,512]{4,0,3,2,1:T(4,128)(2,1)S(1)} %copy.69), channel_id=1, source_target_pairs={{1,0},{2,1},{3,2},{4,3},{5,4},{6,5},{7,6},{0,7},{9,8},{10,9},{11,1... | collective-permute-start | bytes 1474568 | tf_op jit(solution)/shard_map/ppermute | solution.py:25
  75.4 1.5 %copy-start.1 = (bf16[2,8,8,12,512]{4,2,3,1,0:T(8,128)(2,1)S(1)}, bf16[2,8,8,12,512]{4,2,3,1,0:T(8,128)(2,1)}, u32[]{:S(2)}) copy-start(bf16[2,8,8,12,512]{4,2,3,1,0:T(8,128)(2,1)} %param.5) | copy-start | bytes 4718596
  76.9 10.2 %copy-start.2 = (bf16[2,8,8]{2,1,0:T(8,128)(2,1)S(1)}, bf16[2,8,8]{2,1,0:T(8,128)(2,1)}, u32[]{:S(2)}) copy-start(bf16[2,8,8]{2,1,0:T(8,128)(2,1)} %param.9) | copy-start | bytes 772
  97.2 46.5 %all-to-all-start.1 = ((bf16[64,2,6144]{2,1,0:T(2,128)(2,1)}), bf16[64,2,6144]{2,1,0:T(2,128)(2,1)S(1)}, u32[]{:S(2)}, u32[]{:S(2)}) async-start(bf16[64,2,6144]{2,1,0:T(2,128)(2,1)} %all_to_all.19), calls=%async_computation.1 | async-start | bytes 3145728 | tf_op jit(solution)/shard_map/all_to_all | solution.py:112
where the time goes:
time: 151 us; the launch traced here: 150 us
  waiting for transfers between devices  58.9 us (39%)
  starting transfers between devices  38.9 us (26%)
  local copies, waits for them, and re-layouts  21.1 us (14%)
  matrix products  20.3 us (13%)
  other arithmetic  9.62 us (6%)
    all_to_all x1, waiting for transfers between devices, carry_cells(): lax.all_to_all(outgoing, ('gx', 'gz'), split_axis=0, concat_axis=0, tiled...  36.1 us
    ppermute x6, waiting for transfers between devices, extended(): before = lax.ppermute(last, axis, up)  18.7 us
    dot_general x6, matrix products, neighbor_values(): jnp.einsum('abcst,abctj->abcsj', matches, other_values, preferred_element...  17.7 us
    ppermute x6, starting transfers between devices, extended(): after = lax.ppermute(first, axis, down)  12 us
    ppermute x6, starting transfers between devices, extended(): before = lax.ppermute(last, axis, up)  9.82 us
    all_to_all x1, starting transfers between devices, carry_cells(): lax.all_to_all(metadata, ('gx', 'gz'), split_axis=0, concat_axis=0, tiled...  9.73 us
    all_to_all x1, starting transfers between devices, carry_cells(): lax.all_to_all(outgoing, ('gx', 'gz'), split_axis=0, concat_axis=0, tiled...  7.39 us
    ppermute x6, waiting for transfers between devices, extended(): after = lax.ppermute(first, axis, down)  4.11 us
  transfers between devices with their start and end apart: 14, of which 7 were waited for; matrix products, arithmetic and copies ran while one was open for 28% of the time, Pallas kernels for 0%

commit v1 on v0

v1 whole, which is shorter than its diff:
```python
import math

import jax
import jax.numpy as jnp
import numpy as np
from jax import lax
from jax.experimental import pallas as pl
from jax.experimental.pallas import tpu as pltpu
from jax.sharding import PartitionSpec as P

NV1 = 48
BLK = 8
MAXB = 12
EDGE = NV1 // BLK
VB = BLK**3
TILES = 16
ROWS = MAXB * 8
LANES = 128
STEP_COEFF = 0.6
IMPACT_KIND = 0.02
LAM = STEP_COEFF / (NV1 - 1)
F32 = jnp.float32
BF16 = jnp.bfloat16


def iota(shape, dim):
    return lax.broadcasted_iota(jnp.int32, shape, dim)


def mm(a, b):
    return jnp.dot(a.astype(BF16), b.astype(BF16), preferred_element_type=F32)


def spread(rows):
    pick = (iota((8, LANES), 1) % 8 == iota((8, LANES), 0)).astype(F32)
    return mm(rows.astype(F32), pick)


def listed_rows(ids_ref, cnt_ref):
    slots = (iota((MAXB, LANES), 1) // 8 == iota((MAXB, LANES), 0)).astype(F32)
    wide = mm(ids_ref[...].astype(F32), slots)
    mine = iota((LANES, LANES), 1) % 8 == iota((LANES, LANES), 0) % 8
    ids = jnp.sum(jnp.where(mine, wide, 0.0).reshape(TILES, 8, LANES), axis=1)
    lane = iota((TILES, LANES), 1)
    live = ((lane // 8).astype(F32) < spread(cnt_ref[...])) & (lane < ROWS)
    return ids, live


def halo_kernel(d_ref, ids_ref, cnt_ref, ylo, yhi, zlo, zhi, xlo, xhi):
    ids, live = listed_rows(ids_ref, cnt_ref)
    listed = jnp.where(live, ids, -1.0)
    xlo[...] = listed[:8]
    xhi[...] = listed[8:]
    for out, y in ((ylo, 0), (yhi, 7)):
        for x in range(2):
            out[x, :ROWS, :] = d_ref[x * 8 + y]
            row = jnp.broadcast_to(listed[x * 8 + y : x * 8 + y + 1], (8, LANES))
            tail = jnp.concatenate([row, jnp.zeros((8, VB - LANES), F32)], axis=1)
            out[x, ROWS:, :] = tail.astype(BF16)
    lane = iota((TILES, LANES), 1)
    keys = []
    for z, first in ((0, 112), (7, 96)):
        source = iota((LANES, LANES), 0)
        target = iota((LANES, LANES), 1) - first
        move = ((source == target * 8 + z) & (target >= 0) & (target < MAXB)).astype(F32)
        keys.append(jnp.where((lane >= first) & (lane < first + MAXB), mm(listed, move), -1.0))
    row = iota((32, ROWS), 0)
    wanted = jnp.where(row < 16, row * 8, (row - 16) * 8 + 7)
    valid = (row % 16) < MAXB
    select = ((iota((32, ROWS), 1) == wanted) & valid).astype(BF16)
    key_row = iota((16, LANES), 0) == MAXB
    for i in range(TILES):
        faces = jnp.dot(select, d_ref[i], preferred_element_type=F32)
        for out, start, key in ((zlo, 0, keys[0]), (zhi, 16, keys[1])):
            face = faces[start : start + 16]
            first = jnp.where(key_row, jnp.broadcast_to(key[i : i + 1], (16, LANES)), face[:, :LANES])
            out[i, :, :LANES] = first.astype(BF16)
            out[i, :, LANES:] = face[:, LANES:].astype(BF16)


def local_kernel(d_ref, ylo, yhi, zlo, zhi, ids_ref, cnt_ref, rest_ref, vel_ref, acc_ref, cols_ref):
    ids, live = listed_rows(ids_ref, cnt_ref)
    lane = iota((TILES, LANES), 1)
    tile = iota((TILES, LANES), 0)
    zl = lane % 8
    number = ids.astype(jnp.int32)
    bx, by, bz = number // (EDGE * EDGE), number // EDGE % EDGE, number % EDGE
    half = EDGE // 2
    key = ids * 8.0 + zl.astype(F32)
    none = jnp.full((TILES, LANES), -1.0, F32)
    x_low = tile < 8
    inner = live & ((x_low & (bx < half)) | (jnp.logical_not(x_low) & (bx >= half)))
    z_up = bz >= half
    z_step = jnp.where(z_up, -1.0, 1.0)
    z_edge = (z_up & (zl == 0)) | (jnp.logical_not(z_up) & (zl == 7))
    kz = jnp.where(z_edge, ids + jnp.where(z_up, 4096.0, 8192.0), key + z_step)
    centre = lambda b: b.astype(F32) * BLK + ((BLK - 1) / 2.0 - (NV1 - 1) / 2.0)
    widen = 1.0 + spread(rest_ref[...])
    first = jnp.concatenate(
        [
            jnp.where(inner, key, none),
            jnp.where(live & (by >= half), key, none),
            jnp.where(live & (by < half), key, none),
            jnp.where(live, kz, none),
            centre(bx),
            centre(by),
            centre(bz),
            live.astype(F32),
        ],
        axis=0,
    )
    second = jnp.concatenate(
        [jnp.where(live & jnp.logical_not(inner), key, none), widen * widen / 4.0]
        + [jnp.zeros((TILES, LANES), F32)] * 6,
        axis=0,
    )
    first, second = first.T, second.T
    cols_ref[0] = first
    cols_ref[1] = second
    near = jnp.where(live, key, -2.0)
    zrow = zl[:1].astype(F32)
    one_lane = lane[:1]
    column = lambda which, i: first[:ROWS, which * TILES + i : which * TILES + i + 1]

    def halo_key(ref, x):
        got = ref[x, ROWS:, :LANES].astype(F32)[:1]
        return jnp.where(got < 0.0, -2.0, got * 8.0 + zrow)

    def match(col, row):
        return (col == row).astype(F32).astype(BF16)

    for i in range(TILES):
        x, y = divmod(i, 8)
        own = d_ref[i]
        f = own.astype(F32)
        other = (1 - x) * 8 + y
        gx = jnp.dot(match(column(0, i), near[other : other + 1, :ROWS]), d_ref[other], preferred_element_type=F32)
        low, low_key = (ylo[x, :ROWS, :], halo_key(ylo, x)) if y == 0 else (d_ref[i - 1], near[i - 1 : i])
        high, high_key = (yhi[x, :ROWS, :], halo_key(yhi, x)) if y == 7 else (d_ref[i + 1], near[i + 1 : i + 2])
        gy = jnp.dot(match(column(1, i), low_key[:, :ROWS]), low, preferred_element_type=F32)
        gy = gy + jnp.dot(match(column(2, i), high_key[:, :ROWS]), high, preferred_element_type=F32)
        edge = jnp.maximum(zlo[i, :, :LANES].astype(F32)[MAXB : MAXB + 1], zhi[i, :, :LANES].astype(F32)[MAXB : MAXB + 1])
        edge = jnp.where(edge < 0.0, -2.0, edge + jnp.where(one_lane < 112, 4096.0, 8192.0))
        zkey = jnp.where(one_lane < ROWS, near[i : i + 1], edge)
        around = jnp.concatenate([own, zlo[i], zhi[i]], axis=0)
        gz = jnp.dot(match(column(3, i), zkey), around, preferred_element_type=F32)
        acc = f
        for d, g in enumerate((gx, gy, gz)):
            speed = jnp.abs(LAM * column(4 + d, i) + vel_ref[3 + d : 4 + d])
            acc = acc + speed * (g - f)
        acc_ref[i] = acc * column(7, i)


def route_kernel(ids_ref, cnt_ref, own_ref, sel_ref, meta_ref):
    lane = iota((TILES, LANES), 1)
    here = lane // 8 == iota((TILES, LANES), 0)
    flat = lambda v: jnp.sum(jnp.where(here, spread(v), 0.0), axis=0, keepdims=True)
    owner, count = flat(own_ref[...]), flat(cnt_ref[...])
    sub = iota((LANES, LANES), 0)
    cols = jnp.where(sub == 0, owner, jnp.where(sub == 1, count, 0.0)).T
    earlier = (cols[:, :1] == owner) & (sub < iota((LANES, LANES), 1))
    rank = jnp.sum(earlier.astype(F32), axis=0, keepdims=True)
    target = jnp.concatenate([owner * 8.0 + rank + 2.0 * s for s in range(4)], axis=1)
    sel_ref[...] = (iota((512, 512), 0).astype(F32) == target).astype(F32).astype(BF16)
    place = (sub.astype(F32) == owner * 2.0 + rank).astype(F32)
    wide = mm(ids_ref[...].astype(F32), (iota((MAXB, LANES), 0) == iota((MAXB, LANES), 1)).astype(F32))
    info = jnp.where(iota((LANES, LANES), 1) == MAXB, cols[:, 1:2], wide)
    meta_ref[...] = mm(place, info).astype(BF16)


def final_kernel(acc_ref, lo_ref, hi_ref, lokey, hikey, cols_ref, vel_ref, wts_ref, sel_ref, out_ref, read, rows):
    first, second = cols_ref[0], cols_ref[1]
    zrow = (iota((8, LANES), 1) % 8).astype(F32)
    keys = []
    for ref in (lokey, hikey):
        got = ref[...]
        keys.append(jnp.where(got < 0.0, -2.0, got * 8.0 + zrow))
    lane = iota((1, LANES), 1)
    pick = lambda *pairs: sum((lane == at).astype(F32) * value for at, value in pairs)
    plain = pick((0, 1.0), (4, 1.0), (5, 1.0), (6, 1.0), (11, 1.0))
    linear = [pick((1 + d, 1.0), (8 + d, 2.0)) for d in range(3)]
    square = pick((7, 1.0))
    column = lambda src, which, i: src[:ROWS, which * TILES + i : which * TILES + i + 1]
    totals = []
    for i in range(TILES):
        x, y = divmod(i, 8)
        key = keys[x][y : y + 1, :ROWS]
        pick_rows = (column(second, 0, i) == key).astype(F32).astype(BF16)
        g = jnp.dot(pick_rows, (lo_ref, hi_ref)[x][y], preferred_element_type=F32)
        c = [column(first, 4 + d, i) for d in range(3)]
        speed = jnp.abs(LAM * c[0] + vel_ref[3:4])
        now = (acc_ref[i] + speed * g).astype(BF16)
        read[i] = now
        sums = jnp.dot(now, wts_ref[...], preferred_element_type=F32)
        norm = c[0] * c[0] + c[1] * c[1] + c[2] * c[2]
        factor = plain + c[0] * linear[0] + c[1] * linear[1] + c[2] * linear[2] + norm * square
        totals.append(jnp.sum((sums * factor).reshape(MAXB, 8, LANES), axis=0))
    total = jnp.concatenate(totals, axis=0)
    at = lambda k: total[:, k : k + 1]
    mass = at(0)
    u = [(at(1 + d) + at(4 + d)) / mass for d in range(3)]
    energy = at(7) + at(8) + at(9) + at(10) + at(11)
    warm = (energy / mass - (u[0] * u[0] + u[1] * u[1] + u[2] * u[2])) / 3.0
    widen = jnp.concatenate([column(second, 1, i)[:8] for i in range(TILES)], axis=0)
    aim = warm * widen
    rate = 1.0 - jnp.exp(-IMPACT_KIND * (mass / VB) * jnp.sqrt(warm))
    spread_ = 2.0 * math.pi * aim
    scale = mass / (spread_ * jnp.sqrt(spread_))
    sharp = -0.5 * math.log2(math.e) / aim
    for i in range(TILES):
        cell = lambda v: jnp.concatenate([v[i * 8 : i * 8 + 8]] * MAXB, axis=0)
        now = read[i].astype(F32)
        dist = None
        for d in range(3):
            off = (column(first, 4 + d, i) - cell(u[d])) + vel_ref[d : d + 1]
            dist = off * off if dist is None else dist + off * off
        bell = cell(scale) * jnp.exp2(cell(sharp) * dist)
        after = now + (cell(rate) * column(first, 7, i)) * (bell - now)
        rows[:, i * 8 : i * 8 + 8, :] = after.reshape(MAXB, 8, VB).astype(BF16)
    for t in range(3):
        part = rows[4 * t : 4 * t + 4].reshape(512, VB)
        out = jnp.dot(sel_ref[...], part, preferred_element_type=F32)
        out_ref[:, 8 * t : 8 * t + 8, :] = out.reshape(64, 8, VB).astype(BF16)


def unpack_kernel(got_ref, meta_ref, out_ref, ids_ref, cnt_ref):
    row, col = iota((256, 256), 0), iota((256, 256), 1)
    source = (row % 64) // 2 * 8 + row // 64 * 2 + row % 2
    perm = (col == source).astype(F32).astype(BF16)
    for t in range(3):
        for g in range(2):
            part = got_ref[32 * g : 32 * g + 32, 8 * t : 8 * t + 8, :].reshape(256, VB)
            out = jnp.dot(perm, part, preferred_element_type=F32)
            out_ref[4 * t : 4 * t + 4, 64 * g : 64 * g + 64, :] = out.reshape(4, 64, VB).astype(BF16)
    info = meta_ref[...].astype(F32).T.astype(jnp.int32)
    ids_ref[...] = info[:MAXB]
    cnt_ref[...] = info[MAXB : MAXB + 1]


def call(kernel, outs, name, scratch=(), flops=0, moved=0):
    return pl.pallas_call(
        kernel,
        out_shape=[jax.ShapeDtypeStruct(s, d) for s, d in outs],
        scratch_shapes=list(scratch),
        compiler_params=pltpu.CompilerParams(vmem_limit_bytes=48 << 20),
        cost_estimate=pl.CostEstimate(flops=flops, bytes_accessed=moved, transcendentals=0),
        name=name,
    )


def tables():
    j = np.arange(VB)
    w = np.stack([j // (BLK * BLK), j // BLK % BLK, j % BLK]).astype(np.float32) - (BLK - 1) / 2.0
    vel = np.zeros((8, VB), np.float32)
    vel[:3] = w
    vel[3:6] = np.float32(LAM) * w
    weights = np.zeros((VB, LANES), np.float32)
    weights[:, [0, 1, 2, 3, 7]] = 1.0
    for d in range(3):
        weights[:, 4 + d] = w[d]
        weights[:, 8 + d] = w[d]
    weights[:, 11] = (w * w).sum(0)
    return vel, weights


def on_device(distribution, block_ids, cell_counts, owner, restitution):
    nx, ny, nz = (lax.axis_size(a) for a in ("gx", "gy", "gz"))

    def up(v, axis, n):
        return lax.ppermute(v, axis, [(i, (i + 1) % n) for i in range(n)])

    def down(v, axis, n):
        return lax.ppermute(v, axis, [((i + 1) % n, i) for i in range(n)])

    d = distribution.transpose(0, 1, 3, 2, 4).reshape(TILES, ROWS, VB)
    ids = block_ids.reshape(TILES * 8, MAXB)
    cnt = cell_counts.reshape(TILES, 8)
    own = owner.reshape(TILES, 8)
    rest = restitution.reshape(TILES, 8)
    vel, weights = tables()
    vel, weights = jnp.asarray(vel), jnp.asarray(weights, BF16)

    x_hi = down(d[:8], "gx", nx)
    x_lo = up(d[8:], "gx", nx)
    face_y, face_z = ((2, ROWS + 8, VB), BF16), ((TILES, 16, VB), BF16)
    ylo, yhi, zlo, zhi, klo, khi = call(
        halo_kernel, [face_y, face_y, face_z, face_z, ((8, LANES), F32), ((8, LANES), F32)], "halo", flops=10**8, moved=4 * 10**6
    )(d, ids, cnt)
    y_hi, y_lo = down(ylo, "gy", ny), up(yhi, "gy", ny)
    z_hi, z_lo = down(zlo, "gz", nz), up(zhi, "gz", nz)
    k_hi, k_lo = down(klo, "gx", nx), up(khi, "gx", nx)
    acc, cols = call(
        local_kernel, [((TILES, ROWS, VB), F32), ((2, LANES, LANES), F32)], "local", flops=10**9, moved=6 * 10**6
    )(d, y_lo, y_hi, z_lo, z_hi, ids, cnt, rest, vel)
    sel, meta = call(route_kernel, [((512, 512), BF16), ((LANES, LANES), BF16)], "route", flops=10**7, moved=10**6)(ids, cnt, own)
    (out,) = call(
        final_kernel,
        [((64, 24, VB), BF16)],
        "final",
        scratch=[pltpu.VMEM((TILES, ROWS, VB), BF16), pltpu.VMEM((MAXB, LANES, VB), BF16)],
        flops=2 * 10**9,
        moved=8 * 10**6,
    )(acc, x_lo, x_hi, k_lo, k_hi, cols, vel, weights, sel)
    exchange = lambda v: lax.all_to_all(v, ("gx", "gz"), split_axis=0, concat_axis=0, tiled=True)
    got = exchange(out)
    got_meta = exchange(meta.reshape(64, 2, LANES)).reshape(LANES, LANES)
    moved, moved_ids, moved_counts = call(
        unpack_kernel,
        [((MAXB, LANES, VB), BF16), ((MAXB, LANES), jnp.int32), ((1, LANES), jnp.int32)],
        "unpack",
        flops=4 * 10**8,
        moved=4 * 10**6,
    )(got, got_meta)
    return (
        moved.transpose(1, 0, 2).reshape(1, LANES, MAXB, VB),
        moved_ids.T.reshape(1, LANES, MAXB),
        moved_counts,
    )


def solution(mesh):
    placed = (
        P("gx", "gy", "gz", None, None),
        P("gx", "gy", "gz", None),
        P("gx", "gy", "gz"),
        P("gx", "gy", "gz"),
        P("gx", "gy", "gz"),
    )
    return jax.shard_map(
        on_device,
        mesh=mesh,
        in_specs=placed,
        out_specs=(
            P("gy", ("gx", "gz"), None, None),
            P("gy", ("gx", "gz"), None),
            P("gy", ("gx", "gz")),
        ),
        check_vma=False,
    )
```

time: 151 us -> 103 us (0.68)
  waiting for transfers between devices: 58.9 us -> 3.68 us
  blocking collectives: 0 us -> 49.3 us
  matrix products: 20.3 us -> 0 us
  Pallas kernels: 0 us -> 17.7 us
  starting transfers between devices: 38.9 us -> 24 us
  local copies, waits for them, and re-layouts: 21.1 us -> 7.44 us
  other arithmetic: 9.62 us -> 0 us
    all_to_all x0 -> x1, blocking collectives: none -> 49.3 us  [on_device(): lax.all_to_all(v, ('gx', 'gz'), split_axis=0, concat_axis=0, tiled=True)]
    all_to_all x2 -> x1, waiting for transfers between devices: 36.1 us -> 0.01 us  [on_device(): lax.all_to_all(v, ('gx', 'gz'), split_axis=0, concat_axis=0, tiled=True)]
    dot_general x7 -> x0, matrix products: 20.3 us -> none  [the longest x6 17.7 us: neighbor_values(): jnp.einsum('abcst,abctj->abcsj', matches, other_values, preferred_element...]
    ppermute x12 -> x8, waiting for transfers between devices: 22.8 us -> 3.68 us  [the longest x4 3.67 us: up(): return lax.ppermute(v, axis, [(i, (i + 1) % n) for i in range(n)])]
    pallas_call x0 -> x5, Pallas kernels: none -> 17.7 us  [the longest x1 8.48 us: on_device(): call(final_kernel, [((64, 24, VB), BF16)], 'final', scratch=[pltpu.VMEM((...]
    scatter x5 -> x0, local copies, waits for them, and re-layouts: 9.71 us -> none  [the longest x2 4.02 us: on_device(): jnp.zeros((cell_total, row_width), jnp.bfloat16).at[targets]]
    all_to_all x2 -> x1, starting transfers between devices: 17.1 us -> 9.34 us  [on_device(): lax.all_to_all(v, ('gx', 'gz'), split_axis=0, concat_axis=0, tiled=True)]
    ppermute x12 -> x8, starting transfers between devices: 21.8 us -> 14.7 us  [the longest x4 9.63 us: down(): return lax.ppermute(v, axis, [((i + 1) % n, i) for i in range(n)])]
  transfers between devices with their start and end apart: 14 -> 9, of which waited for: 7 -> 1; matrix products, arithmetic and copies ran while one was open for 28% -> 0% of each run, Pallas kernels for 0% -> 15%
where the time goes in v1:
time: 103 us
  blocking collectives  49.3 us (48%)
  starting transfers between devices  24 us (23%)
  Pallas kernels  17.7 us (17%)
  local copies, waits for them, and re-layouts  7.44 us (7%)
  waiting for transfers between devices  3.68 us (4%)
    all_to_all x1, blocking collectives, on_device(): lax.all_to_all(v, ('gx', 'gz'), split_axis=0, concat_axis=0, tiled=True)  49.3 us
    ppermute x4, starting transfers between devices, down(): return lax.ppermute(v, axis, [((i + 1) % n, i) for i in range(n)])  9.63 us
    all_to_all x1, starting transfers between devices, on_device(): lax.all_to_all(v, ('gx', 'gz'), split_axis=0, concat_axis=0, tiled=True)  9.34 us
    pallas_call x1, Pallas kernels, on_device(): call(final_kernel, [((64, 24, VB), BF16)], 'final', scratch=[pltpu.VMEM((...  8.48 us
    pallas_call x1, Pallas kernels, on_device(): call(local_kernel, [((TILES, ROWS, VB), F32), ((2, LANES, LANES), F32)],...  5.09 us
    ppermute x4, starting transfers between devices, up(): return lax.ppermute(v, axis, [(i, (i + 1) % n) for i in range(n)])  5.06 us
    unnamed x25, local copies, waits for them, and re-layouts  4.67 us
    ppermute x4, waiting for transfers between devices, up(): return lax.ppermute(v, axis, [(i, (i + 1) % n) for i in range(n)])  3.67 us
  transfers between devices with their start and end apart: 9, of which 1 were waited for; matrix products, arithmetic and copies ran while one was open for 0% of the time, Pallas kernels for 15%

profile of v1, /device:TPU:1, one launch (start us, length us, event | category | flops | bytes accessed | tf_op | source)
XLA Modules:
  0.0 102.9 jit_solution(5098640321892588181)
XLA Ops:
  0.7 2.8 %slice_bitcast_fusion = (bf16[8,96,512]{2,1,0:T(8,128)(2,1)}, bf16[8,96,512]{2,1,0:T(8,128)(2,1)}) fusion(bf16[2,8,12,8,512]{4,3,2,1,0:T(8,128)(2,1)} %bitcast.19), kind=kLoop, calls=%fused_computation | loop fusion | bytes 3145728 | tf_op jit(solution)/shard_map/slice | solution.py:283
  3.4 6.5 %collective-permute-start.5 = (bf16[8,96,512]{2,1,0:T(8,128)(2,1)}, bf16[8,96,512]{2,1,0:T(8,128)(2,1)S(1)}, u32[]{:S(2)}, u32[]{:S(2)}) collective-permute-start(bf16[8,96,512]{2,1,0:T(8,128)(2,1)} %get-tuple-element.32), channel_id=1, source_target_pairs={{32,0},{64,32},{96,64},{128,96},{160,128},{192,160},{224,192},{0,2... | collective-permute-start | bytes 2359304 | tf_op jit(solution)/shard_map/ppermute | solution.py:273
  9.9 0.0 collective-permute-start.4
  9.9 0.0 copy-done.2
  9.9 1.2 %halo.1 = (bf16[2,104,512]{2,1,0:T(8,128)(2,1)}, bf16[2,104,512]{2,1,0:T(8,128)(2,1)S(1)}, bf16[16,16,512]{2,1,0:T(8,128)(2,1)S(1)}, bf16[16,16,512]{2,1,0:T(8,1...) custom-call(bf16[16,96,512]{2,1,0:T(8,128)(2,1)S(1)} %bitcast.20, s32[128,12]{1,0:T(8,128)S(1)} %bitcast.22, ...), custom_call_target="tpu_custom_call" | custom-call | flops 100000000 | bytes 4000000 | tf_op jit(solution)/shard_map/halo/pallas_call | solution.py:286
  11.1 1.3 %collective-permute-start = (bf16[2,104,512]{2,1,0:T(8,128)(2,1)S(1)}, bf16[2,104,512]{2,1,0:T(8,128)(2,1)S(1)}, u32[]{:S(2)}, u32[]{:S(2)}) collective-permute-start(bf16[2,104,512]{2,1,0:T(8,128)(2,1)S(1)} %get-tuple-element.16), channel_id=1, source_target_pairs={{0,8},{8,16},{16,24},{24,0},{1,9},{9,17},{17,25},{25,1},{2,10},{10... | collective-permute-start | bytes 638984 | tf_op jit(solution)/shard_map/ppermute | solution.py:270
  12.4 2.3 %collective-permute-start.2 = (bf16[16,16,512]{2,1,0:T(8,128)(2,1)}, bf16[16,16,512]{2,1,0:T(8,128)(2,1)}, u32[]{:S(2)}, u32[]{:S(2)}) collective-permute-start(bf16[16,16,512]{2,1,0:T(8,128)(2,1)} %get-tuple-element.18), channel_id=1, source_target_pairs={{0,1},{1,2},{2,3},{3,4},{4,5},{5,6},{6,7},{7,0},{8,9},{9,10},{10,1... | collective-permute-start | bytes 786440 | tf_op jit(solution)/shard_map/ppermute | solution.py:270
  14.8 0.0 collective-permute-start.3
  14.8 3.7 %collective-permute-done.ylo = bf16[2,104,512]{2,1,0:T(8,128)(2,1)S(1)} collective-permute-done((bf16[2,104,512]{2,1,0:T(8,128)(2,1)S(1)}, bf16[2,104,512]{2,1,0:T(8,128)(2,1)S(1)}, u32[]{:S(2)}, u32[]{:S(2)}) %collective-permute-start) | collective-permute-done | bytes 213024 | tf_op jit(solution)/shard_map/ppermute | solution.py:270
  18.4 0.7 copy-done.6
  19.1 1.4 %collective-permute-start.1 = (bf16[2,104,512]{2,1,0:T(8,128)(2,1)}, bf16[2,104,512]{2,1,0:T(8,128)(2,1)}, u32[]{:S(2)}, u32[]{:S(2)}) collective-permute-start(bf16[2,104,512]{2,1,0:T(8,128)(2,1)} %get-tuple-element.17), channel_id=1, source_target_pairs={{8,0},{16,8},{24,16},{0,24},{9,1},{17,9},{25,17},{1,25},{10,2},{18... | collective-permute-start | bytes 638984 | tf_op jit(solution)/shard_map/ppermute | solution.py:273
  20.5 1.2 %route.1 = (bf16[512,512]{1,0:T(8,128)(2,1)S(1)}, bf16[128,128]{1,0:T(8,128)(2,1)}) custom-call(s32[128,12]{1,0:T(8,128)S(1)} %bitcast.23, s32[16,8]{1,0:T(8,128)S(1)} %bitcast.27, s32[16,8]{1,0:T(8,128)S(1)} %bitcast.29), custom_call_target="tpu_custom_call" | custom-call | flops 10000000 | bytes 1000000 | tf_op jit(solution)/shard_map/route/pallas_call | solution.py:295
  21.7 0.8 copy-done.4
  22.5 9.3 %all-to-all-start.1 = ((bf16[64,2,128]{2,1,0:T(2,128)(2,1)}), bf16[64,2,128]{2,1,0:T(2,128)(2,1)S(1)}, u32[]{:S(2)}, u32[]{:S(2)}) async-start(bf16[64,2,128]{2,1,0:T(2,128)(2,1)} %bitcast.9), calls=%async_computation.1 | async-start | bytes 65536 | tf_op jit(solution)/shard_map/all_to_all | solution.py:304
  31.8 0.0 collective-permute-done.1.yhi
  31.9 1.4 %collective-permute-start.6 = (f32[8,128]{1,0:T(8,128)S(1)}, f32[8,128]{1,0:T(8,128)S(1)}, u32[]{:S(2)}, u32[]{:S(2)}) collective-permute-start(f32[8,128]{1,0:T(8,128)S(1)} %get-tuple-element.21), channel_id=1, source_target_pairs={{0,32},{32,64},{64,96},{96,128},{128,160},{160,192},{192,224},{224... | collective-permute-start | bytes 12296 | tf_op jit(solution)/shard_map/ppermute | solution.py:270
  33.3 0.0 collective-permute-done.2.zlo
  33.3 1.8 %collective-permute-start.7 = (f32[8,128]{1,0:T(8,128)S(1)}, f32[8,128]{1,0:T(8,128)S(1)}, u32[]{:S(2)}, u32[]{:S(2)}) collective-permute-start(f32[8,128]{1,0:T(8,128)S(1)} %get-tuple-element.22), channel_id=1, source_target_pairs={{32,0},{64,32},{96,64},{128,96},{160,128},{192,160},{224,192},{0,2... | collective-permute-start | bytes 12296 | tf_op jit(solution)/shard_map/ppermute | solution.py:273
  35.0 0.0 collective-permute-done.3.zhi
  35.0 0.0 copy-done.8
  35.1 0.9 copy-done.7
  36.0 5.1 %local.1 = (f32[16,96,512]{2,1,0:T(8,128)S(1)}, f32[2,128,128]{2,1,0:T(8,128)S(1)}) custom-call(bf16[16,96,512]{2,1,0:T(8,128)(2,1)S(1)} %bitcast.21, bf16[2,104,512]{2,1,0:T(8,128)(2,1)S(1)} %copy-done.7, bf16[2,104,512]{2,1,0:T(8,128)(2,1)} %collective-permute-done.1.yhi, bf16[16,16,512]{2,1,0:T(8,128)(2,1)} %collective-permute-done.2.zlo, ...), custom_call_target="tpu_custom_call" | custom-call | flops 1000000000 | bytes 6000000 | tf_op jit(solution)/shard_map/local/pallas_call | solution.py:292
  41.1 1.6 %copy-done.11 = f32[16,96,512]{2,1,0:T(8,128)} copy-done((f32[16,96,512]{2,1,0:T(8,128)}, f32[16,96,512]{2,1,0:T(8,128)S(1)}, u32[]{:S(2)}) %copy-start.11) | copy-done | bytes 3145752
  42.7 0.0 collective-permute-done.6.lokey
  42.7 0.0 collective-permute-done.7.hikey
  42.7 0.0 collective-permute-done.5.hi_ref
  42.7 0.0 collective-permute-done.4.lo_ref
  42.8 8.5 %final.1 = bf16[64,24,512]{2,1,0:T(8,128)(2,1)S(1)} custom-call(f32[16,96,512]{2,1,0:T(8,128)} %copy-done.11, bf16[8,96,512]{2,1,0:T(8,128)(2,1)S(1)} %collective-permute-done.4.lo_ref, bf16[8,96,512]{2,1,0:T(8,128)(2,1)S(1)} %collective-permute-done.5.hi_ref, f32[8,128]{1,0:T(8,128)S(1)} %collective-permute-done.6.lokey, ...), custom_call_target="tpu_custom_call" | custom-call | flops 2000000000 | bytes 8000000 | tf_op jit(solution)/shard_map/final/pallas_call | solution.py:296
  51.3 0.0 all-to-all-done.1
  51.3 49.3 %all_to_all.10.got_ref = bf16[64,24,512]{2,1,0:T(8,128)(2,1)S(1)} all-to-all(bf16[64,24,512]{2,1,0:T(8,128)(2,1)S(1)} %final.1), channel_id=1, replica_groups=mesh['gx'=8,'gy'=4,'gz'=8] {'gx','gz'}, dimensions={0} | all-to-all | bytes 3145728 | tf_op jit(solution)/shard_map/all_to_all | solution.py:304
  100.5 1.7 %unpack.1 = (bf16[12,128,512]{2,1,0:T(8,128)(2,1)}, s32[12,128]{1,0:T(8,128)S(1)}, s32[1,128]{1,0:T(1,128)}) custom-call(bf16[64,24,512]{2,1,0:T(8,128)(2,1)S(1)} %all_to_all.10.got_ref, bf16[128,128]{1,0:T(8,128)(2,1)S(1)} %bitcast.25), custom_call_target="tpu_custom_call" | custom-call | flops 400000000 | bytes 4000000 | tf_op jit(solution)/shard_map/unpack/pallas_call | solution.py:307
  102.3 0.6 copy.18
  (18 shorter events, 0.0 us)
Async XLA Ops:
  0.6 9.3 %copy-start = (bf16[2,8,8,12,512]{4,2,3,1,0:T(8,128)(2,1)S(1)}, bf16[2,8,8,12,512]{4,2,3,1,0:T(8,128)(2,1)}, u32[]{:S(2)}) copy-start(bf16[2,8,8,12,512]{4,2,3,1,0:T(8,128)(2,1)} %param.7) | copy-start | bytes 4718596
  0.6 9.3 %copy-start.1 = (s32[2,8,8,12]{3,2,1,0:T(8,128)S(1)}, s32[2,8,8,12]{3,2,1,0:T(8,128)}, u32[]{:S(2)}) copy-start(s32[2,8,8,12]{3,2,1,0:T(8,128)} %param.8) | copy-start | bytes 18436
  0.7 9.3 %copy-start.2 = (s32[2,8,8]{2,1,0:T(8,128)S(1)}, s32[2,8,8]{2,1,0:T(8,128)}, u32[]{:S(2)}) copy-start(s32[2,8,8]{2,1,0:T(8,128)} %param.9) | copy-start | bytes 1540
  3.4 17.1 %copy-start.3 = (s32[2,8,8]{2,1,0:T(8,128)S(1)}, s32[2,8,8]{2,1,0:T(8,128)}, u32[]{:S(2)}) copy-start(s32[2,8,8]{2,1,0:T(8,128)} %param.10) | copy-start | bytes 1540
  3.4 31.6 %copy-start.8 = (bf16[2,8,8]{2,1,0:T(8,128)(2,1)S(1)}, bf16[2,8,8]{2,1,0:T(8,128)(2,1)}, u32[]{:S(2)}) copy-start(bf16[2,8,8]{2,1,0:T(8,128)(2,1)} %param.11) | copy-start | bytes 772
  3.4 31.6 %copy-start.10 = (f32[8,512]{1,0:T(8,128)S(1)}, f32[8,512]{1,0:T(8,128)}, u32[]{:S(2)}) copy-start(f32[8,512]{1,0:T(8,128)} %constant.4.clone.vel_ref) | copy-start | bytes 49156
  3.4 39.3 %collective-permute-start.5 = (bf16[8,96,512]{2,1,0:T(8,128)(2,1)}, bf16[8,96,512]{2,1,0:T(8,128)(2,1)S(1)}, u32[]{:S(2)}, u32[]{:S(2)}) collective-permute-start(bf16[8,96,512]{2,1,0:T(8,128)(2,1)} %get-tuple-element.32), channel_id=1, source_target_pairs={{32,0},{64,32},{96,64},{128,96},{160,128},{192,160},{224,192},{0,2... | collective-permute-start | bytes 2359304 | tf_op jit(solution)/shard_map/ppermute | solution.py:273
  9.9 32.8 %collective-permute-start.4 = (bf16[8,96,512]{2,1,0:T(8,128)(2,1)}, bf16[8,96,512]{2,1,0:T(8,128)(2,1)S(1)}, u32[]{:S(2)}, u32[]{:S(2)}) collective-permute-start(bf16[8,96,512]{2,1,0:T(8,128)(2,1)} %get-tuple-element.33), channel_id=1, source_target_pairs={{0,32},{32,64},{64,96},{96,128},{128,160},{160,192},{192,224},{224... | collective-permute-start | bytes 2359304 | tf_op jit(solution)/shard_map/ppermute | solution.py:270
  11.1 7.3 %collective-permute-start = (bf16[2,104,512]{2,1,0:T(8,128)(2,1)S(1)}, bf16[2,104,512]{2,1,0:T(8,128)(2,1)S(1)}, u32[]{:S(2)}, u32[]{:S(2)}) collective-permute-start(bf16[2,104,512]{2,1,0:T(8,128)(2,1)S(1)} %get-tuple-element.16), channel_id=1, source_target_pairs={{0,8},{8,16},{16,24},{24,0},{1,9},{9,17},{17,25},{25,1},{2,10},{10... | collective-permute-start | bytes 638984 | tf_op jit(solution)/shard_map/ppermute | solution.py:270
  12.4 20.9 %collective-permute-start.2 = (bf16[16,16,512]{2,1,0:T(8,128)(2,1)}, bf16[16,16,512]{2,1,0:T(8,128)(2,1)}, u32[]{:S(2)}, u32[]{:S(2)}) collective-permute-start(bf16[16,16,512]{2,1,0:T(8,128)(2,1)} %get-tuple-element.18), channel_id=1, source_target_pairs={{0,1},{1,2},{2,3},{3,4},{4,5},{5,6},{6,7},{7,0},{8,9},{9,10},{10,1... | collective-permute-start | bytes 786440 | tf_op jit(solution)/shard_map/ppermute | solution.py:270
  14.8 20.3 %collective-permute-start.3 = (bf16[16,16,512]{2,1,0:T(8,128)(2,1)S(1)}, bf16[16,16,512]{2,1,0:T(8,128)(2,1)}, u32[]{:S(2)}, u32[]{:S(2)}) collective-permute-start(bf16[16,16,512]{2,1,0:T(8,128)(2,1)S(1)} %get-tuple-element.19), channel_id=1, source_target_pairs={{1,0},{2,1},{3,2},{4,3},{5,4},{6,5},{7,6},{0,7},{9,8},{10,9},{11,1... | collective-permute-start | bytes 786440 | tf_op jit(solution)/shard_map/ppermute | solution.py:273
  18.4 0.7 copy-start.6
  19.1 12.7 %collective-permute-start.1 = (bf16[2,104,512]{2,1,0:T(8,128)(2,1)}, bf16[2,104,512]{2,1,0:T(8,128)(2,1)}, u32[]{:S(2)}, u32[]{:S(2)}) collective-permute-start(bf16[2,104,512]{2,1,0:T(8,128)(2,1)} %get-tuple-element.17), channel_id=1, source_target_pairs={{8,0},{16,8},{24,16},{0,24},{9,1},{17,9},{25,17},{1,25},{10,2},{18... | collective-permute-start | bytes 638984 | tf_op jit(solution)/shard_map/ppermute | solution.py:273
  21.7 0.8 copy-start.4
  22.5 28.8 %all-to-all-start.1 = ((bf16[64,2,128]{2,1,0:T(2,128)(2,1)}), bf16[64,2,128]{2,1,0:T(2,128)(2,1)S(1)}, u32[]{:S(2)}, u32[]{:S(2)}) async-start(bf16[64,2,128]{2,1,0:T(2,128)(2,1)} %bitcast.9), calls=%async_computation.1 | async-start | bytes 65536 | tf_op jit(solution)/shard_map/all_to_all | solution.py:304
  31.9 10.9 %collective-permute-start.6 = (f32[8,128]{1,0:T(8,128)S(1)}, f32[8,128]{1,0:T(8,128)S(1)}, u32[]{:S(2)}, u32[]{:S(2)}) collective-permute-start(f32[8,128]{1,0:T(8,128)S(1)} %get-tuple-element.21), channel_id=1, source_target_pairs={{0,32},{32,64},{64,96},{96,128},{128,160},{160,192},{192,224},{224... | collective-permute-start | bytes 12296 | tf_op jit(solution)/shard_map/ppermute | solution.py:270
  33.3 9.4 %collective-permute-start.7 = (f32[8,128]{1,0:T(8,128)S(1)}, f32[8,128]{1,0:T(8,128)S(1)}, u32[]{:S(2)}, u32[]{:S(2)}) collective-permute-start(f32[8,128]{1,0:T(8,128)S(1)} %get-tuple-element.22), channel_id=1, source_target_pairs={{32,0},{64,32},{96,64},{128,96},{160,128},{192,160},{224,192},{0,2... | collective-permute-start | bytes 12296 | tf_op jit(solution)/shard_map/ppermute | solution.py:273
  35.1 0.9 copy-start.7
  36.0 6.8 %copy-start.5 = (bf16[512,512]{1,0:T(8,128)(2,1)S(1)}, bf16[512,512]{1,0:T(8,128)(2,1)}, u32[]{:S(2)}) copy-start(bf16[512,512]{1,0:T(8,128)(2,1)} %copy-done.4) | copy-start | bytes 1572868
  36.0 6.8 %copy-start.9 = (bf16[512,128]{1,0:T(8,128)(2,1)S(1)}, bf16[512,128]{1,0:T(8,128)(2,1)}, u32[]{:S(2)}) copy-start(bf16[512,128]{1,0:T(8,128)(2,1)} %constant.5.clone.wts_ref) | copy-start | bytes 393220
  41.1 1.6 %copy-start.11 = (f32[16,96,512]{2,1,0:T(8,128)}, f32[16,96,512]{2,1,0:T(8,128)S(1)}, u32[]{:S(2)}) copy-start(f32[16,96,512]{2,1,0:T(8,128)S(1)} %get-tuple-element.20.acc_ref) | copy-start | bytes 9437188

commit v2 on v1

v2 whole, which is shorter than its diff:
```python
import functools
import math

import jax
import jax.numpy as jnp
import numpy as np
from jax import lax
from jax.experimental import pallas as pl
from jax.experimental.pallas import tpu as pltpu
from jax.sharding import PartitionSpec as P


NV1 = 48
BLK = 8
MAXB = 12
EDGE = NV1 // BLK
VB = BLK**3
TILES = 16
HALF = 4
ROWS = MAXB * 8
LANES = 128
STEP_COEFF = 0.6
IMPACT_KIND = 0.02
FAR = 1.0e6
LAM = STEP_COEFF / (NV1 - 1)
F32 = jnp.float32
BF16 = jnp.bfloat16


def iota(shape, dim):
    return lax.broadcasted_iota(jnp.int32, shape, dim)


def mm(a, b):
    return jnp.dot(a.astype(BF16), b.astype(BF16), preferred_element_type=F32)


def spread(rows):
    pick = (iota((8, LANES), 1) % 8 == iota((8, LANES), 0)).astype(F32)
    return mm(rows.astype(F32), pick)


def centre(b):
    return b.astype(F32) * BLK + ((BLK - 1) / 2.0 - (NV1 - 1) / 2.0)


def listed_rows(ids_ref, cnt_ref):
    slots = (iota((MAXB, LANES), 1) // 8 == iota((MAXB, LANES), 0)).astype(F32)
    wide = mm(ids_ref[...].astype(F32), slots)
    mine = iota((LANES, LANES), 1) % 8 == iota((LANES, LANES), 0) % 8
    ids = jnp.sum(jnp.where(mine, wide, 0.0).reshape(TILES, 8, LANES), axis=1)
    lane = iota((TILES, LANES), 1)
    live = ((lane // 8).astype(F32) < spread(cnt_ref[...])) & (lane < ROWS)
    return ids, live


def x_copies(part, d_ref, outs, sems):
    copies = []
    for k, out in enumerate(outs):
        source = d_ref.at[pl.ds((8 * k + HALF * part) * ROWS, HALF * ROWS)]
        copies.append(pltpu.make_async_copy(source, out.at[pl.ds(0, HALF * ROWS)], sems.at[k]))
    return copies


def put_keys(listed, outs):
    for k, out in enumerate(outs):
        out[HALF * ROWS :, :LANES] = listed[8 * k : 8 * k + 8].astype(BF16)
        out[HALF * ROWS :, LANES:] = jnp.zeros((8, VB - LANES), BF16)


def face_kernel(d_ref, ids_ref, cnt_ref, lo, hi, sems):
    copies = x_copies(1, d_ref, (lo, hi), sems)
    for copy in copies:
        copy.start()
    ids, live = listed_rows(ids_ref, cnt_ref)
    put_keys(jnp.where(live, ids, -1.0), (lo, hi))
    for copy in copies:
        copy.wait()


def front_kernel(d_hbm, ids_hbm, cnt_hbm, lo, hi, ylo, yhi, zlo, zhi, d_ref, ids_ref, cnt_ref, sems):
    small = [pltpu.make_async_copy(ids_hbm, ids_ref, sems.at[2]), pltpu.make_async_copy(cnt_hbm, cnt_ref, sems.at[3])]
    large = x_copies(0, d_hbm, (lo, hi), sems)
    quarter = TILES // 4 * ROWS
    parts = [pl.ds(q * quarter, quarter) for q in range(4)]
    whole = [pltpu.make_async_copy(d_hbm.at[p], d_ref.at[p], sems.at[4 + q]) for q, p in enumerate(parts)]
    for copy in small + whole + large:
        copy.start()
    for copy in small:
        copy.wait()
    ids, live = listed_rows(ids_ref, cnt_ref)
    listed = jnp.where(live, ids, -1.0)
    put_keys(listed, (lo, hi))
    lane = iota((TILES, LANES), 1)
    keys = []
    for z, first in ((0, 112), (7, 96)):
        source = iota((LANES, LANES), 0)
        target = iota((LANES, LANES), 1) - first
        move = ((source == target * 8 + z) & (target >= 0) & (target < MAXB)).astype(F32)
        keys.append(jnp.where((lane >= first) & (lane < first + MAXB), mm(listed, move), -1.0))
    row = iota((32, ROWS), 0)
    wanted = jnp.where(row < 16, row * 8, (row - 16) * 8 + 7)
    valid = (row % 16) < MAXB
    select = ((iota((32, ROWS), 1) == wanted) & valid).astype(BF16)
    key_row = iota((16, LANES), 0) == MAXB
    for i in range(TILES):
        if i % 4 == 0:
            whole[i // 4].wait()
        tile = d_ref[i * ROWS : i * ROWS + ROWS, :]
        if i % 8 in (0, 7):
            out = yhi if i % 8 else ylo
            out[i // 8, :ROWS, :] = tile
            tail = jnp.concatenate([jnp.broadcast_to(listed[i : i + 1], (8, LANES)), jnp.zeros((8, VB - LANES), F32)], axis=1)
            out[i // 8, ROWS:, :] = tail.astype(BF16)
        faces = jnp.dot(select, tile, preferred_element_type=F32)
        for out, start, key in ((zlo, 0, keys[0]), (zhi, 16, keys[1])):
            face = faces[start : start + 16]
            first = jnp.where(key_row, jnp.broadcast_to(key[i : i + 1], (16, LANES)), face[:, :LANES])
            out[i, :, :LANES] = first.astype(BF16)
            out[i, :, LANES:] = face[:, LANES:].astype(BF16)
    for copy in large:
        copy.wait()


def local_kernel(d_ref, ylo, yhi, zlo, zhi, ids_ref, cnt_ref, vel_ref, acc_ref):
    ids, live = listed_rows(ids_ref, cnt_ref)
    lane = iota((TILES, LANES), 1)
    tile = iota((TILES, LANES), 0)
    zl = lane % 8
    number = ids.astype(jnp.int32)
    bx, by, bz = number // (EDGE * EDGE), number // EDGE % EDGE, number % EDGE
    half = EDGE // 2
    key = ids * 8.0 + zl.astype(F32)
    none = jnp.full((TILES, LANES), -1.0, F32)
    x_low = tile < 8
    inner = live & ((x_low & (bx < half)) | (jnp.logical_not(x_low) & (bx >= half)))
    z_up = bz >= half
    z_step = jnp.where(z_up, -1.0, 1.0)
    z_edge = (z_up & (zl == 0)) | (jnp.logical_not(z_up) & (zl == 7))
    kz = jnp.where(z_edge, ids + jnp.where(z_up, 4096.0, 8192.0), key + z_step)
    first = jnp.concatenate(
        [
            jnp.where(inner, key, none),
            jnp.where(live & (by >= half), key, none),
            jnp.where(live & (by < half), key, none),
            jnp.where(live, kz, none),
            centre(bx),
            centre(by),
            centre(bz),
            live.astype(F32),
        ],
        axis=0,
    )
    first = first.T
    near = jnp.where(live, key, -2.0)
    zrow = zl[:1].astype(F32)
    one_lane = lane[:1]
    column = lambda which, i: first[:ROWS, which * TILES + i : which * TILES + i + 1]

    def halo_key(ref, x):
        got = ref[x, ROWS:, :LANES].astype(F32)[:1]
        return jnp.where(got < 0.0, -2.0, got * 8.0 + zrow)

    def match(col, row):
        return (col == row).astype(F32).astype(BF16)

    for i in range(TILES):
        x, y = divmod(i, 8)
        own = d_ref[i]
        f = own.astype(F32)
        other = (1 - x) * 8 + y
        gx = jnp.dot(match(column(0, i), near[other : other + 1, :ROWS]), d_ref[other], preferred_element_type=F32)
        low, low_key = (ylo[x, :ROWS, :], halo_key(ylo, x)) if y == 0 else (d_ref[i - 1], near[i - 1 : i])
        high, high_key = (yhi[x, :ROWS, :], halo_key(yhi, x)) if y == 7 else (d_ref[i + 1], near[i + 1 : i + 2])
        gy = jnp.dot(match(column(1, i), low_key[:, :ROWS]), low, preferred_element_type=F32)
        gy = gy + jnp.dot(match(column(2, i), high_key[:, :ROWS]), high, preferred_element_type=F32)
        edge = jnp.maximum(zlo[i, :, :LANES].astype(F32)[MAXB : MAXB + 1], zhi[i, :, :LANES].astype(F32)[MAXB : MAXB + 1])
        edge = jnp.where(edge < 0.0, -2.0, edge + jnp.where(one_lane < 112, 4096.0, 8192.0))
        zkey = jnp.where(one_lane < ROWS, near[i : i + 1], edge)
        around = jnp.concatenate([own, zlo[i], zhi[i]], axis=0)
        gz = jnp.dot(match(column(3, i), zkey), around, preferred_element_type=F32)
        acc = f
        for d, g in enumerate((gx, gy, gz)):
            speed = jnp.abs(LAM * column(4 + d, i) + vel_ref[3 + d : 4 + d])
            acc = acc + speed * (g - f)
        acc_ref[i] = acc * column(7, i)


def route_kernel(ids_ref, cnt_ref, own_ref, rest_ref, sel_ref, meta_ref, key_ref, cen_ref, fac_ref, widen_ref):
    lane = iota((TILES, LANES), 1)
    here = lane // 8 == iota((TILES, LANES), 0)
    flat = lambda v: jnp.sum(jnp.where(here, spread(v), 0.0), axis=0, keepdims=True)
    owner, count = flat(own_ref[...]), flat(cnt_ref[...])
    sub = iota((LANES, LANES), 0)
    cols = jnp.where(sub == 0, owner, jnp.where(sub == 1, count, 0.0)).T
    earlier = (cols[:, :1] == owner) & (sub < iota((LANES, LANES), 1))
    rank = jnp.sum(earlier.astype(F32), axis=0, keepdims=True)
    home = owner * 8.0 + rank
    for part in range(2):
        mine = jnp.concatenate([home[:, 64 * x + 32 * part : 64 * x + 32 * part + 32] for x in range(2)], axis=1)
        target = jnp.concatenate([mine + 2.0 * s for s in range(4)], axis=1)
        sel_ref[part] = (iota((512, 256), 0).astype(F32) == target).astype(F32).astype(BF16)
    place = (iota((512, LANES), 0).astype(F32) == home).astype(F32)
    wide = mm(ids_ref[...].astype(F32), (iota((MAXB, LANES), 0) == iota((MAXB, LANES), 1)).astype(F32))
    info = jnp.where(iota((LANES, LANES), 1) == MAXB, cols[:, 1:2], wide)
    meta_ref[...] = mm(place, info).astype(BF16)

    ids, live = listed_rows(ids_ref, cnt_ref)
    number = ids.astype(jnp.int32)
    bx, by, bz = number // (EDGE * EDGE), number // EDGE % EDGE, number % EDGE
    outer = live & (((iota((TILES, LANES), 0) < 8) & (bx >= EDGE // 2)) | ((iota((TILES, LANES), 0) >= 8) & (bx < EDGE // 2)))
    widen = 1.0 + spread(rest_ref[...])
    table = jnp.concatenate(
        [
            jnp.where(outer, ids * 8.0 + (lane % 8).astype(F32), -1.0),
            centre(bx),
            centre(by),
            centre(bz),
            live.astype(F32),
            widen * widen / 4.0,
            jnp.zeros((2 * TILES, LANES), F32),
        ],
        axis=0,
    ).T
    one = iota((1, LANES), 1)
    pick = lambda *pairs: sum((one == at).astype(F32) * value for at, value in pairs)
    plain = pick((0, 1.0), (4, 1.0), (5, 1.0), (6, 1.0), (11, 1.0))
    linear = [pick((1 + d, 1.0), (8 + d, 2.0)) for d in range(3)]
    square = pick((7, 1.0))
    for i in range(TILES):
        wide = lambda which: jnp.broadcast_to(table[:ROWS, which * TILES + i : which * TILES + i + 1], (ROWS, LANES))
        key_ref[i] = wide(0)
        c = [wide(1 + d) for d in range(3)]
        norm = c[0] * c[0] + c[1] * c[1] + c[2] * c[2]
        fac_ref[i] = plain + c[0] * linear[0] + c[1] * linear[1] + c[2] * linear[2] + norm * square
        cen_ref[0, i] = c[0]
        cen_ref[1, i] = jnp.where(wide(4) > 0.0, c[1], FAR)
        cen_ref[2, i] = c[2]
        widen_ref[i] = wide(5)[:8]


def final_kernel(
    part, acc_ref, lo_ref, hi_ref, key_ref, cen_ref, fac_ref, widen_ref, vel_ref, wts_ref, sel_ref, prev_ref, out_ref,
    read, rows, total_ref, cell_ref,
):
    zrow = (iota((8, LANES), 1) % 8).astype(F32)
    tiles4 = [slice(LANES * t, LANES * t + LANES) for t in range(4)]
    places = [(x, y, x * 8 + HALF * part + y, x * HALF + y) for y in range(HALF) for x in range(2)]
    slots = lambda v: v.reshape(MAXB, 8, LANES)
    near = []
    for ref in (lo_ref, hi_ref):
        got = ref[HALF * ROWS :, :LANES].astype(F32)
        near.append(jnp.where(got < 0.0, -2.0, got * 8.0 + zrow))

    for x, y, i, k in places:
        halo = (lo_ref, hi_ref)[x][y * ROWS : y * ROWS + ROWS, :]
        row = near[x][HALF * part + y : HALF * part + y + 1]
        pick_rows = (key_ref[i][:, :ROWS] == row[:, :ROWS]).astype(F32).astype(BF16)
        g = jnp.dot(pick_rows, halo, preferred_element_type=F32)
        cx = cen_ref[0, i]
        speed = jnp.abs(LAM * cx + vel_ref[3:4, :LANES])
        step = jnp.where(cx > 0.0, 2.0 * LAM, -2.0 * LAM)
        parts = []
        for at in tiles4:
            parts.append((acc_ref[i, :, at] + speed * g[:, at]).astype(BF16))
            speed = speed + step
        now = jnp.concatenate(parts, axis=1)
        read[k] = now
        sums = jnp.dot(now, wts_ref[...], preferred_element_type=F32)
        total_ref[k] = jnp.sum(slots(sums * fac_ref[i]), axis=0)

    cells = 2 * HALF * 8
    total = total_ref[...].reshape(cells, LANES)
    at = lambda k: total[:, k : k + 1]
    mass = at(0)
    per = 1.0 / mass
    u = [(at(1 + d) + at(4 + d)) * per for d in range(3)]
    energy = at(7) + at(8) + at(9) + at(10) + at(11)
    warm = (energy * per - (u[0] * u[0] + u[1] * u[1] + u[2] * u[2])) / 3.0
    widen = jnp.concatenate([widen_ref[x * 8 + HALF * part : x * 8 + HALF * part + HALF] for x in range(2)], axis=0)
    aim = warm * widen.reshape(cells, LANES)[:, :1]
    rate = 1.0 - jnp.exp(-IMPACT_KIND * (mass / VB) * jnp.sqrt(warm))
    area = 2.0 * math.pi * aim
    scale = rate * mass / (area * jnp.sqrt(area))
    sharp = 0.5 * math.log2(math.e) / aim
    for k, v in enumerate((u[0], u[1], u[2], -sharp, jnp.sqrt(sharp), scale, 1.0 - rate)):
        cell_ref[k] = jnp.broadcast_to(v, (cells, LANES)).reshape(2 * HALF, 8, LANES)

    for x, y, i, k in places:
        ux, uy, uz, fall, root, scale, keep = (cell_ref[q, k][None] for q in range(7))
        off_y = slots(cen_ref[1, i]) - uy + vel_ref[1:2, :LANES][None]
        off_z = slots(cen_ref[2, i]) - uz + vel_ref[2:3, :LANES][None]
        side = (off_y * off_y + off_z * off_z) * fall
        off_x = (slots(cen_ref[0, i]) - ux + vel_ref[:1, :LANES][None]) * root
        step = root + root
        for at in tiles4:
            now = slots(read[k, :, at].astype(F32))
            after = now * keep + scale * jnp.exp2(side - off_x * off_x)
            rows[:, k * 8 : k * 8 + 8, at] = after.astype(BF16)
            off_x = off_x + step

    for t in range(3):
        out = jnp.dot(sel_ref[part], rows[4 * t : 4 * t + 4].reshape(256, VB), preferred_element_type=F32)
        for k, at in enumerate(tiles4):
            where = slice(32 * t + 8 * k, 32 * t + 8 * k + 8)
            block = out[:, at].reshape(64, 8, LANES)
            if part:
                block = block + prev_ref[:, where, :].astype(F32)
            out_ref[:, where, :] = block.astype(BF16)
    out_ref[:, 96:, :] = prev_ref[:, 96:, :] if part else prev_ref[...].reshape(64, 8, LANES)


def unpack_kernel(got_ref, out_ref, ids_ref, cnt_ref, rows, sems):
    row, col = iota((256, 256), 0), iota((256, 256), 1)
    source = (row % 64) // 2 * 8 + row // 64 * 2 + row % 2
    perm = (col == source).astype(F32).astype(BF16)
    place = iota((LANES, 512), 0)
    pick = (iota((LANES, 512), 1) == place // 2 * 8 + place % 2).astype(F32).astype(BF16)
    meta = got_ref[:, 96:, :].reshape(512, LANES)
    info = jnp.dot(pick, meta, preferred_element_type=F32).T.astype(jnp.int32)
    copies = []
    for t in range(3):
        for g in range(2):
            parts = [got_ref[32 * g : 32 * g + 32, 32 * t + 8 * k : 32 * t + 8 * k + 8, :].reshape(256, LANES) for k in range(4)]
            out = jnp.dot(perm, jnp.concatenate(parts, axis=1), preferred_element_type=F32)
            where = (pl.ds(4 * t, 4), pl.ds(64 * g, 64))
            rows[where] = out.reshape(4, 64, VB).astype(BF16)
            copies.append(pltpu.make_async_copy(rows.at[where], out_ref.at[where], sems.at[2 * t + g]))
            copies[-1].start()
    ids_ref[...] = info[:MAXB].reshape(MAXB, 1, LANES)
    cnt_ref[...] = info[MAXB : MAXB + 1]
    for copy in copies:
        copy.wait()


def call(kernel, outs, scratch=(), flops=0, moved=0, vmem=16 << 20, **extra):
    return pl.pallas_call(
        kernel,
        out_shape=[jax.ShapeDtypeStruct(s, d) for s, d in outs],
        scratch_shapes=list(scratch),
        compiler_params=pltpu.CompilerParams(vmem_limit_bytes=vmem),
        cost_estimate=pl.CostEstimate(flops=flops, bytes_accessed=moved, transcendentals=0),
        **extra,
    )


def tables():
    j = np.arange(VB)
    w = np.stack([j // (BLK * BLK), j // BLK % BLK, j % BLK]).astype(np.float32) - (BLK - 1) / 2.0
    vel = np.zeros((8, VB), np.float32)
    vel[:3] = w
    vel[3:6] = np.float32(LAM) * w
    weights = np.zeros((VB, LANES), np.float32)
    weights[:, [0, 1, 2, 3, 7]] = 1.0
    for d in range(3):
        weights[:, 4 + d] = w[d]
        weights[:, 8 + d] = w[d]
    weights[:, 11] = (w * w).sum(0)
    return vel, weights


def advance(distribution, block_ids, cell_counts, owner, restitution):
    nx, ny, nz = (lax.axis_size(a) for a in ("gx", "gy", "gz"))

    def up(v, axis, n):
        return lax.ppermute(v, axis, [(i, (i + 1) % n) for i in range(n)])

    def down(v, axis, n):
        return lax.ppermute(v, axis, [((i + 1) % n, i) for i in range(n)])

    d = distribution.transpose(0, 1, 3, 2, 4).reshape(TILES, ROWS, VB)
    ids = block_ids.reshape(TILES * 8, MAXB)
    cnt = cell_counts.reshape(TILES, 8)
    own = owner.reshape(TILES, 8)
    rest = restitution.reshape(TILES, 8)
    vel, weights = tables()
    vel, weights = jnp.asarray(vel), jnp.asarray(weights, BF16)

    face_x = ((HALF * ROWS + 8, VB), BF16)
    face_y, face_z = ((2, ROWS + 8, VB), BF16), ((TILES, 16, VB), BF16)
    flat = d.reshape(TILES * ROWS, VB)
    hbm, whole = pl.BlockSpec(memory_space=pltpu.HBM), pl.BlockSpec(memory_space=pltpu.VMEM)
    xlo, xhi, ylo, yhi, zlo, zhi = call(
        front_kernel,
        [face_x, face_x, face_y, face_y, face_z, face_z],
        scratch=[
            pltpu.VMEM((TILES * ROWS, VB), BF16),
            pltpu.VMEM((TILES * 8, MAXB), jnp.int32),
            pltpu.VMEM((TILES, 8), jnp.int32),
            pltpu.SemaphoreType.DMA((8,)),
        ],
        flops=10**8,
        moved=4 * 10**6,
        in_specs=[hbm] * 3,
    )(*(pltpu.with_memory_space_constraint(v, pltpu.HBM) for v in (flat, ids, cnt)))
    near_x = [(up(xhi, "gx", nx), down(xlo, "gx", nx))]
    xlo, xhi = call(
        face_kernel,
        [face_x, face_x],
        scratch=[pltpu.SemaphoreType.DMA((2,))],
        moved=2 * 10**6,
        in_specs=[pl.BlockSpec(memory_space=pl.ANY), whole, whole],
    )(flat, ids, cnt)
    near_x.append((up(xhi, "gx", nx), down(xlo, "gx", nx)))
    y_hi, y_lo = down(ylo, "gy", ny), up(yhi, "gy", ny)
    z_hi, z_lo = down(zlo, "gz", nz), up(zhi, "gz", nz)
    (acc,) = call(local_kernel, [((TILES, ROWS, VB), F32)], flops=10**9, moved=6 * 10**6)(
        d, y_lo, y_hi, z_lo, z_hi, ids, cnt, vel
    )
    wide = ((TILES, ROWS, LANES), F32)
    sel, meta, keys, centres, factors, widen = call(
        route_kernel,
        [((2, 512, 256), BF16), ((512, LANES), BF16), wide, ((3, TILES, ROWS, LANES), F32), wide, ((TILES, 8, LANES), F32)],
        flops=10**7,
        moved=10**6,
    )(ids, cnt, own, rest)
    out = meta
    for part in range(2):
        (out,) = call(
            functools.partial(final_kernel, part),
            [((64, 104, LANES), BF16)],
            scratch=[
                pltpu.VMEM((2 * HALF, ROWS, VB), BF16),
                pltpu.VMEM((MAXB, 2 * HALF * 8, VB), BF16),
                pltpu.VMEM((2 * HALF, 8, LANES), F32),
                pltpu.VMEM((7, 2 * HALF, 8, LANES), F32),
            ],
            flops=10**9,
            moved=4 * 10**6,
        )(acc, *near_x[part], keys, centres, factors, widen, vel, weights, sel, out)
    got = lax.all_to_all(out, ("gx", "gz"), split_axis=0, concat_axis=0, tiled=True)
    moved, moved_ids, moved_counts = call(
        unpack_kernel,
        [((MAXB, LANES, VB), BF16), ((MAXB, 1, LANES), jnp.int32), ((1, LANES), jnp.int32)],
        scratch=[pltpu.VMEM((MAXB, LANES, VB), BF16), pltpu.SemaphoreType.DMA((6,))],
        flops=4 * 10**8,
        moved=4 * 10**6,
        out_specs=[pl.BlockSpec(memory_space=pl.ANY), whole, whole],
    )(got)
    return (
        moved.transpose(1, 0, 2).reshape(1, LANES, MAXB, VB),
        moved_ids.transpose(1, 2, 0),
        moved_counts,
    )


def solution(mesh):
    placed = (
        P("gx", "gy", "gz", None, None),
        P("gx", "gy", "gz", None),
        P("gx", "gy", "gz"),
        P("gx", "gy", "gz"),
        P("gx", "gy", "gz"),
    )
    return jax.shard_map(
        advance,
        mesh=mesh,
        in_specs=placed,
        out_specs=(
            P("gy", ("gx", "gz"), None, None),
            P("gy", ("gx", "gz"), None),
            P("gy", ("gx", "gz")),
        ),
        check_vma=False,
    )
```

time: 103 us -> 88 us (0.85)
  starting transfers between devices: 24 us -> 16.5 us
  local copies, waits for them, and re-layouts: 7.44 us -> 1.41 us
  waiting for transfers between devices: 3.68 us -> 1.04 us
  blocking collectives: 49.3 us -> 51.3 us
  Pallas kernels: 17.7 us -> 16.4 us
    all_to_all x1 -> x0, starting transfers between devices: 9.34 us -> none  [on_device(): lax.all_to_all(v, ('gx', 'gz'), split_axis=0, concat_axis=0, tiled=True)]
    unnamed x25 -> x14, local copies, waits for them, and re-layouts: 4.67 us -> 1.41 us
    slice x1 -> x0, local copies, waits for them, and re-layouts: 2.77 us -> none  [on_device(): x_hi = down(d[:8], 'gx', nx)]
    ppermute x4, waiting for transfers between devices: 3.67 us -> 1.03 us  [up(): return lax.ppermute(v, axis, [(i, (i + 1) % n) for i in range(n)])]
    all_to_all x1, blocking collectives: 49.3 us -> 51.3 us  [advance(): lax.all_to_all(out, ('gx', 'gz'), split_axis=0, concat_axis=0, tiled=True)]
    pallas_call x5 -> x7, Pallas kernels: 17.7 us -> 16.4 us  [the longest x2 5.59 us: advance(): call(functools.partial(final_kernel, part), [((64, 104, LANES), BF16)], s...]
  transfers between devices with their start and end apart: 9 -> 8, of which waited for: 1 -> 1; matrix products, arithmetic and copies ran while one was open for 0% -> 0% of each run, Pallas kernels for 15% -> 11%
where the time goes in v2:
time: 88 us; the launch traced here: 87.6 us
  blocking collectives  51.3 us (58%)
  starting transfers between devices  16.5 us (19%)
  Pallas kernels  16.4 us (19%)
  local copies, waits for them, and re-layouts  1.41 us (2%)
  waiting for transfers between devices  1.04 us (1%)
  between operations  0.93 us (1%)
    all_to_all x1, blocking collectives, advance(): lax.all_to_all(out, ('gx', 'gz'), split_axis=0, concat_axis=0, tiled=True)  51.3 us
    ppermute x4, starting transfers between devices, down(): return lax.ppermute(v, axis, [((i + 1) % n, i) for i in range(n)])  10.4 us
    ppermute x4, starting transfers between devices, up(): return lax.ppermute(v, axis, [(i, (i + 1) % n) for i in range(n)])  6.04 us
    pallas_call x2, Pallas kernels, advance(): call(functools.partial(final_kernel, part), [((64, 104, LANES), BF16)], s...  5.59 us
    pallas_call x1, Pallas kernels, advance(): call(local_kernel, [((TILES, ROWS, VB), F32)], flops=10 ** 9, moved=6 * 1...  4.11 us
    pallas_call x1, Pallas kernels, advance(): call(route_kernel, [((2, 512, 256), BF16), ((512, LANES), BF16), wide, ((...  2.11 us
    pallas_call x1, Pallas kernels, advance(): call(front_kernel, [face_x, face_x, face_y, face_y, face_z, face_z], scra...  2.07 us
    pallas_call x1, Pallas kernels, advance(): call(unpack_kernel, [((MAXB, LANES, VB), BF16), ((MAXB, 1, LANES), jnp.in...  2.03 us
  transfers between devices with their start and end apart: 8, of which 1 were waited for; matrix products, arithmetic and copies ran while one was open for 0% of the time, Pallas kernels for 11%

profile of v2, /device:TPU:1, one launch (start us, length us, event | category | flops | bytes accessed | tf_op | source)
XLA Modules:
  0.0 87.6 jit_solution(7261073963883938482)
XLA Ops:
  0.6 0.0 copy-start.3
  0.6 0.0 copy-start
  0.7 2.1 %shard_map.94 = (bf16[392,512]{1,0:T(8,128)(2,1)S(1)}, bf16[392,512]{1,0:T(8,128)(2,1)S(1)}, bf16[2,104,512]{2,1,0:T(8,128)(2,1)S(1)}, bf16[2,104,512]{2,1,0:T(8...) custom-call(bf16[1536,512]{1,0:T(8,128)(2,1)} %bitcast.13, s32[128,12]{1,0:T(8,128)} %bitcast.16, ...), custom_call_target="tpu_custom_call" | custom-call | flops 100000000 | bytes 4000000 | tf_op jit(solution)/shard_map/pallas_call | solution.py:383
  2.7 2.6 %collective-permute-start.2 = (bf16[16,16,512]{2,1,0:T(8,128)(2,1)S(1)}, bf16[16,16,512]{2,1,0:T(8,128)(2,1)S(1)}, u32[]{:S(2)}, u32[]{:S(2)}) collective-permute-start(bf16[16,16,512]{2,1,0:T(8,128)(2,1)S(1)} %get-tuple-element.22), channel_id=1, source_target_pairs={{0,1},{1,2},{2,3},{3,4},{4,5},{5,6},{6,7},{7,0},{8,9},{9,10},{10,1... | collective-permute-start | bytes 786440 | tf_op jit(solution)/shard_map/ppermute | solution.py:366
  5.4 1.3 %collective-permute-start = (bf16[2,104,512]{2,1,0:T(8,128)(2,1)S(1)}, bf16[2,104,512]{2,1,0:T(8,128)(2,1)S(1)}, u32[]{:S(2)}, u32[]{:S(2)}) collective-permute-start(bf16[2,104,512]{2,1,0:T(8,128)(2,1)S(1)} %get-tuple-element.20), channel_id=1, source_target_pairs={{0,8},{8,16},{16,24},{24,0},{1,9},{9,17},{17,25},{25,1},{2,10},{10... | collective-permute-start | bytes 638984 | tf_op jit(solution)/shard_map/ppermute | solution.py:366
  6.6 1.4 %collective-permute-start.1 = (bf16[2,104,512]{2,1,0:T(8,128)(2,1)S(1)}, bf16[2,104,512]{2,1,0:T(8,128)(2,1)S(1)}, u32[]{:S(2)}, u32[]{:S(2)}) collective-permute-start(bf16[2,104,512]{2,1,0:T(8,128)(2,1)S(1)} %get-tuple-element.21), channel_id=1, source_target_pairs={{8,0},{16,8},{24,16},{0,24},{9,1},{17,9},{25,17},{1,25},{10,2},{18... | collective-permute-start | bytes 638984 | tf_op jit(solution)/shard_map/ppermute | solution.py:369
  8.1 1.6 %collective-permute-start.6 = (bf16[392,512]{1,0:T(8,128)(2,1)S(1)}, bf16[392,512]{1,0:T(8,128)(2,1)S(1)}, u32[]{:S(2)}, u32[]{:S(2)}) collective-permute-start(bf16[392,512]{1,0:T(8,128)(2,1)S(1)} %get-tuple-element.31), channel_id=1, source_target_pairs={{0,32},{32,64},{64,96},{96,128},{128,160},{160,192},{192,224},{224... | collective-permute-start | bytes 1204232 | tf_op jit(solution)/shard_map/ppermute | solution.py:366
  9.7 3.9 %collective-permute-start.7 = (bf16[392,512]{1,0:T(8,128)(2,1)S(1)}, bf16[392,512]{1,0:T(8,128)(2,1)S(1)}, u32[]{:S(2)}, u32[]{:S(2)}) collective-permute-start(bf16[392,512]{1,0:T(8,128)(2,1)S(1)} %get-tuple-element.32), channel_id=1, source_target_pairs={{32,0},{64,32},{96,64},{128,96},{160,128},{192,160},{224,192},{0,2... | collective-permute-start | bytes 1204232 | tf_op jit(solution)/shard_map/ppermute | solution.py:369
  13.7 0.0 collective-permute-done.ylo
  13.7 0.6 collective-permute-start.3
  14.3 0.0 copy-done
  14.3 0.7 copy-done.4
  15.0 0.5 shard_map.96
  15.5 0.0 collective-permute-done.1.yhi
  15.5 0.5 collective-permute-start.4
  16.0 0.0 collective-permute-done.2.zlo
  16.1 4.4 %collective-permute-start.5 = (bf16[392,512]{1,0:T(8,128)(2,1)S(1)}, bf16[392,512]{1,0:T(8,128)(2,1)S(1)}, u32[]{:S(2)}, u32[]{:S(2)}) collective-permute-start(bf16[392,512]{1,0:T(8,128)(2,1)S(1)} %get-tuple-element.25), channel_id=1, source_target_pairs={{32,0},{64,32},{96,64},{128,96},{160,128},{192,160},{224,192},{0,2... | collective-permute-start | bytes 1204232 | tf_op jit(solution)/shard_map/ppermute | solution.py:369
  20.5 0.7 copy-done.6
  21.2 2.1 %shard_map.97 = (bf16[2,512,256]{2,1,0:T(8,128)(2,1)S(1)}, bf16[512,128]{1,0:T(8,128)(2,1)S(1)}, f32[16,96,128]{2,1,0:T(8,128)S(1)}, f32[3,16,96,128]{3,2,1,0:T(...) custom-call(s32[128,12]{1,0:T(8,128)S(1)} %bitcast.18, s32[16,8]{1,0:T(8,128)S(1)} %bitcast.22, ...), custom_call_target="tpu_custom_call" | custom-call | flops 10000000 | bytes 1000000 | tf_op jit(solution)/shard_map/pallas_call | solution.py:411
  23.3 0.0 collective-permute-done.3.zhi
  23.3 0.0 copy-done.3
  23.3 0.0 copy-start.2
  23.3 4.1 %shard_map.95.acc_ref = f32[16,96,512]{2,1,0:T(8,128)S(1)} custom-call(bf16[16,96,512]{2,1,0:T(8,128)(2,1)S(1)} %bitcast.15, bf16[2,104,512]{2,1,0:T(8,128)(2,1)S(1)} %collective-permute-done.ylo, bf16[2,104,512]{2,1,0:T(8,128)(2,1)S(1)} %collective-permute-done.1.yhi, bf16[16,16,512]{2,1,0:T(8,128)(2,1)S(1)} %collective-permute-done.2.zlo, ...), custom_call_target="tpu_custom_call" | custom-call | flops 1000000000 | bytes 6000000 | tf_op jit(solution)/shard_map/pallas_call | solution.py:407
  27.5 0.0 collective-permute-done.6.lo_ref
  27.5 0.0 collective-permute-done.7.hi_ref
  27.5 0.0 copy-done.2
  27.5 2.8 %shard_map.98.prev_ref = bf16[64,104,128]{2,1,0:T(8,128)(2,1)S(1)} custom-call(f32[16,96,512]{2,1,0:T(8,128)S(1)} %shard_map.95.acc_ref, bf16[392,512]{1,0:T(8,128)(2,1)S(1)} %collective-permute-done.6.lo_ref, bf16[392,512]{1,0:T(8,128)(2,1)S(1)} %collective-permute-done.7.hi_ref, f32[16,96,128]{2,1,0:T(8,128)S(1)} %get-tuple-element.26.key_ref, ...), custom_call_target="tpu_custom_call" | custom-call | flops 1000000000 | bytes 4000000 | tf_op jit(solution)/shard_map/pallas_call | solution.py:419
  30.3 1.0 %collective-permute-done.4.lo_ref = bf16[392,512]{1,0:T(8,128)(2,1)S(1)} collective-permute-done((bf16[392,512]{1,0:T(8,128)(2,1)S(1)}, bf16[392,512]{1,0:T(8,128)(2,1)S(1)}, u32[]{:S(2)}, u32[]{:S(2)}) %collective-permute-start.4) | collective-permute-done | bytes 401440 | tf_op jit(solution)/shard_map/ppermute | solution.py:366
  31.3 0.0 collective-permute-done.5.hi_ref
  31.3 2.8 %shard_map.99 = bf16[64,104,128]{2,1,0:T(8,128)(2,1)S(1)} custom-call(f32[16,96,512]{2,1,0:T(8,128)S(1)} %shard_map.95.acc_ref, bf16[392,512]{1,0:T(8,128)(2,1)S(1)} %collective-permute-done.4.lo_ref, bf16[392,512]{1,0:T(8,128)(2,1)S(1)} %collective-permute-done.5.hi_ref, f32[16,96,128]{2,1,0:T(8,128)S(1)} %get-tuple-element.26.key_ref, ...), custom_call_target="tpu_custom_call" | custom-call | flops 1000000000 | bytes 4000000 | tf_op jit(solution)/shard_map/pallas_call | solution.py:419
  34.1 51.3 %all_to_all.5.got_ref = bf16[64,104,128]{2,1,0:T(8,128)(2,1)S(1)} all-to-all(bf16[64,104,128]{2,1,0:T(8,128)(2,1)S(1)} %shard_map.99), channel_id=1, replica_groups=mesh['gx'=8,'gy'=4,'gz'=8] {'gx','gz'}, dimensions={0} | all-to-all | bytes 3407872 | tf_op jit(solution)/shard_map/all_to_all | solution.py:431
  85.4 2.0 %shard_map.100 = (bf16[12,128,512]{2,1,0:T(8,128)(2,1)}, s32[12,1,128]{2,1,0:T(1,128)}, s32[1,128]{1,0:T(1,128)}) custom-call(bf16[64,104,128]{2,1,0:T(8,128)(2,1)S(1)} %all_to_all.5.got_ref), custom_call_target="tpu_custom_call" | custom-call | flops 400000000 | bytes 4000000 | tf_op jit(solution)/shard_map/pallas_call | solution.py:432
  (6 shorter events, 0.0 us)
Async XLA Ops:
  0.6 22.7 %copy-start.3 = (f32[8,512]{1,0:T(8,128)S(1)}, f32[8,512]{1,0:T(8,128)}, u32[]{:S(2)}) copy-start(f32[8,512]{1,0:T(8,128)} %constant.4.clone.vel_ref) | copy-start | bytes 49156
  0.6 13.6 %copy-start = (bf16[2,8,8,12,512]{4,2,3,1,0:T(8,128)(2,1)S(1)}, bf16[2,8,8,12,512]{4,2,3,1,0:T(8,128)(2,1)}, u32[]{:S(2)}) copy-start(bf16[2,8,8,12,512]{4,2,3,1,0:T(8,128)(2,1)} %param.7) | copy-start | bytes 4718596
  0.7 13.6 %copy-start.1 = (s32[2,8,8,12]{3,2,1,0:T(8,128)S(1)}, s32[2,8,8,12]{3,2,1,0:T(8,128)}, u32[]{:S(2)}) copy-start(s32[2,8,8,12]{3,2,1,0:T(8,128)} %param.8) | copy-start | bytes 18436
  0.7 19.8 %copy-start.5 = (s32[2,8,8]{2,1,0:T(8,128)S(1)}, s32[2,8,8]{2,1,0:T(8,128)}, u32[]{:S(2)}) copy-start(s32[2,8,8]{2,1,0:T(8,128)} %param.10) | copy-start | bytes 1540
  2.7 13.3 %collective-permute-start.2 = (bf16[16,16,512]{2,1,0:T(8,128)(2,1)S(1)}, bf16[16,16,512]{2,1,0:T(8,128)(2,1)S(1)}, u32[]{:S(2)}, u32[]{:S(2)}) collective-permute-start(bf16[16,16,512]{2,1,0:T(8,128)(2,1)S(1)} %get-tuple-element.22), channel_id=1, source_target_pairs={{0,1},{1,2},{2,3},{3,4},{4,5},{5,6},{6,7},{7,0},{8,9},{9,10},{10,1... | collective-permute-start | bytes 786440 | tf_op jit(solution)/shard_map/ppermute | solution.py:366
  5.4 8.3 %collective-permute-start = (bf16[2,104,512]{2,1,0:T(8,128)(2,1)S(1)}, bf16[2,104,512]{2,1,0:T(8,128)(2,1)S(1)}, u32[]{:S(2)}, u32[]{:S(2)}) collective-permute-start(bf16[2,104,512]{2,1,0:T(8,128)(2,1)S(1)} %get-tuple-element.20), channel_id=1, source_target_pairs={{0,8},{8,16},{16,24},{24,0},{1,9},{9,17},{17,25},{25,1},{2,10},{10... | collective-permute-start | bytes 638984 | tf_op jit(solution)/shard_map/ppermute | solution.py:366
  6.6 8.9 %collective-permute-start.1 = (bf16[2,104,512]{2,1,0:T(8,128)(2,1)S(1)}, bf16[2,104,512]{2,1,0:T(8,128)(2,1)S(1)}, u32[]{:S(2)}, u32[]{:S(2)}) collective-permute-start(bf16[2,104,512]{2,1,0:T(8,128)(2,1)S(1)} %get-tuple-element.21), channel_id=1, source_target_pairs={{8,0},{16,8},{24,16},{0,24},{9,1},{17,9},{25,17},{1,25},{10,2},{18... | collective-permute-start | bytes 638984 | tf_op jit(solution)/shard_map/ppermute | solution.py:369
  8.1 19.4 %collective-permute-start.6 = (bf16[392,512]{1,0:T(8,128)(2,1)S(1)}, bf16[392,512]{1,0:T(8,128)(2,1)S(1)}, u32[]{:S(2)}, u32[]{:S(2)}) collective-permute-start(bf16[392,512]{1,0:T(8,128)(2,1)S(1)} %get-tuple-element.31), channel_id=1, source_target_pairs={{0,32},{32,64},{64,96},{96,128},{128,160},{160,192},{192,224},{224... | collective-permute-start | bytes 1204232 | tf_op jit(solution)/shard_map/ppermute | solution.py:366
  9.7 17.7 %collective-permute-start.7 = (bf16[392,512]{1,0:T(8,128)(2,1)S(1)}, bf16[392,512]{1,0:T(8,128)(2,1)S(1)}, u32[]{:S(2)}, u32[]{:S(2)}) collective-permute-start(bf16[392,512]{1,0:T(8,128)(2,1)S(1)} %get-tuple-element.32), channel_id=1, source_target_pairs={{32,0},{64,32},{96,64},{128,96},{160,128},{192,160},{224,192},{0,2... | collective-permute-start | bytes 1204232 | tf_op jit(solution)/shard_map/ppermute | solution.py:369
  13.7 9.6 %collective-permute-start.3 = (bf16[16,16,512]{2,1,0:T(8,128)(2,1)S(1)}, bf16[16,16,512]{2,1,0:T(8,128)(2,1)S(1)}, u32[]{:S(2)}, u32[]{:S(2)}) collective-permute-start(bf16[16,16,512]{2,1,0:T(8,128)(2,1)S(1)} %get-tuple-element.23), channel_id=1, source_target_pairs={{1,0},{2,1},{3,2},{4,3},{5,4},{6,5},{7,6},{0,7},{9,8},{10,9},{11,1... | collective-permute-start | bytes 786440 | tf_op jit(solution)/shard_map/ppermute | solution.py:369
  14.3 0.7 copy-start.4
  15.5 15.7 %collective-permute-start.4 = (bf16[392,512]{1,0:T(8,128)(2,1)S(1)}, bf16[392,512]{1,0:T(8,128)(2,1)S(1)}, u32[]{:S(2)}, u32[]{:S(2)}) collective-permute-start(bf16[392,512]{1,0:T(8,128)(2,1)S(1)} %get-tuple-element.24), channel_id=1, source_target_pairs={{0,32},{32,64},{64,96},{96,128},{128,160},{160,192},{192,224},{224... | collective-permute-start | bytes 1204232 | tf_op jit(solution)/shard_map/ppermute | solution.py:366
  16.1 15.2 %collective-permute-start.5 = (bf16[392,512]{1,0:T(8,128)(2,1)S(1)}, bf16[392,512]{1,0:T(8,128)(2,1)S(1)}, u32[]{:S(2)}, u32[]{:S(2)}) collective-permute-start(bf16[392,512]{1,0:T(8,128)(2,1)S(1)} %get-tuple-element.25), channel_id=1, source_target_pairs={{32,0},{64,32},{96,64},{128,96},{160,128},{192,160},{224,192},{0,2... | collective-permute-start | bytes 1204232 | tf_op jit(solution)/shard_map/ppermute | solution.py:369
  20.5 0.7 copy-start.6
  23.3 4.2 %copy-start.2 = (bf16[512,128]{1,0:T(8,128)(2,1)S(1)}, bf16[512,128]{1,0:T(8,128)(2,1)}, u32[]{:S(2)}) copy-start(bf16[512,128]{1,0:T(8,128)(2,1)} %constant.5.clone.wts_ref) | copy-start | bytes 393220

commit v3 on v2

--- a/solution.py
+++ b/solution.py
@@ -78,13 +78,16 @@
         copy.wait()
 
 
-def front_kernel(d_hbm, ids_hbm, cnt_hbm, lo, hi, ylo, yhi, zlo, zhi, d_ref, ids_ref, cnt_ref, sems):
+def front_kernel(
+    d_hbm, ids_hbm, cnt_hbm, own_hbm, rest_hbm, lo, hi, ylo, yhi, zlo, zhi, ids_ref, cnt_ref, own_ref, rest_ref, d_ref, sems
+):
     small = [pltpu.make_async_copy(ids_hbm, ids_ref, sems.at[2]), pltpu.make_async_copy(cnt_hbm, cnt_ref, sems.at[3])]
+    later = [pltpu.make_async_copy(own_hbm, own_ref, sems.at[8]), pltpu.make_async_copy(rest_hbm, rest_ref, sems.at[9])]
     large = x_copies(0, d_hbm, (lo, hi), sems)
     quarter = TILES // 4 * ROWS
     parts = [pl.ds(q * quarter, quarter) for q in range(4)]
     whole = [pltpu.make_async_copy(d_hbm.at[p], d_ref.at[p], sems.at[4 + q]) for q, p in enumerate(parts)]
-    for copy in small + whole + large:
+    for copy in small + whole + large + later:
         copy.start()
     for copy in small:
         copy.wait()
@@ -118,7 +121,7 @@
             first = jnp.where(key_row, jnp.broadcast_to(key[i : i + 1], (16, LANES)), face[:, :LANES])
             out[i, :, :LANES] = first.astype(BF16)
             out[i, :, LANES:] = face[:, LANES:].astype(BF16)
-    for copy in large:
+    for copy in large + later:
         copy.wait()
 
 
@@ -198,9 +201,12 @@
     home = owner * 8.0 + rank
     for part in range(2):
         mine = jnp.concatenate([home[:, 64 * x + 32 * part : 64 * x + 32 * part + 32] for x in range(2)], axis=1)
-        target = jnp.concatenate([mine + 2.0 * s for s in range(4)], axis=1)
+        mine = mine.astype(jnp.int32)
+        shifts = [(mine % 8 + mine // 8 * 2 + 2 * s) % 8 for s in range(4)]
+        target = jnp.concatenate([mine // 8 * 8 + shift for shift in shifts], axis=1).astype(F32)
         sel_ref[part] = (iota((512, 256), 0).astype(F32) == target).astype(F32).astype(BF16)
-    place = (iota((512, LANES), 0).astype(F32) == home).astype(F32)
+    phase = 2 * (owner.astype(jnp.int32) % 4)
+    place = (iota((512, LANES), 0).astype(F32) == home + phase.astype(F32)).astype(F32)
     wide = mm(ids_ref[...].astype(F32), (iota((MAXB, LANES), 0) == iota((MAXB, LANES), 1)).astype(F32))
     info = jnp.where(iota((LANES, LANES), 1) == MAXB, cols[:, 1:2], wide)
     meta_ref[...] = mm(place, info).astype(BF16)
@@ -299,34 +305,60 @@
             rows[:, k * 8 : k * 8 + 8, at] = after.astype(BF16)
             off_x = off_x + step
 
+    def put(tile, value):
+        where = slice(8 * tile, 8 * tile + 8)
+        if part:
+            value = value + prev_ref[:, where, :].astype(F32)
+        out_ref[:, where, :] = value.astype(BF16)
+
+    sub = iota((16, 8, LANES), 1)
+    info = jnp.zeros((16, 4, 8, LANES), F32) if part else prev_ref[...].astype(F32).reshape(16, 4, 8, LANES)
+    before = [None] + [info[:, p - 1] for p in range(1, 4)]
     for t in range(3):
         out = jnp.dot(sel_ref[part], rows[4 * t : 4 * t + 4].reshape(256, VB), preferred_element_type=F32)
+        out = out.reshape(16, 4, 8, VB)
         for k, at in enumerate(tiles4):
-            where = slice(32 * t + 8 * k, 32 * t + 8 * k + 8)
-            block = out[:, at].reshape(64, 8, LANES)
-            if part:
-                block = block + prev_ref[:, where, :].astype(F32)
-            out_ref[:, where, :] = block.astype(BF16)
-    out_ref[:, 96:, :] = prev_ref[:, 96:, :] if part else prev_ref[...].reshape(64, 8, LANES)
+            for p in range(4):
+                value = out[:, p, :, at]
+                put(12 * p + 4 * t + k, jnp.where(sub >= 2 * p, value, before[p]) if p else value)
+                before[p] = value
+    put(48, jnp.where(sub >= 6, info[:, 3], before[3]))
+    for p in (1, 2):
+        where = slice(96 * (p + 1), 96 * (p + 1) + 8)
+        value = out_ref[:, where, :].astype(F32) + jnp.where(sub < 2 * p, before[p], 0.0)
+        out_ref[:, where, :] = value.astype(BF16)
 
 
 def unpack_kernel(got_ref, out_ref, ids_ref, cnt_ref, rows, sems):
     row, col = iota((256, 256), 0), iota((256, 256), 1)
-    source = (row % 64) // 2 * 8 + row // 64 * 2 + row % 2
-    perm = (col == source).astype(F32).astype(BF16)
-    place = iota((LANES, 512), 0)
-    pick = (iota((LANES, 512), 1) == place // 2 * 8 + place % 2).astype(F32).astype(BF16)
-    meta = got_ref[:, 96:, :].reshape(512, LANES)
-    info = jnp.dot(pick, meta, preferred_element_type=F32).T.astype(jnp.int32)
+    slot, source, rank = row // 64, row % 64 // 2, row % 2
+    phase = source % 4
+    perm = (col == phase * 64 + source // 4 * 8 + (2 * slot + rank + 2 * phase) % 8).astype(F32).astype(BF16)
+    sub = iota((1, 8, LANES), 1)
+    upper = [None] + [(sub >= 2 * p).astype(F32).astype(BF16) for p in range(1, 4)]
+    lower = [None] + [(sub < 2 * p).astype(F32).astype(BF16) for p in range(1, 4)]
     copies = []
     for t in range(3):
         for g in range(2):
-            parts = [got_ref[32 * g : 32 * g + 32, 32 * t + 8 * k : 32 * t + 8 * k + 8, :].reshape(256, LANES) for k in range(4)]
-            out = jnp.dot(perm, jnp.concatenate(parts, axis=1), preferred_element_type=F32)
+            tile = lambda n: got_ref[8 * g : 8 * g + 8, 8 * n : 8 * n + 8, :]
+            lanes = []
+            for k in range(4):
+                parts = [tile(4 * t + k).reshape(64, LANES)]
+                for p in range(1, 4):
+                    n = 12 * p + 4 * t + k
+                    parts.append((tile(n) * upper[p] + tile(n + 1) * lower[p]).reshape(64, LANES))
+                lanes.append(jnp.concatenate(parts, axis=0))
+            out = jnp.dot(perm, jnp.concatenate(lanes, axis=1), preferred_element_type=F32)
             where = (pl.ds(4 * t, 4), pl.ds(64 * g, 64))
             rows[where] = out.reshape(4, 64, VB).astype(BF16)
             copies.append(pltpu.make_async_copy(rows.at[where], out_ref.at[where], sems.at[2 * t + g]))
             copies[-1].start()
+    place = iota((LANES, 512), 0)
+    source, rank = place // 2, place % 2
+    phase = source % 4
+    pick = (iota((LANES, 512), 1) == phase * 128 + source // 4 * 8 + 2 * phase + rank).astype(F32).astype(BF16)
+    meta = jnp.concatenate([got_ref[:, 96 * p : 96 * p + 8, :].reshape(128, LANES) for p in range(1, 5)], axis=0)
+    info = jnp.dot(pick, meta, preferred_element_type=F32).T.astype(jnp.int32)
     ids_ref[...] = info[:MAXB].reshape(MAXB, 1, LANES)
     cnt_ref[...] = info[MAXB : MAXB + 1]
     for copy in copies:
@@ -380,19 +412,15 @@
     face_y, face_z = ((2, ROWS + 8, VB), BF16), ((TILES, 16, VB), BF16)
     flat = d.reshape(TILES * ROWS, VB)
     hbm, whole = pl.BlockSpec(memory_space=pltpu.HBM), pl.BlockSpec(memory_space=pltpu.VMEM)
-    xlo, xhi, ylo, yhi, zlo, zhi = call(
+    small = [((TILES * 8, MAXB), jnp.int32), ((TILES, 8), jnp.int32), ((TILES, 8), jnp.int32), ((TILES, 8), BF16)]
+    xlo, xhi, ylo, yhi, zlo, zhi, ids, cnt, own, rest = call(
         front_kernel,
-        [face_x, face_x, face_y, face_y, face_z, face_z],
-        scratch=[
-            pltpu.VMEM((TILES * ROWS, VB), BF16),
-            pltpu.VMEM((TILES * 8, MAXB), jnp.int32),
-            pltpu.VMEM((TILES, 8), jnp.int32),
-            pltpu.SemaphoreType.DMA((8,)),
-        ],
+        [face_x, face_x, face_y, face_y, face_z, face_z] + small,
+        scratch=[pltpu.VMEM((TILES * ROWS, VB), BF16), pltpu.SemaphoreType.DMA((10,))],
         flops=10**8,
         moved=4 * 10**6,
-        in_specs=[hbm] * 3,
-    )(*(pltpu.with_memory_space_constraint(v, pltpu.HBM) for v in (flat, ids, cnt)))
+        in_specs=[hbm] * 5,
+    )(*(pltpu.with_memory_space_constraint(v, pltpu.HBM) for v in (flat, ids, cnt, own, rest)))
     near_x = [(up(xhi, "gx", nx), down(xlo, "gx", nx))]
     xlo, xhi = call(
         face_kernel,
@@ -418,7 +446,7 @@
     for part in range(2):
         (out,) = call(
             functools.partial(final_kernel, part),
-            [((64, 104, LANES), BF16)],
+            [((16, 392, LANES), BF16)],
             scratch=[
                 pltpu.VMEM((2 * HALF, ROWS, VB), BF16),
                 pltpu.VMEM((MAXB, 2 * HALF * 8, VB), BF16),
@@ -428,7 +456,8 @@
             flops=10**9,
             moved=4 * 10**6,
         )(acc, *near_x[part], keys, centres, factors, widen, vel, weights, sel, out)
-    got = lax.all_to_all(out, ("gx", "gz"), split_axis=0, concat_axis=0, tiled=True)
+    out = out.reshape(64, 49, 2, LANES)
+    got = lax.all_to_all(out, ("gx", "gz"), split_axis=0, concat_axis=0, tiled=True).reshape(16, 392, LANES)
     moved, moved_ids, moved_counts = call(
         unpack_kernel,
         [((MAXB, LANES, VB), BF16), ((MAXB, 1, LANES), jnp.int32), ((1, LANES), jnp.int32)],

time: 88 us -> 86 us (0.977)
  blocking collectives: 51.3 us -> 49 us
  waiting for transfers between devices: 1.04 us -> 2.72 us
  local copies, waits for them, and re-layouts: 1.41 us -> 0.02 us
    all_to_all x1, blocking collectives: 51.3 us -> 49 us  [advance(): lax.all_to_all(out, ('gx', 'gz'), split_axis=0, concat_axis=0, tiled=True)]
    ppermute x4, waiting for transfers between devices: 1.03 us -> 2.71 us  [up(): return lax.ppermute(v, axis, [(i, (i + 1) % n) for i in range(n)])]
    unnamed x14 -> x6, local copies, waits for them, and re-layouts: 1.41 us -> 0.02 us
where the time goes in v3:
time: 86 us; the launch traced here: 85.9 us
  blocking collectives  49 us (57%)
  Pallas kernels  16.7 us (19%)
  starting transfers between devices  16.5 us (19%)
  waiting for transfers between devices  2.72 us (3%)
  between operations  0.92 us (1%)
    all_to_all x1, blocking collectives, advance(): lax.all_to_all(out, ('gx', 'gz'), split_axis=0, concat_axis=0, tiled=True)  49 us
    ppermute x4, starting transfers between devices, down(): return lax.ppermute(v, axis, [((i + 1) % n, i) for i in range(n)])  10.4 us
    ppermute x4, starting transfers between devices, up(): return lax.ppermute(v, axis, [(i, (i + 1) % n) for i in range(n)])  6.03 us
    pallas_call x2, Pallas kernels, advance(): call(functools.partial(final_kernel, part), [((16, 392, LANES), BF16)], s...  5.66 us
    pallas_call x1, Pallas kernels, advance(): call(local_kernel, [((TILES, ROWS, VB), F32)], flops=10 ** 9, moved=6 * 1...  4.11 us
    ppermute x4, waiting for transfers between devices, up(): return lax.ppermute(v, axis, [(i, (i + 1) % n) for i in range(n)])  2.71 us
    pallas_call x1, Pallas kernels, advance(): call(unpack_kernel, [((MAXB, LANES, VB), BF16), ((MAXB, 1, LANES), jnp.in...  2.21 us
    pallas_call x1, Pallas kernels, advance(): call(route_kernel, [((2, 512, 256), BF16), ((512, LANES), BF16), wide, ((...  2.12 us
  transfers between devices with their start and end apart: 8, of which 1 were waited for; matrix products, arithmetic and copies ran while one was open for 0% of the time, Pallas kernels for 11%

profile of v3, /device:TPU:1, one launch (start us, length us, event | category | flops | bytes accessed | tf_op | source)
XLA Modules:
  0.0 85.9 jit_solution(17772691270154048816)
XLA Ops:
  0.6 0.0 copy-start
  0.6 0.0 copy-start.2
  0.7 2.1 %shard_map.94 = (bf16[392,512]{1,0:T(8,128)(2,1)S(1)}, bf16[392,512]{1,0:T(8,128)(2,1)S(1)}, bf16[2,104,512]{2,1,0:T(8,128)(2,1)S(1)}, bf16[2,104,512]{2,1,0:T(8...) custom-call(bf16[1536,512]{1,0:T(8,128)(2,1)} %bitcast.15, ...), custom_call_target="tpu_custom_call" | custom-call | flops 100000000 | bytes 4000000 | tf_op jit(solution)/shard_map/pallas_call | solution.py:416
  2.8 2.6 %collective-permute-start.2 = (bf16[16,16,512]{2,1,0:T(8,128)(2,1)S(1)}, bf16[16,16,512]{2,1,0:T(8,128)(2,1)S(1)}, u32[]{:S(2)}, u32[]{:S(2)}) collective-permute-start(bf16[16,16,512]{2,1,0:T(8,128)(2,1)S(1)} %get-tuple-element.26), channel_id=1, source_target_pairs={{0,1},{1,2},{2,3},{3,4},{4,5},{5,6},{6,7},{7,0},{8,9},{9,10},{10,1... | collective-permute-start | bytes 786440 | tf_op jit(solution)/shard_map/ppermute | solution.py:398
  5.3 1.3 %collective-permute-start = (bf16[2,104,512]{2,1,0:T(8,128)(2,1)S(1)}, bf16[2,104,512]{2,1,0:T(8,128)(2,1)S(1)}, u32[]{:S(2)}, u32[]{:S(2)}) collective-permute-start(bf16[2,104,512]{2,1,0:T(8,128)(2,1)S(1)} %get-tuple-element.24), channel_id=1, source_target_pairs={{0,8},{8,16},{16,24},{24,0},{1,9},{9,17},{17,25},{25,1},{2,10},{10... | collective-permute-start | bytes 638984 | tf_op jit(solution)/shard_map/ppermute | solution.py:398
  6.6 1.4 %collective-permute-start.1 = (bf16[2,104,512]{2,1,0:T(8,128)(2,1)S(1)}, bf16[2,104,512]{2,1,0:T(8,128)(2,1)S(1)}, u32[]{:S(2)}, u32[]{:S(2)}) collective-permute-start(bf16[2,104,512]{2,1,0:T(8,128)(2,1)S(1)} %get-tuple-element.25), channel_id=1, source_target_pairs={{8,0},{16,8},{24,16},{0,24},{9,1},{17,9},{25,17},{1,25},{10,2},{18... | collective-permute-start | bytes 638984 | tf_op jit(solution)/shard_map/ppermute | solution.py:401
  8.1 1.6 %collective-permute-start.6 = (bf16[392,512]{1,0:T(8,128)(2,1)S(1)}, bf16[392,512]{1,0:T(8,128)(2,1)S(1)}, u32[]{:S(2)}, u32[]{:S(2)}) collective-permute-start(bf16[392,512]{1,0:T(8,128)(2,1)S(1)} %get-tuple-element.39), channel_id=1, source_target_pairs={{0,32},{32,64},{64,96},{96,128},{128,160},{160,192},{192,224},{224... | collective-permute-start | bytes 1204232 | tf_op jit(solution)/shard_map/ppermute | solution.py:398
  9.7 3.9 %collective-permute-start.7 = (bf16[392,512]{1,0:T(8,128)(2,1)S(1)}, bf16[392,512]{1,0:T(8,128)(2,1)S(1)}, u32[]{:S(2)}, u32[]{:S(2)}) collective-permute-start(bf16[392,512]{1,0:T(8,128)(2,1)S(1)} %get-tuple-element.40), channel_id=1, source_target_pairs={{32,0},{64,32},{96,64},{128,96},{160,128},{192,160},{224,192},{0,2... | collective-permute-start | bytes 1204232 | tf_op jit(solution)/shard_map/ppermute | solution.py:401
  13.7 0.0 collective-permute-done.ylo
  13.7 0.6 collective-permute-start.3
  14.3 0.0 copy-done
  14.3 0.5 shard_map.96
  14.8 0.0 collective-permute-done.1.yhi
  14.8 0.5 collective-permute-start.4
  15.3 0.0 collective-permute-done.2.zlo
  15.3 4.4 %collective-permute-start.5 = (bf16[392,512]{1,0:T(8,128)(2,1)S(1)}, bf16[392,512]{1,0:T(8,128)(2,1)S(1)}, u32[]{:S(2)}, u32[]{:S(2)}) collective-permute-start(bf16[392,512]{1,0:T(8,128)(2,1)S(1)} %get-tuple-element.31), channel_id=1, source_target_pairs={{32,0},{64,32},{96,64},{128,96},{160,128},{192,160},{224,192},{0,2... | collective-permute-start | bytes 1204232 | tf_op jit(solution)/shard_map/ppermute | solution.py:401
  19.8 2.1 %shard_map.97 = (bf16[2,512,256]{2,1,0:T(8,128)(2,1)S(1)}, bf16[512,128]{1,0:T(8,128)(2,1)S(1)}, f32[16,96,128]{2,1,0:T(8,128)S(1)}, f32[3,16,96,128]{3,2,1,0:T(...) custom-call(s32[128,12]{1,0:T(8,128)S(1)} %get-tuple-element.28.ids_ref, ...), custom_call_target="tpu_custom_call" | custom-call | flops 10000000 | bytes 1000000 | tf_op jit(solution)/shard_map/pallas_call | solution.py:439
  21.9 0.0 collective-permute-done.3.zhi
  21.9 0.0 copy-done.2
  21.9 0.0 copy-start.1
  21.9 4.1 %shard_map.95.acc_ref = f32[16,96,512]{2,1,0:T(8,128)S(1)} custom-call(bf16[16,96,512]{2,1,0:T(8,128)(2,1)S(1)} %bitcast.17, bf16[2,104,512]{2,1,0:T(8,128)(2,1)S(1)} %collective-permute-done.ylo, bf16[2,104,512]{2,1,0:T(8,128)(2,1)S(1)} %collective-permute-done.1.yhi, bf16[16,16,512]{2,1,0:T(8,128)(2,1)S(1)} %collective-permute-done.2.zlo, ...), custom_call_target="tpu_custom_call" | custom-call | flops 1000000000 | bytes 6000000 | tf_op jit(solution)/shard_map/pallas_call | solution.py:435
  26.1 0.0 collective-permute-done.6.lo_ref
  26.1 0.0 collective-permute-done.7.hi_ref
  26.1 0.0 copy-done.1
  26.1 2.8 %shard_map.98.prev_ref = bf16[16,392,128]{2,1,0:T(8,128)(2,1)S(1)} custom-call(f32[16,96,512]{2,1,0:T(8,128)S(1)} %shard_map.95.acc_ref, bf16[392,512]{1,0:T(8,128)(2,1)S(1)} %collective-permute-done.6.lo_ref, bf16[392,512]{1,0:T(8,128)(2,1)S(1)} %collective-permute-done.7.hi_ref, f32[16,96,128]{2,1,0:T(8,128)S(1)} %get-tuple-element.34.key_ref, ...), custom_call_target="tpu_custom_call" | custom-call | flops 1000000000 | bytes 4000000 | tf_op jit(solution)/shard_map/pallas_call | solution.py:447
  28.9 2.7 %collective-permute-done.4.lo_ref = bf16[392,512]{1,0:T(8,128)(2,1)S(1)} collective-permute-done((bf16[392,512]{1,0:T(8,128)(2,1)S(1)}, bf16[392,512]{1,0:T(8,128)(2,1)S(1)}, u32[]{:S(2)}, u32[]{:S(2)}) %collective-permute-start.4) | collective-permute-done | bytes 401440 | tf_op jit(solution)/shard_map/ppermute | solution.py:398
  31.6 0.0 collective-permute-done.5.hi_ref
  31.6 2.9 %shard_map.99 = bf16[16,392,128]{2,1,0:T(8,128)(2,1)S(1)} custom-call(f32[16,96,512]{2,1,0:T(8,128)S(1)} %shard_map.95.acc_ref, bf16[392,512]{1,0:T(8,128)(2,1)S(1)} %collective-permute-done.4.lo_ref, bf16[392,512]{1,0:T(8,128)(2,1)S(1)} %collective-permute-done.5.hi_ref, f32[16,96,128]{2,1,0:T(8,128)S(1)} %get-tuple-element.34.key_ref, ...), custom_call_target="tpu_custom_call" | custom-call | flops 1000000000 | bytes 4000000 | tf_op jit(solution)/shard_map/pallas_call | solution.py:447
  34.5 49.0 %all_to_all.5 = bf16[64,49,2,128]{3,2,1,0:T(2,128)(2,1)S(1)} all-to-all(bf16[64,49,2,128]{3,2,1,0:T(2,128)(2,1)S(1)} %bitcast.19), channel_id=1, replica_groups=mesh['gx'=8,'gy'=4,'gz'=8] {'gx','gz'}, dimensions={0} | all-to-all | bytes 3211264 | tf_op jit(solution)/shard_map/all_to_all | solution.py:460
  83.5 2.2 %shard_map.100 = (bf16[12,128,512]{2,1,0:T(8,128)(2,1)}, s32[12,1,128]{2,1,0:T(1,128)}, s32[1,128]{1,0:T(1,128)}) custom-call(bf16[16,392,128]{2,1,0:T(8,128)(2,1)S(1)} %bitcast.18), custom_call_target="tpu_custom_call" | custom-call | flops 400000000 | bytes 4000000 | tf_op jit(solution)/shard_map/pallas_call | solution.py:461
Async XLA Ops:
  0.6 13.7 %copy-start = (bf16[2,8,8,12,512]{4,2,3,1,0:T(8,128)(2,1)S(1)}, bf16[2,8,8,12,512]{4,2,3,1,0:T(8,128)(2,1)}, u32[]{:S(2)}) copy-start(bf16[2,8,8,12,512]{4,2,3,1,0:T(8,128)(2,1)} %param.7) | copy-start | bytes 4718596
  0.6 21.3 %copy-start.2 = (f32[8,512]{1,0:T(8,128)S(1)}, f32[8,512]{1,0:T(8,128)}, u32[]{:S(2)}) copy-start(f32[8,512]{1,0:T(8,128)} %constant.4.clone.vel_ref) | copy-start | bytes 49156
  2.8 12.6 %collective-permute-start.2 = (bf16[16,16,512]{2,1,0:T(8,128)(2,1)S(1)}, bf16[16,16,512]{2,1,0:T(8,128)(2,1)S(1)}, u32[]{:S(2)}, u32[]{:S(2)}) collective-permute-start(bf16[16,16,512]{2,1,0:T(8,128)(2,1)S(1)} %get-tuple-element.26), channel_id=1, source_target_pairs={{0,1},{1,2},{2,3},{3,4},{4,5},{5,6},{6,7},{7,0},{8,9},{9,10},{10,1... | collective-permute-start | bytes 786440 | tf_op jit(solution)/shard_map/ppermute | solution.py:398
  5.3 8.3 %collective-permute-start = (bf16[2,104,512]{2,1,0:T(8,128)(2,1)S(1)}, bf16[2,104,512]{2,1,0:T(8,128)(2,1)S(1)}, u32[]{:S(2)}, u32[]{:S(2)}) collective-permute-start(bf16[2,104,512]{2,1,0:T(8,128)(2,1)S(1)} %get-tuple-element.24), channel_id=1, source_target_pairs={{0,8},{8,16},{16,24},{24,0},{1,9},{9,17},{17,25},{25,1},{2,10},{10... | collective-permute-start | bytes 638984 | tf_op jit(solution)/shard_map/ppermute | solution.py:398
  6.6 8.2 %collective-permute-start.1 = (bf16[2,104,512]{2,1,0:T(8,128)(2,1)S(1)}, bf16[2,104,512]{2,1,0:T(8,128)(2,1)S(1)}, u32[]{:S(2)}, u32[]{:S(2)}) collective-permute-start(bf16[2,104,512]{2,1,0:T(8,128)(2,1)S(1)} %get-tuple-element.25), channel_id=1, source_target_pairs={{8,0},{16,8},{24,16},{0,24},{9,1},{17,9},{25,17},{1,25},{10,2},{18... | collective-permute-start | bytes 638984 | tf_op jit(solution)/shard_map/ppermute | solution.py:401
  8.1 18.0 %collective-permute-start.6 = (bf16[392,512]{1,0:T(8,128)(2,1)S(1)}, bf16[392,512]{1,0:T(8,128)(2,1)S(1)}, u32[]{:S(2)}, u32[]{:S(2)}) collective-permute-start(bf16[392,512]{1,0:T(8,128)(2,1)S(1)} %get-tuple-element.39), channel_id=1, source_target_pairs={{0,32},{32,64},{64,96},{96,128},{128,160},{160,192},{192,224},{224... | collective-permute-start | bytes 1204232 | tf_op jit(solution)/shard_map/ppermute | solution.py:398
  9.7 16.4 %collective-permute-start.7 = (bf16[392,512]{1,0:T(8,128)(2,1)S(1)}, bf16[392,512]{1,0:T(8,128)(2,1)S(1)}, u32[]{:S(2)}, u32[]{:S(2)}) collective-permute-start(bf16[392,512]{1,0:T(8,128)(2,1)S(1)} %get-tuple-element.40), channel_id=1, source_target_pairs={{32,0},{64,32},{96,64},{128,96},{160,128},{192,160},{224,192},{0,2... | collective-permute-start | bytes 1204232 | tf_op jit(solution)/shard_map/ppermute | solution.py:401
  13.7 8.2 %collective-permute-start.3 = (bf16[16,16,512]{2,1,0:T(8,128)(2,1)S(1)}, bf16[16,16,512]{2,1,0:T(8,128)(2,1)S(1)}, u32[]{:S(2)}, u32[]{:S(2)}) collective-permute-start(bf16[16,16,512]{2,1,0:T(8,128)(2,1)S(1)} %get-tuple-element.27), channel_id=1, source_target_pairs={{1,0},{2,1},{3,2},{4,3},{5,4},{6,5},{7,6},{0,7},{9,8},{10,9},{11,1... | collective-permute-start | bytes 786440 | tf_op jit(solution)/shard_map/ppermute | solution.py:401
  14.8 16.7 %collective-permute-start.4 = (bf16[392,512]{1,0:T(8,128)(2,1)S(1)}, bf16[392,512]{1,0:T(8,128)(2,1)S(1)}, u32[]{:S(2)}, u32[]{:S(2)}) collective-permute-start(bf16[392,512]{1,0:T(8,128)(2,1)S(1)} %get-tuple-element.30), channel_id=1, source_target_pairs={{0,32},{32,64},{64,96},{96,128},{128,160},{160,192},{192,224},{224... | collective-permute-start | bytes 1204232 | tf_op jit(solution)/shard_map/ppermute | solution.py:398
  15.3 16.2 %collective-permute-start.5 = (bf16[392,512]{1,0:T(8,128)(2,1)S(1)}, bf16[392,512]{1,0:T(8,128)(2,1)S(1)}, u32[]{:S(2)}, u32[]{:S(2)}) collective-permute-start(bf16[392,512]{1,0:T(8,128)(2,1)S(1)} %get-tuple-element.31), channel_id=1, source_target_pairs={{32,0},{64,32},{96,64},{128,96},{160,128},{192,160},{224,192},{0,2... | collective-permute-start | bytes 1204232 | tf_op jit(solution)/shard_map/ppermute | solution.py:401
  21.9 4.2 %copy-start.1 = (bf16[512,128]{1,0:T(8,128)(2,1)S(1)}, bf16[512,128]{1,0:T(8,128)(2,1)}, u32[]{:S(2)}) copy-start(bf16[512,128]{1,0:T(8,128)(2,1)} %constant.5.clone.wts_ref) | copy-start | bytes 393220

commit v4 on v3

--- a/solution.py
+++ b/solution.py
@@ -16,7 +16,7 @@
 EDGE = NV1 // BLK
 VB = BLK**3
 TILES = 16
-HALF = 4
+PARTS = ((0, 6), (6, 2))
 ROWS = MAXB * 8
 LANES = 128
 STEP_COEFF = 0.6
@@ -55,45 +55,46 @@
 
 
 def x_copies(part, d_ref, outs, sems):
+    first, count = PARTS[part]
     copies = []
     for k, out in enumerate(outs):
-        source = d_ref.at[pl.ds((8 * k + HALF * part) * ROWS, HALF * ROWS)]
-        copies.append(pltpu.make_async_copy(source, out.at[pl.ds(0, HALF * ROWS)], sems.at[k]))
+        source = d_ref.at[pl.ds((8 * k + first) * ROWS, count * ROWS)]
+        copies.append(pltpu.make_async_copy(source, out.at[pl.ds(0, count * ROWS)], sems.at[k]))
     return copies
 
 
 def put_keys(listed, outs):
+    start = PARTS[0][1] * ROWS
     for k, out in enumerate(outs):
-        out[HALF * ROWS :, :LANES] = listed[8 * k : 8 * k + 8].astype(BF16)
-        out[HALF * ROWS :, LANES:] = jnp.zeros((8, VB - LANES), BF16)
-
-
-def face_kernel(d_ref, ids_ref, cnt_ref, lo, hi, sems):
+        out[start:, :LANES] = listed[8 * k : 8 * k + 8].astype(BF16)
+        out[start:, LANES:] = jnp.zeros((8, VB - LANES), BF16)
+
+
+def face_kernel(d_ref, lo, hi, sems):
     copies = x_copies(1, d_ref, (lo, hi), sems)
     for copy in copies:
         copy.start()
+    for copy in copies:
+        copy.wait()
+
+
+def front_kernel(d_hbm, ids_hbm, cnt_hbm, own_hbm, rest_hbm, lo, hi, ids_ref, cnt_ref, own_ref, rest_ref, sems):
+    pairs = ((ids_hbm, ids_ref), (cnt_hbm, cnt_ref), (own_hbm, own_ref), (rest_hbm, rest_ref))
+    small = [pltpu.make_async_copy(a, b, sems.at[2 + n]) for n, (a, b) in enumerate(pairs)]
+    large = x_copies(0, d_hbm, (lo, hi), sems)
+    for copy in small + large:
+        copy.start()
+    for copy in small[:2]:
+        copy.wait()
     ids, live = listed_rows(ids_ref, cnt_ref)
     put_keys(jnp.where(live, ids, -1.0), (lo, hi))
-    for copy in copies:
+    for copy in large + small[2:]:
         copy.wait()
 
 
-def front_kernel(
-    d_hbm, ids_hbm, cnt_hbm, own_hbm, rest_hbm, lo, hi, ylo, yhi, zlo, zhi, ids_ref, cnt_ref, own_ref, rest_ref, d_ref, sems
-):
-    small = [pltpu.make_async_copy(ids_hbm, ids_ref, sems.at[2]), pltpu.make_async_copy(cnt_hbm, cnt_ref, sems.at[3])]
-    later = [pltpu.make_async_copy(own_hbm, own_ref, sems.at[8]), pltpu.make_async_copy(rest_hbm, rest_ref, sems.at[9])]
-    large = x_copies(0, d_hbm, (lo, hi), sems)
-    quarter = TILES // 4 * ROWS
-    parts = [pl.ds(q * quarter, quarter) for q in range(4)]
-    whole = [pltpu.make_async_copy(d_hbm.at[p], d_ref.at[p], sems.at[4 + q]) for q, p in enumerate(parts)]
-    for copy in small + whole + large + later:
-        copy.start()
-    for copy in small:
-        copy.wait()
+def side_kernel(d_ref, ids_ref, cnt_ref, ylo, yhi, zlo, zhi):
     ids, live = listed_rows(ids_ref, cnt_ref)
     listed = jnp.where(live, ids, -1.0)
-    put_keys(listed, (lo, hi))
     lane = iota((TILES, LANES), 1)
     keys = []
     for z, first in ((0, 112), (7, 96)):
@@ -107,9 +108,7 @@
     select = ((iota((32, ROWS), 1) == wanted) & valid).astype(BF16)
     key_row = iota((16, LANES), 0) == MAXB
     for i in range(TILES):
-        if i % 4 == 0:
-            whole[i // 4].wait()
-        tile = d_ref[i * ROWS : i * ROWS + ROWS, :]
+        tile = d_ref[i]
         if i % 8 in (0, 7):
             out = yhi if i % 8 else ylo
             out[i // 8, :ROWS, :] = tile
@@ -121,11 +120,9 @@
             first = jnp.where(key_row, jnp.broadcast_to(key[i : i + 1], (16, LANES)), face[:, :LANES])
             out[i, :, :LANES] = first.astype(BF16)
             out[i, :, LANES:] = face[:, LANES:].astype(BF16)
-    for copy in large + later:
-        copy.wait()
-
-
-def local_kernel(d_ref, ylo, yhi, zlo, zhi, ids_ref, cnt_ref, vel_ref, acc_ref):
+
+
+def local_kernel(d_ref, ylo, yhi, zlo, zhi, ids_ref, cnt_ref, cen_ref, vel_ref, acc_ref):
     ids, live = listed_rows(ids_ref, cnt_ref)
     lane = iota((TILES, LANES), 1)
     tile = iota((TILES, LANES), 0)
@@ -147,10 +144,7 @@
             jnp.where(live & (by >= half), key, none),
             jnp.where(live & (by < half), key, none),
             jnp.where(live, kz, none),
-            centre(bx),
-            centre(by),
-            centre(bz),
-            live.astype(F32),
+            jnp.zeros((4 * TILES, LANES), F32),
         ],
         axis=0,
     )
@@ -170,7 +164,6 @@
     for i in range(TILES):
         x, y = divmod(i, 8)
         own = d_ref[i]
-        f = own.astype(F32)
         other = (1 - x) * 8 + y
         gx = jnp.dot(match(column(0, i), near[other : other + 1, :ROWS]), d_ref[other], preferred_element_type=F32)
         low, low_key = (ylo[x, :ROWS, :], halo_key(ylo, x)) if y == 0 else (d_ref[i - 1], near[i - 1 : i])
@@ -182,14 +175,21 @@
         zkey = jnp.where(one_lane < ROWS, near[i : i + 1], edge)
         around = jnp.concatenate([own, zlo[i], zhi[i]], axis=0)
         gz = jnp.dot(match(column(3, i), zkey), around, preferred_element_type=F32)
-        acc = f
-        for d, g in enumerate((gx, gy, gz)):
-            speed = jnp.abs(LAM * column(4 + d, i) + vel_ref[3 + d : 4 + d])
-            acc = acc + speed * (g - f)
-        acc_ref[i] = acc * column(7, i)
-
-
-def route_kernel(ids_ref, cnt_ref, own_ref, rest_ref, sel_ref, meta_ref, key_ref, cen_ref, fac_ref, widen_ref):
+        c = [cen_ref[k, i] for k in range(3)]
+        speed = [jnp.abs(LAM * c[k] + vel_ref[3 + k : 4 + k, :LANES]) for k in range(3)]
+        step = jnp.where(c[0] > 0.0, 2.0 * LAM, -2.0 * LAM)
+        real = c[1] < FAR / 2
+        for t in range(4):
+            at = slice(LANES * t, LANES * t + LANES)
+            f = own[:, at].astype(F32)
+            acc = f
+            for k, g in enumerate((gx, gy, gz)):
+                acc = acc + speed[k] * (g[:, at] - f)
+            acc_ref[i, :, at] = jnp.where(real, acc, 0.0)
+            speed[0] = speed[0] + step
+
+
+def route_kernel(ids_ref, cnt_ref, own_ref, rest_ref, sel0, sel1, meta_ref, key_ref, cen_ref, fac_ref, widen_ref):
     lane = iota((TILES, LANES), 1)
     here = lane // 8 == iota((TILES, LANES), 0)
     flat = lambda v: jnp.sum(jnp.where(here, spread(v), 0.0), axis=0, keepdims=True)
@@ -199,12 +199,12 @@
     earlier = (cols[:, :1] == owner) & (sub < iota((LANES, LANES), 1))
     rank = jnp.sum(earlier.astype(F32), axis=0, keepdims=True)
     home = owner * 8.0 + rank
-    for part in range(2):
-        mine = jnp.concatenate([home[:, 64 * x + 32 * part : 64 * x + 32 * part + 32] for x in range(2)], axis=1)
+    for (first, count), out in zip(PARTS, (sel0, sel1)):
+        mine = jnp.concatenate([home[:, 64 * x + 8 * first : 64 * x + 8 * (first + count)] for x in range(2)], axis=1)
         mine = mine.astype(jnp.int32)
         shifts = [(mine % 8 + mine // 8 * 2 + 2 * s) % 8 for s in range(4)]
         target = jnp.concatenate([mine // 8 * 8 + shift for shift in shifts], axis=1).astype(F32)
-        sel_ref[part] = (iota((512, 256), 0).astype(F32) == target).astype(F32).astype(BF16)
+        out[...] = (iota((512, 64 * count), 0).astype(F32) == target).astype(F32).astype(BF16)
     phase = 2 * (owner.astype(jnp.int32) % 4)
     place = (iota((512, LANES), 0).astype(F32) == home + phase.astype(F32)).astype(F32)
     wide = mm(ids_ref[...].astype(F32), (iota((MAXB, LANES), 0) == iota((MAXB, LANES), 1)).astype(F32))
@@ -246,76 +246,83 @@
 
 
 def final_kernel(
-    part, acc_ref, lo_ref, hi_ref, key_ref, cen_ref, fac_ref, widen_ref, vel_ref, wts_ref, sel_ref, prev_ref, out_ref,
-    read, rows, total_ref, cell_ref,
+    part, acc_ref, lo_key, hi_key, lo_ref, hi_ref, key_ref, cen_ref, fac_ref, widen_ref, vel_ref, wts_ref, sel_ref, prev_ref, out_ref,
+    read, rows, cell_ref,
 ):
     zrow = (iota((8, LANES), 1) % 8).astype(F32)
     tiles4 = [slice(LANES * t, LANES * t + LANES) for t in range(4)]
-    places = [(x, y, x * 8 + HALF * part + y, x * HALF + y) for y in range(HALF) for x in range(2)]
-    slots = lambda v: v.reshape(MAXB, 8, LANES)
+    start, count = PARTS[part]
+    slots = lambda v: v.reshape(-1, 8, LANES)
+    cells = count * 8
     near = []
-    for ref in (lo_ref, hi_ref):
-        got = ref[HALF * ROWS :, :LANES].astype(F32)
+    for ref in (lo_key, hi_key):
+        got = ref[PARTS[0][1] * ROWS :, :LANES].astype(F32)
         near.append(jnp.where(got < 0.0, -2.0, got * 8.0 + zrow))
 
-    for x, y, i, k in places:
-        halo = (lo_ref, hi_ref)[x][y * ROWS : y * ROWS + ROWS, :]
-        row = near[x][HALF * part + y : HALF * part + y + 1]
-        pick_rows = (key_ref[i][:, :ROWS] == row[:, :ROWS]).astype(F32).astype(BF16)
-        g = jnp.dot(pick_rows, halo, preferred_element_type=F32)
-        cx = cen_ref[0, i]
-        speed = jnp.abs(LAM * cx + vel_ref[3:4, :LANES])
-        step = jnp.where(cx > 0.0, 2.0 * LAM, -2.0 * LAM)
-        parts = []
-        for at in tiles4:
-            parts.append((acc_ref[i, :, at] + speed * g[:, at]).astype(BF16))
-            speed = speed + step
-        now = jnp.concatenate(parts, axis=1)
-        read[k] = now
-        sums = jnp.dot(now, wts_ref[...], preferred_element_type=F32)
-        total_ref[k] = jnp.sum(slots(sums * fac_ref[i]), axis=0)
-
-    cells = 2 * HALF * 8
-    total = total_ref[...].reshape(cells, LANES)
-    at = lambda k: total[:, k : k + 1]
-    mass = at(0)
-    per = 1.0 / mass
-    u = [(at(1 + d) + at(4 + d)) * per for d in range(3)]
-    energy = at(7) + at(8) + at(9) + at(10) + at(11)
-    warm = (energy * per - (u[0] * u[0] + u[1] * u[1] + u[2] * u[2])) / 3.0
-    widen = jnp.concatenate([widen_ref[x * 8 + HALF * part : x * 8 + HALF * part + HALF] for x in range(2)], axis=0)
-    aim = warm * widen.reshape(cells, LANES)[:, :1]
-    rate = 1.0 - jnp.exp(-IMPACT_KIND * (mass / VB) * jnp.sqrt(warm))
-    area = 2.0 * math.pi * aim
-    scale = rate * mass / (area * jnp.sqrt(area))
-    sharp = 0.5 * math.log2(math.e) / aim
-    for k, v in enumerate((u[0], u[1], u[2], -sharp, jnp.sqrt(sharp), scale, 1.0 - rate)):
-        cell_ref[k] = jnp.broadcast_to(v, (cells, LANES)).reshape(2 * HALF, 8, LANES)
-
-    for x, y, i, k in places:
+    for x in range(2):
+        mine = slice(x * count, x * count + count)
+        for y in range(count):
+            i, k = x * 8 + start + y, x * count + y
+            halo = (lo_ref, hi_ref)[x][y * ROWS : y * ROWS + ROWS, :]
+            row = near[x][start + y : start + y + 1]
+            pick_rows = (key_ref[i][:, :ROWS] == row[:, :ROWS]).astype(F32).astype(BF16)
+            g = jnp.dot(pick_rows, halo, preferred_element_type=F32)
+            cx = cen_ref[0, i]
+            speed = jnp.abs(LAM * cx + vel_ref[3:4, :LANES])
+            step = jnp.where(cx > 0.0, 2.0 * LAM, -2.0 * LAM)
+            parts = []
+            for at in tiles4:
+                parts.append((acc_ref[i, :, at] + speed * g[:, at]).astype(BF16))
+                speed = speed + step
+            read[k] = jnp.concatenate(parts, axis=1)
+        sums = jnp.dot(read[mine].reshape(count * ROWS, VB), wts_ref[...], preferred_element_type=F32)
+        total = []
+        for y in range(count):
+            total.append(jnp.sum(slots(sums[y * ROWS : y * ROWS + ROWS] * fac_ref[x * 8 + start + y]), axis=0))
+        total = jnp.concatenate(total, axis=0)
+        at = lambda k: total[:, k : k + 1]
+        mass = at(0)
+        per = 1.0 / mass
+        u = [(at(1 + d) + at(4 + d)) * per for d in range(3)]
+        energy = at(7) + at(8) + at(9) + at(10) + at(11)
+        warm = (energy * per - (u[0] * u[0] + u[1] * u[1] + u[2] * u[2])) / 3.0
+        widen = widen_ref[x * 8 + start : x * 8 + start + count]
+        aim = warm * widen.reshape(cells, LANES)[:, :1]
+        rate = 1.0 - jnp.exp(-IMPACT_KIND * (mass / VB) * jnp.sqrt(warm))
+        area = 2.0 * math.pi * aim
+        scale = rate * mass / (area * jnp.sqrt(area))
+        sharp = 0.5 * math.log2(math.e) / aim
+        for k, v in enumerate((u[0], u[1], u[2], -sharp, jnp.sqrt(sharp), scale, 1.0 - rate)):
+            cell_ref[k, mine] = jnp.broadcast_to(v, (cells, LANES)).reshape(count, 8, LANES)
+
+    def collide(t, x, y):
+        i, k = x * 8 + start + y, x * count + y
+        some = slice(32 * t, 32 * t + 32)
         ux, uy, uz, fall, root, scale, keep = (cell_ref[q, k][None] for q in range(7))
-        off_y = slots(cen_ref[1, i]) - uy + vel_ref[1:2, :LANES][None]
-        off_z = slots(cen_ref[2, i]) - uz + vel_ref[2:3, :LANES][None]
+        off_y = slots(cen_ref[1, i, some]) - uy + vel_ref[1:2, :LANES][None]
+        off_z = slots(cen_ref[2, i, some]) - uz + vel_ref[2:3, :LANES][None]
         side = (off_y * off_y + off_z * off_z) * fall
-        off_x = (slots(cen_ref[0, i]) - ux + vel_ref[:1, :LANES][None]) * root
+        off_x = (slots(cen_ref[0, i, some]) - ux + vel_ref[:1, :LANES][None]) * root
         step = root + root
         for at in tiles4:
-            now = slots(read[k, :, at].astype(F32))
+            now = slots(read[k, some, at].astype(F32))
             after = now * keep + scale * jnp.exp2(side - off_x * off_x)
-            rows[:, k * 8 : k * 8 + 8, at] = after.astype(BF16)
+            rows[4 * t : 4 * t + 4, k * 8 : k * 8 + 8, at] = after.astype(BF16)
             off_x = off_x + step
 
     def put(tile, value):
         where = slice(8 * tile, 8 * tile + 8)
-        if part:
-            value = value + prev_ref[:, where, :].astype(F32)
-        out_ref[:, where, :] = value.astype(BF16)
+        value = value.astype(BF16)
+        out_ref[:, where, :] = value + prev_ref[:, where, :] if part else value
 
     sub = iota((16, 8, LANES), 1)
     info = jnp.zeros((16, 4, 8, LANES), F32) if part else prev_ref[...].astype(F32).reshape(16, 4, 8, LANES)
     before = [None] + [info[:, p - 1] for p in range(1, 4)]
     for t in range(3):
-        out = jnp.dot(sel_ref[part], rows[4 * t : 4 * t + 4].reshape(256, VB), preferred_element_type=F32)
+        for x in range(2):
+            for y in range(count):
+                collide(t, x, y)
+        out = jnp.dot(sel_ref[...], rows[4 * t : 4 * t + 4].reshape(64 * count, VB), preferred_element_type=F32)
         out = out.reshape(16, 4, 8, VB)
         for k, at in enumerate(tiles4):
             for p in range(4):
@@ -325,18 +332,16 @@
     put(48, jnp.where(sub >= 6, info[:, 3], before[3]))
     for p in (1, 2):
         where = slice(96 * (p + 1), 96 * (p + 1) + 8)
-        value = out_ref[:, where, :].astype(F32) + jnp.where(sub < 2 * p, before[p], 0.0)
-        out_ref[:, where, :] = value.astype(BF16)
+        out_ref[:, where, :] = out_ref[:, where, :] + jnp.where(sub < 2 * p, before[p], 0.0).astype(BF16)
 
 
 def unpack_kernel(got_ref, out_ref, ids_ref, cnt_ref, rows, sems):
-    row, col = iota((256, 256), 0), iota((256, 256), 1)
-    slot, source, rank = row // 64, row % 64 // 2, row % 2
-    phase = source % 4
-    perm = (col == phase * 64 + source // 4 * 8 + (2 * slot + rank + 2 * phase) % 8).astype(F32).astype(BF16)
+    col = iota((1, 256), 1)
+    phase, shifted = col // 64, (col % 8 - 2 * (col // 64) + 8) % 8
+    source = col % 64 // 8 * 4 + phase
+    perm = (iota((256, 256), 0) == shifted // 2 * 64 + source * 2 + shifted % 2).astype(F32).astype(BF16)
     sub = iota((1, 8, LANES), 1)
-    upper = [None] + [(sub >= 2 * p).astype(F32).astype(BF16) for p in range(1, 4)]
-    lower = [None] + [(sub < 2 * p).astype(F32).astype(BF16) for p in range(1, 4)]
+    upper = [None] + [jnp.broadcast_to((sub >= 2 * p).astype(F32).astype(BF16), (8, 8, LANES)) > 0 for p in range(1, 4)]
     copies = []
     for t in range(3):
         for g in range(2):
@@ -346,17 +351,17 @@
                 parts = [tile(4 * t + k).reshape(64, LANES)]
                 for p in range(1, 4):
                     n = 12 * p + 4 * t + k
-                    parts.append((tile(n) * upper[p] + tile(n + 1) * lower[p]).reshape(64, LANES))
+                    parts.append(jnp.where(upper[p], tile(n), tile(n + 1)).reshape(64, LANES))
                 lanes.append(jnp.concatenate(parts, axis=0))
             out = jnp.dot(perm, jnp.concatenate(lanes, axis=1), preferred_element_type=F32)
             where = (pl.ds(4 * t, 4), pl.ds(64 * g, 64))
             rows[where] = out.reshape(4, 64, VB).astype(BF16)
             copies.append(pltpu.make_async_copy(rows.at[where], out_ref.at[where], sems.at[2 * t + g]))
             copies[-1].start()
-    place = iota((LANES, 512), 0)
-    source, rank = place // 2, place % 2
-    phase = source % 4
-    pick = (iota((LANES, 512), 1) == phase * 128 + source // 4 * 8 + 2 * phase + rank).astype(F32).astype(BF16)
+    col = iota((1, 512), 1)
+    phase, at = col // 128, col % 8
+    target = jnp.where(at // 2 == phase, (col % 128 // 8 * 4 + phase) * 2 + at % 2, -1)
+    pick = (iota((LANES, 512), 0) == target).astype(F32).astype(BF16)
     meta = jnp.concatenate([got_ref[:, 96 * p : 96 * p + 8, :].reshape(128, LANES) for p in range(1, 5)], axis=0)
     info = jnp.dot(pick, meta, preferred_element_type=F32).T.astype(jnp.int32)
     ids_ref[...] = info[:MAXB].reshape(MAXB, 1, LANES)
@@ -408,54 +413,54 @@
     vel, weights = tables()
     vel, weights = jnp.asarray(vel), jnp.asarray(weights, BF16)
 
-    face_x = ((HALF * ROWS + 8, VB), BF16)
+    face_x = [((PARTS[0][1] * ROWS + 8, VB), BF16), ((PARTS[1][1] * ROWS, VB), BF16)]
     face_y, face_z = ((2, ROWS + 8, VB), BF16), ((TILES, 16, VB), BF16)
     flat = d.reshape(TILES * ROWS, VB)
     hbm, whole = pl.BlockSpec(memory_space=pltpu.HBM), pl.BlockSpec(memory_space=pltpu.VMEM)
     small = [((TILES * 8, MAXB), jnp.int32), ((TILES, 8), jnp.int32), ((TILES, 8), jnp.int32), ((TILES, 8), BF16)]
-    xlo, xhi, ylo, yhi, zlo, zhi, ids, cnt, own, rest = call(
+    xlo, xhi, ids, cnt, own, rest = call(
         front_kernel,
-        [face_x, face_x, face_y, face_y, face_z, face_z] + small,
-        scratch=[pltpu.VMEM((TILES * ROWS, VB), BF16), pltpu.SemaphoreType.DMA((10,))],
-        flops=10**8,
-        moved=4 * 10**6,
+        [face_x[0]] * 2 + small,
+        scratch=[pltpu.SemaphoreType.DMA((6,))],
+        moved=2 * 10**6,
         in_specs=[hbm] * 5,
     )(*(pltpu.with_memory_space_constraint(v, pltpu.HBM) for v in (flat, ids, cnt, own, rest)))
     near_x = [(up(xhi, "gx", nx), down(xlo, "gx", nx))]
+    ylo, yhi, zlo, zhi = call(side_kernel, [face_y, face_y, face_z, face_z], flops=10**8, moved=4 * 10**6)(d, ids, cnt)
     xlo, xhi = call(
         face_kernel,
-        [face_x, face_x],
+        [face_x[1]] * 2,
         scratch=[pltpu.SemaphoreType.DMA((2,))],
         moved=2 * 10**6,
-        in_specs=[pl.BlockSpec(memory_space=pl.ANY), whole, whole],
-    )(flat, ids, cnt)
+        in_specs=[pl.BlockSpec(memory_space=pl.ANY)],
+    )(flat)
     near_x.append((up(xhi, "gx", nx), down(xlo, "gx", nx)))
     y_hi, y_lo = down(ylo, "gy", ny), up(yhi, "gy", ny)
     z_hi, z_lo = down(zlo, "gz", nz), up(zhi, "gz", nz)
-    (acc,) = call(local_kernel, [((TILES, ROWS, VB), F32)], flops=10**9, moved=6 * 10**6)(
-        d, y_lo, y_hi, z_lo, z_hi, ids, cnt, vel
-    )
     wide = ((TILES, ROWS, LANES), F32)
-    sel, meta, keys, centres, factors, widen = call(
+    *sel, meta, keys, centres, factors, widen = call(
         route_kernel,
-        [((2, 512, 256), BF16), ((512, LANES), BF16), wide, ((3, TILES, ROWS, LANES), F32), wide, ((TILES, 8, LANES), F32)],
+        [((512, 64 * count), BF16) for _, count in PARTS]
+        + [((512, LANES), BF16), wide, ((3, TILES, ROWS, LANES), F32), wide, ((TILES, 8, LANES), F32)],
         flops=10**7,
         moved=10**6,
     )(ids, cnt, own, rest)
+    (acc,) = call(local_kernel, [((TILES, ROWS, VB), F32)], flops=10**9, moved=6 * 10**6)(
+        d, y_lo, y_hi, z_lo, z_hi, ids, cnt, centres, vel
+    )
     out = meta
-    for part in range(2):
+    for part, (_, count) in enumerate(PARTS):
         (out,) = call(
             functools.partial(final_kernel, part),
             [((16, 392, LANES), BF16)],
             scratch=[
-                pltpu.VMEM((2 * HALF, ROWS, VB), BF16),
-                pltpu.VMEM((MAXB, 2 * HALF * 8, VB), BF16),
-                pltpu.VMEM((2 * HALF, 8, LANES), F32),
-                pltpu.VMEM((7, 2 * HALF, 8, LANES), F32),
+                pltpu.VMEM((2 * count, ROWS, VB), BF16),
+                pltpu.VMEM((MAXB, 2 * count * 8, VB), BF16),
+                pltpu.VMEM((7, 2 * count, 8, LANES), F32),
             ],
             flops=10**9,
             moved=4 * 10**6,
-        )(acc, *near_x[part], keys, centres, factors, widen, vel, weights, sel, out)
+        )(acc, *near_x[0], *near_x[part], keys, centres, factors, widen, vel, weights, sel[part], out)
     out = out.reshape(64, 49, 2, LANES)
     got = lax.all_to_all(out, ("gx", "gz"), split_axis=0, concat_axis=0, tiled=True).reshape(16, 392, LANES)
     moved, moved_ids, moved_counts = call(

time: 86 us -> 87.6 us (1.019)
  waiting for transfers between devices: 2.72 us -> 6.74 us
  Pallas kernels: 16.7 us -> 14.3 us
  starting transfers between devices: 16.5 us -> 14.3 us
  blocking collectives: 49 us -> 51.1 us
    ppermute x4, waiting for transfers between devices: 0.01 us -> 3.17 us  [down(): return lax.ppermute(v, axis, [((i + 1) % n, i) for i in range(n)])]
    ppermute x4, starting transfers between devices: 10.4 us -> 8.11 us  [down(): return lax.ppermute(v, axis, [((i + 1) % n, i) for i in range(n)])]
    all_to_all x1, blocking collectives: 49 us -> 51.1 us  [advance(): lax.all_to_all(out, ('gx', 'gz'), split_axis=0, concat_axis=0, tiled=True)]
    pallas_call x1, Pallas kernels: 4.11 us -> 3.04 us  [advance(): call(local_kernel, [((TILES, ROWS, VB), F32)], flops=10 ** 9, moved=6 * 1...]
    pallas_call x2, Pallas kernels: 5.66 us -> 4.62 us  [advance(): call(functools.partial(final_kernel, part), [((16, 392, LANES), BF16)], s...]
    pallas_call x3 -> x4, Pallas kernels: 4.74 us -> 4.64 us  [the longest x1 2.18 us: advance(): call(route_kernel, [((512, 64 * count), BF16) for _, count in PARTS] + [(...]
  transfers between devices with their start and end apart: 8 -> 8, of which waited for: 1 -> 2; matrix products, arithmetic and copies ran while one was open for 0% -> 0% of each run, Pallas kernels for 11% -> 11%
where the time goes in v4:
time: 87.6 us; the launch traced here: 87.5 us
  blocking collectives  51.1 us (58%)
  Pallas kernels  14.3 us (16%)
  starting transfers between devices  14.3 us (16%)
  waiting for transfers between devices  6.74 us (8%)
  between operations  0.92 us (1%)
    all_to_all x1, blocking collectives, advance(): lax.all_to_all(out, ('gx', 'gz'), split_axis=0, concat_axis=0, tiled=True)  51.1 us
    ppermute x4, starting transfers between devices, down(): return lax.ppermute(v, axis, [((i + 1) % n, i) for i in range(n)])  8.11 us
    ppermute x4, starting transfers between devices, up(): return lax.ppermute(v, axis, [(i, (i + 1) % n) for i in range(n)])  6.24 us
    pallas_call x2, Pallas kernels, advance(): call(functools.partial(final_kernel, part), [((16, 392, LANES), BF16)], s...  4.62 us
    ppermute x4, waiting for transfers between devices, up(): return lax.ppermute(v, axis, [(i, (i + 1) % n) for i in range(n)])  3.57 us
    ppermute x4, waiting for transfers between devices, down(): return lax.ppermute(v, axis, [((i + 1) % n, i) for i in range(n)])  3.17 us
    pallas_call x1, Pallas kernels, advance(): call(local_kernel, [((TILES, ROWS, VB), F32)], flops=10 ** 9, moved=6 * 1...  3.04 us
    pallas_call x1, Pallas kernels, advance(): call(route_kernel, [((512, 64 * count), BF16) for _, count in PARTS] + [(...  2.18 us
  transfers between devices with their start and end apart: 8, of which 2 were waited for; matrix products, arithmetic and copies ran while one was open for 0% of the time, Pallas kernels for 11%

profile of v4, /device:TPU:1, one launch (start us, length us, event | category | flops | bytes accessed | tf_op | source)
XLA Modules:
  0.0 87.5 jit_solution(6130501912146928858)
XLA Ops:
  0.6 0.0 copy-start
  0.6 1.5 %shard_map.94 = (bf16[584,512]{1,0:T(8,128)(2,1)S(1)}, bf16[584,512]{1,0:T(8,128)(2,1)S(1)}, s32[128,12]{1,0:T(8,128)S(1)}, s32[16,8]{1,0:T(8,128)S(1)}, s32[16,8]{1,0:T(8,128)S(1)}, /*index=5*/bf16[16,8]{1,0:T(8,128)(2,1)S(1)}) custom-call(bf16[1536,512]{1,0:T(8,128)(2,1)} %bitcast.15, s32[128,12]{1,0:T(8,128)} %bitcast.21, s32[16,8]{1,0:T(8,128)} %bitcast.22, ...), custom_call_target="tpu_custom_call" | custom-call | bytes 2000000 | tf_op jit(solution)/shard_map/pallas_call | solution.py:421
  2.1 2.5 %collective-permute-start.4 = (bf16[584,512]{1,0:T(8,128)(2,1)S(1)}, bf16[584,512]{1,0:T(8,128)(2,1)S(1)}, u32[]{:S(2)}, u32[]{:S(2)}) collective-permute-start(bf16[584,512]{1,0:T(8,128)(2,1)S(1)} %get-tuple-element.34), channel_id=1, source_target_pairs={{0,32},{32,64},{64,96},{96,128},{128,160},{160,192},{192,224},{224... | collective-permute-start | bytes 1794056 | tf_op jit(solution)/shard_map/ppermute | solution.py:403
  4.7 4.0 %collective-permute-start.5 = (bf16[584,512]{1,0:T(8,128)(2,1)S(1)}, bf16[584,512]{1,0:T(8,128)(2,1)S(1)}, u32[]{:S(2)}, u32[]{:S(2)}) collective-permute-start(bf16[584,512]{1,0:T(8,128)(2,1)S(1)} %get-tuple-element.35), channel_id=1, source_target_pairs={{32,0},{64,32},{96,64},{128,96},{160,128},{192,160},{224,192},{0,2... | collective-permute-start | bytes 1794056 | tf_op jit(solution)/shard_map/ppermute | solution.py:406
  8.7 0.0 copy-done
  8.7 0.0 copy-start.2
  8.7 0.5 shard_map.95
  9.2 1.4 %collective-permute-start = (bf16[2,104,512]{2,1,0:T(8,128)(2,1)S(1)}, bf16[2,104,512]{2,1,0:T(8,128)(2,1)S(1)}, u32[]{:S(2)}, u32[]{:S(2)}) collective-permute-start(bf16[2,104,512]{2,1,0:T(8,128)(2,1)S(1)} %get-tuple-element.27), channel_id=1, source_target_pairs={{0,8},{8,16},{16,24},{24,0},{1,9},{9,17},{17,25},{25,1},{2,10},{10... | collective-permute-start | bytes 638984 | tf_op jit(solution)/shard_map/ppermute | solution.py:403
  10.6 2.3 %collective-permute-start.2 = (bf16[16,16,512]{2,1,0:T(8,128)(2,1)S(1)}, bf16[16,16,512]{2,1,0:T(8,128)(2,1)S(1)}, u32[]{:S(2)}, u32[]{:S(2)}) collective-permute-start(bf16[16,16,512]{2,1,0:T(8,128)(2,1)S(1)} %get-tuple-element.29), channel_id=1, source_target_pairs={{0,1},{1,2},{2,3},{3,4},{4,5},{5,6},{6,7},{7,0},{8,9},{9,10},{10,1... | collective-permute-start | bytes 786440 | tf_op jit(solution)/shard_map/ppermute | solution.py:403
  12.9 0.0 collective-permute-start.3
  12.9 3.6 %collective-permute-done.ylo = bf16[2,104,512]{2,1,0:T(8,128)(2,1)S(1)} collective-permute-done((bf16[2,104,512]{2,1,0:T(8,128)(2,1)S(1)}, bf16[2,104,512]{2,1,0:T(8,128)(2,1)S(1)}, u32[]{:S(2)}, u32[]{:S(2)}) %collective-permute-start) | collective-permute-done | bytes 213024 | tf_op jit(solution)/shard_map/ppermute | solution.py:403
  16.5 1.4 %collective-permute-start.1 = (bf16[2,104,512]{2,1,0:T(8,128)(2,1)S(1)}, bf16[2,104,512]{2,1,0:T(8,128)(2,1)S(1)}, u32[]{:S(2)}, u32[]{:S(2)}) collective-permute-start(bf16[2,104,512]{2,1,0:T(8,128)(2,1)S(1)} %get-tuple-element.28), channel_id=1, source_target_pairs={{8,0},{16,8},{24,16},{0,24},{9,1},{17,9},{25,17},{1,25},{10,2},{18... | collective-permute-start | bytes 638984 | tf_op jit(solution)/shard_map/ppermute | solution.py:406
  17.9 0.5 shard_map.98
  18.4 3.2 %collective-permute-done.1.yhi = bf16[2,104,512]{2,1,0:T(8,128)(2,1)S(1)} collective-permute-done((bf16[2,104,512]{2,1,0:T(8,128)(2,1)S(1)}, bf16[2,104,512]{2,1,0:T(8,128)(2,1)S(1)}, u32[]{:S(2)}, u32[]{:S(2)}) %collective-permute-start.1) | collective-permute-done | bytes 213024 | tf_op jit(solution)/shard_map/ppermute | solution.py:406
  21.5 0.0 collective-permute-start.6
  21.5 0.0 collective-permute-done.2.zlo
  21.5 2.7 %collective-permute-start.7 = (bf16[192,512]{1,0:T(8,128)(2,1)S(1)}, bf16[192,512]{1,0:T(8,128)(2,1)S(1)}, u32[]{:S(2)}, u32[]{:S(2)}) collective-permute-start(bf16[192,512]{1,0:T(8,128)(2,1)S(1)} %get-tuple-element.37), channel_id=1, source_target_pairs={{32,0},{64,32},{96,64},{128,96},{160,128},{192,160},{224,192},{0,2... | collective-permute-start | bytes 589832 | tf_op jit(solution)/shard_map/ppermute | solution.py:406
  24.2 2.2 %shard_map.96 = (bf16[512,384]{1,0:T(8,128)(2,1)S(1)}, bf16[512,128]{1,0:T(8,128)(2,1)S(1)}, bf16[512,128]{1,0:T(8,128)(2,1)S(1)}, f32[16,96,128]{2,1,0:T(8,128)...) custom-call(s32[128,12]{1,0:T(8,128)S(1)} %get-tuple-element.25.ids_ref, ...), custom_call_target="tpu_custom_call" | custom-call | flops 10000000 | bytes 1000000 | tf_op jit(solution)/shard_map/pallas_call | solution.py:441
  26.4 0.0 collective-permute-done.3.zhi
  26.4 0.0 copy-done.2
  26.4 0.0 copy-start.1
  26.4 3.0 %shard_map.97.acc_ref = f32[16,96,512]{2,1,0:T(8,128)S(1)} custom-call(bf16[16,96,512]{2,1,0:T(8,128)(2,1)S(1)} %bitcast.18, bf16[2,104,512]{2,1,0:T(8,128)(2,1)S(1)} %collective-permute-done.ylo, bf16[2,104,512]{2,1,0:T(8,128)(2,1)S(1)} %collective-permute-done.1.yhi, bf16[16,16,512]{2,1,0:T(8,128)(2,1)S(1)} %collective-permute-done.2.zlo, ...), custom_call_target="tpu_custom_call" | custom-call | flops 1000000000 | bytes 6000000 | tf_op jit(solution)/shard_map/pallas_call | solution.py:448
  29.5 0.0 collective-permute-done.4.lo_key.lo_ref
  29.5 0.0 collective-permute-done.5.hi_key.hi_ref
  29.5 0.0 copy-done.1
  29.5 3.0 %shard_map.99.prev_ref = bf16[16,392,128]{2,1,0:T(8,128)(2,1)S(1)} custom-call(f32[16,96,512]{2,1,0:T(8,128)S(1)} %shard_map.97.acc_ref, bf16[584,512]{1,0:T(8,128)(2,1)S(1)} %collective-permute-done.4.lo_key.lo_ref, bf16[584,512]{1,0:T(8,128)(2,1)S(1)} %collective-permute-done.5.hi_key.hi_ref, bf16[584,512]{1,0:T(8,128)(2,1)S(1)} %collective-permute-done.4.lo_key.lo_ref, ...), custom_call_target="tpu_custom_call" | custom-call | flops 1000000000 | bytes 4000000 | tf_op jit(solution)/shard_map/pallas_call | solution.py:453
  32.5 0.0 collective-permute-done.6.lo_ref
  32.5 0.0 collective-permute-done.7.hi_ref
  32.5 1.6 %shard_map.100 = bf16[16,392,128]{2,1,0:T(8,128)(2,1)S(1)} custom-call(f32[16,96,512]{2,1,0:T(8,128)S(1)} %shard_map.97.acc_ref, bf16[584,512]{1,0:T(8,128)(2,1)S(1)} %collective-permute-done.4.lo_key.lo_ref, bf16[584,512]{1,0:T(8,128)(2,1)S(1)} %collective-permute-done.5.hi_key.hi_ref, bf16[192,512]{1,0:T(8,128)(2,1)S(1)} %collective-permute-done.6.lo_ref, ...), custom_call_target="tpu_custom_call" | custom-call | flops 1000000000 | bytes 4000000 | tf_op jit(solution)/shard_map/pallas_call | solution.py:453
  34.2 51.1 %all_to_all.5 = bf16[64,49,2,128]{3,2,1,0:T(2,128)(2,1)S(1)} all-to-all(bf16[64,49,2,128]{3,2,1,0:T(2,128)(2,1)S(1)} %bitcast.19), channel_id=1, replica_groups=mesh['gx'=8,'gy'=4,'gz'=8] {'gx','gz'}, dimensions={0} | all-to-all | bytes 3211264 | tf_op jit(solution)/shard_map/all_to_all | solution.py:465
  85.3 2.0 %shard_map.101 = (bf16[12,128,512]{2,1,0:T(8,128)(2,1)}, s32[12,1,128]{2,1,0:T(1,128)}, s32[1,128]{1,0:T(1,128)}) custom-call(bf16[16,392,128]{2,1,0:T(8,128)(2,1)S(1)} %bitcast.20), custom_call_target="tpu_custom_call" | custom-call | flops 400000000 | bytes 4000000 | tf_op jit(solution)/shard_map/pallas_call | solution.py:466
Async XLA Ops:
  0.6 8.1 %copy-start = (bf16[2,8,8,12,512]{4,2,3,1,0:T(8,128)(2,1)S(1)}, bf16[2,8,8,12,512]{4,2,3,1,0:T(8,128)(2,1)}, u32[]{:S(2)}) copy-start(bf16[2,8,8,12,512]{4,2,3,1,0:T(8,128)(2,1)} %param.7) | copy-start | bytes 4718596
  2.1 27.3 %collective-permute-start.4 = (bf16[584,512]{1,0:T(8,128)(2,1)S(1)}, bf16[584,512]{1,0:T(8,128)(2,1)S(1)}, u32[]{:S(2)}, u32[]{:S(2)}) collective-permute-start(bf16[584,512]{1,0:T(8,128)(2,1)S(1)} %get-tuple-element.34), channel_id=1, source_target_pairs={{0,32},{32,64},{64,96},{96,128},{128,160},{160,192},{192,224},{224... | collective-permute-start | bytes 1794056 | tf_op jit(solution)/shard_map/ppermute | solution.py:403
  4.7 24.8 %collective-permute-start.5 = (bf16[584,512]{1,0:T(8,128)(2,1)S(1)}, bf16[584,512]{1,0:T(8,128)(2,1)S(1)}, u32[]{:S(2)}, u32[]{:S(2)}) collective-permute-start(bf16[584,512]{1,0:T(8,128)(2,1)S(1)} %get-tuple-element.35), channel_id=1, source_target_pairs={{32,0},{64,32},{96,64},{128,96},{160,128},{192,160},{224,192},{0,2... | collective-permute-start | bytes 1794056 | tf_op jit(solution)/shard_map/ppermute | solution.py:406
  8.7 17.7 %copy-start.2 = (f32[8,512]{1,0:T(8,128)S(1)}, f32[8,512]{1,0:T(8,128)}, u32[]{:S(2)}) copy-start(f32[8,512]{1,0:T(8,128)} %constant.4.clone.vel_ref) | copy-start | bytes 49156
  9.2 7.3 %collective-permute-start = (bf16[2,104,512]{2,1,0:T(8,128)(2,1)S(1)}, bf16[2,104,512]{2,1,0:T(8,128)(2,1)S(1)}, u32[]{:S(2)}, u32[]{:S(2)}) collective-permute-start(bf16[2,104,512]{2,1,0:T(8,128)(2,1)S(1)} %get-tuple-element.27), channel_id=1, source_target_pairs={{0,8},{8,16},{16,24},{24,0},{1,9},{9,17},{17,25},{25,1},{2,10},{10... | collective-permute-start | bytes 638984 | tf_op jit(solution)/shard_map/ppermute | solution.py:403
  10.6 11.0 %collective-permute-start.2 = (bf16[16,16,512]{2,1,0:T(8,128)(2,1)S(1)}, bf16[16,16,512]{2,1,0:T(8,128)(2,1)S(1)}, u32[]{:S(2)}, u32[]{:S(2)}) collective-permute-start(bf16[16,16,512]{2,1,0:T(8,128)(2,1)S(1)} %get-tuple-element.29), channel_id=1, source_target_pairs={{0,1},{1,2},{2,3},{3,4},{4,5},{5,6},{6,7},{7,0},{8,9},{9,10},{10,1... | collective-permute-start | bytes 786440 | tf_op jit(solution)/shard_map/ppermute | solution.py:403
  12.9 13.5 %collective-permute-start.3 = (bf16[16,16,512]{2,1,0:T(8,128)(2,1)S(1)}, bf16[16,16,512]{2,1,0:T(8,128)(2,1)S(1)}, u32[]{:S(2)}, u32[]{:S(2)}) collective-permute-start(bf16[16,16,512]{2,1,0:T(8,128)(2,1)S(1)} %get-tuple-element.30), channel_id=1, source_target_pairs={{1,0},{2,1},{3,2},{4,3},{5,4},{6,5},{7,6},{0,7},{9,8},{10,9},{11,1... | collective-permute-start | bytes 786440 | tf_op jit(solution)/shard_map/ppermute | solution.py:406
  16.5 5.1 %collective-permute-start.1 = (bf16[2,104,512]{2,1,0:T(8,128)(2,1)S(1)}, bf16[2,104,512]{2,1,0:T(8,128)(2,1)S(1)}, u32[]{:S(2)}, u32[]{:S(2)}) collective-permute-start(bf16[2,104,512]{2,1,0:T(8,128)(2,1)S(1)} %get-tuple-element.28), channel_id=1, source_target_pairs={{8,0},{16,8},{24,16},{0,24},{9,1},{17,9},{25,17},{1,25},{10,2},{18... | collective-permute-start | bytes 638984 | tf_op jit(solution)/shard_map/ppermute | solution.py:406
  21.5 11.0 %collective-permute-start.6 = (bf16[192,512]{1,0:T(8,128)(2,1)S(1)}, bf16[192,512]{1,0:T(8,128)(2,1)S(1)}, u32[]{:S(2)}, u32[]{:S(2)}) collective-permute-start(bf16[192,512]{1,0:T(8,128)(2,1)S(1)} %get-tuple-element.36), channel_id=1, source_target_pairs={{0,32},{32,64},{64,96},{96,128},{128,160},{160,192},{192,224},{224... | collective-permute-start | bytes 589832 | tf_op jit(solution)/shard_map/ppermute | solution.py:403
  21.5 11.0 %collective-permute-start.7 = (bf16[192,512]{1,0:T(8,128)(2,1)S(1)}, bf16[192,512]{1,0:T(8,128)(2,1)S(1)}, u32[]{:S(2)}, u32[]{:S(2)}) collective-permute-start(bf16[192,512]{1,0:T(8,128)(2,1)S(1)} %get-tuple-element.37), channel_id=1, source_target_pairs={{32,0},{64,32},{96,64},{128,96},{160,128},{192,160},{224,192},{0,2... | collective-permute-start | bytes 589832 | tf_op jit(solution)/shard_map/ppermute | solution.py:406
  26.4 3.1 %copy-start.1 = (bf16[512,128]{1,0:T(8,128)(2,1)S(1)}, bf16[512,128]{1,0:T(8,128)(2,1)}, u32[]{:S(2)}) copy-start(bf16[512,128]{1,0:T(8,128)(2,1)} %constant.5.clone.wts_ref) | copy-start | bytes 393220

commit v5 on v4

--- a/solution.py
+++ b/solution.py
@@ -220,11 +220,10 @@
         [
             jnp.where(outer, ids * 8.0 + (lane % 8).astype(F32), -1.0),
             centre(bx),
-            centre(by),
+            jnp.where(live, centre(by), FAR),
             centre(bz),
-            live.astype(F32),
             widen * widen / 4.0,
-            jnp.zeros((2 * TILES, LANES), F32),
+            jnp.zeros((3 * TILES, LANES), F32),
         ],
         axis=0,
     ).T
@@ -234,15 +233,16 @@
     linear = [pick((1 + d, 1.0), (8 + d, 2.0)) for d in range(3)]
     square = pick((7, 1.0))
     for i in range(TILES):
-        wide = lambda which: jnp.broadcast_to(table[:ROWS, which * TILES + i : which * TILES + i + 1], (ROWS, LANES))
+        column = lambda which, n: jnp.broadcast_to(table[:n, which * TILES + i : which * TILES + i + 1], (n, LANES))
+        wide = lambda which: column(which, ROWS)
         key_ref[i] = wide(0)
         c = [wide(1 + d) for d in range(3)]
         norm = c[0] * c[0] + c[1] * c[1] + c[2] * c[2]
         fac_ref[i] = plain + c[0] * linear[0] + c[1] * linear[1] + c[2] * linear[2] + norm * square
         cen_ref[0, i] = c[0]
-        cen_ref[1, i] = jnp.where(wide(4) > 0.0, c[1], FAR)
+        cen_ref[1, i] = c[1]
         cen_ref[2, i] = c[2]
-        widen_ref[i] = wide(5)[:8]
+        widen_ref[i] = column(4, 8)
 
 
 def final_kernel(
@@ -335,14 +335,13 @@
         out_ref[:, where, :] = out_ref[:, where, :] + jnp.where(sub < 2 * p, before[p], 0.0).astype(BF16)
 
 
-def unpack_kernel(got_ref, out_ref, ids_ref, cnt_ref, rows, sems):
+def unpack_kernel(got_ref, rows, ids_ref, cnt_ref):
     col = iota((1, 256), 1)
     phase, shifted = col // 64, (col % 8 - 2 * (col // 64) + 8) % 8
     source = col % 64 // 8 * 4 + phase
     perm = (iota((256, 256), 0) == shifted // 2 * 64 + source * 2 + shifted % 2).astype(F32).astype(BF16)
     sub = iota((1, 8, LANES), 1)
     upper = [None] + [jnp.broadcast_to((sub >= 2 * p).astype(F32).astype(BF16), (8, 8, LANES)) > 0 for p in range(1, 4)]
-    copies = []
     for t in range(3):
         for g in range(2):
             tile = lambda n: got_ref[8 * g : 8 * g + 8, 8 * n : 8 * n + 8, :]
@@ -356,8 +355,6 @@
             out = jnp.dot(perm, jnp.concatenate(lanes, axis=1), preferred_element_type=F32)
             where = (pl.ds(4 * t, 4), pl.ds(64 * g, 64))
             rows[where] = out.reshape(4, 64, VB).astype(BF16)
-            copies.append(pltpu.make_async_copy(rows.at[where], out_ref.at[where], sems.at[2 * t + g]))
-            copies[-1].start()
     col = iota((1, 512), 1)
     phase, at = col // 128, col % 8
     target = jnp.where(at // 2 == phase, (col % 128 // 8 * 4 + phase) * 2 + at % 2, -1)
@@ -366,8 +363,6 @@
     info = jnp.dot(pick, meta, preferred_element_type=F32).T.astype(jnp.int32)
     ids_ref[...] = info[:MAXB].reshape(MAXB, 1, LANES)
     cnt_ref[...] = info[MAXB : MAXB + 1]
-    for copy in copies:
-        copy.wait()
 
 
 def call(kernel, outs, scratch=(), flops=0, moved=0, vmem=16 << 20, **extra):
@@ -466,10 +461,8 @@
     moved, moved_ids, moved_counts = call(
         unpack_kernel,
         [((MAXB, LANES, VB), BF16), ((MAXB, 1, LANES), jnp.int32), ((1, LANES), jnp.int32)],
-        scratch=[pltpu.VMEM((MAXB, LANES, VB), BF16), pltpu.SemaphoreType.DMA((6,))],
         flops=4 * 10**8,
         moved=4 * 10**6,
-        out_specs=[pl.BlockSpec(memory_space=pl.ANY), whole, whole],
     )(got)
     return (
         moved.transpose(1, 0, 2).reshape(1, LANES, MAXB, VB),

time: 87.6 us -> 87 us (level)
  transfers between devices with their start and end apart: 8 -> 8, of which waited for: 2 -> 2; matrix products, arithmetic and copies ran while one was open for 0% -> 0% of each run, Pallas kernels for 11% -> 10%
where the time goes in v5:
time: 87 us; the launch traced here: 86.8 us
  blocking collectives  51.1 us (59%)
  starting transfers between devices  14.3 us (16%)
  Pallas kernels  13.8 us (16%)
  waiting for transfers between devices  6.74 us (8%)
    all_to_all x1, blocking collectives, advance(): lax.all_to_all(out, ('gx', 'gz'), split_axis=0, concat_axis=0, tiled=True)  51.1 us
    ppermute x4, starting transfers between devices, down(): return lax.ppermute(v, axis, [((i + 1) % n, i) for i in range(n)])  8.11 us
    ppermute x4, starting transfers between devices, up(): return lax.ppermute(v, axis, [(i, (i + 1) % n) for i in range(n)])  6.24 us
    pallas_call x2, Pallas kernels, advance(): call(functools.partial(final_kernel, part), [((16, 392, LANES), BF16)], s...  4.64 us
    ppermute x4, waiting for transfers between devices, up(): return lax.ppermute(v, axis, [(i, (i + 1) % n) for i in range(n)])  3.57 us
    ppermute x4, waiting for transfers between devices, down(): return lax.ppermute(v, axis, [((i + 1) % n, i) for i in range(n)])  3.17 us
    pallas_call x1, Pallas kernels, advance(): call(local_kernel, [((TILES, ROWS, VB), F32)], flops=10 ** 9, moved=6 * 1...  3.04 us
    pallas_call x1, Pallas kernels, advance(): call(route_kernel, [((512, 64 * count), BF16) for _, count in PARTS] + [(...  1.96 us
  transfers between devices with their start and end apart: 8, of which 2 were waited for; matrix products, arithmetic and copies ran while one was open for 0% of the time, Pallas kernels for 10%

profile of v5, /device:TPU:1, one launch (start us, length us, event | category | flops | bytes accessed | tf_op | source)
XLA Modules:
  0.0 86.8 jit_solution(7925825301023672308)
XLA Ops:
  0.6 0.0 copy-start
  0.6 1.5 %shard_map.94 = (bf16[584,512]{1,0:T(8,128)(2,1)S(1)}, bf16[584,512]{1,0:T(8,128)(2,1)S(1)}, s32[128,12]{1,0:T(8,128)S(1)}, s32[16,8]{1,0:T(8,128)S(1)}, s32[16,8]{1,0:T(8,128)S(1)}, /*index=5*/bf16[16,8]{1,0:T(8,128)(2,1)S(1)}) custom-call(bf16[1536,512]{1,0:T(8,128)(2,1)} %bitcast.15, s32[128,12]{1,0:T(8,128)} %bitcast.21, s32[16,8]{1,0:T(8,128)} %bitcast.22, ...), custom_call_target="tpu_custom_call" | custom-call | bytes 2000000 | tf_op jit(solution)/shard_map/pallas_call | solution.py:416
  2.1 2.5 %collective-permute-start.4 = (bf16[584,512]{1,0:T(8,128)(2,1)S(1)}, bf16[584,512]{1,0:T(8,128)(2,1)S(1)}, u32[]{:S(2)}, u32[]{:S(2)}) collective-permute-start(bf16[584,512]{1,0:T(8,128)(2,1)S(1)} %get-tuple-element.34), channel_id=1, source_target_pairs={{0,32},{32,64},{64,96},{96,128},{128,160},{160,192},{192,224},{224... | collective-permute-start | bytes 1794056 | tf_op jit(solution)/shard_map/ppermute | solution.py:398
  4.7 4.0 %collective-permute-start.5 = (bf16[584,512]{1,0:T(8,128)(2,1)S(1)}, bf16[584,512]{1,0:T(8,128)(2,1)S(1)}, u32[]{:S(2)}, u32[]{:S(2)}) collective-permute-start(bf16[584,512]{1,0:T(8,128)(2,1)S(1)} %get-tuple-element.35), channel_id=1, source_target_pairs={{32,0},{64,32},{96,64},{128,96},{160,128},{192,160},{224,192},{0,2... | collective-permute-start | bytes 1794056 | tf_op jit(solution)/shard_map/ppermute | solution.py:401
  8.7 0.0 copy-done
  8.7 0.0 copy-start.2
  8.7 0.5 shard_map.95
  9.2 1.4 %collective-permute-start = (bf16[2,104,512]{2,1,0:T(8,128)(2,1)S(1)}, bf16[2,104,512]{2,1,0:T(8,128)(2,1)S(1)}, u32[]{:S(2)}, u32[]{:S(2)}) collective-permute-start(bf16[2,104,512]{2,1,0:T(8,128)(2,1)S(1)} %get-tuple-element.27), channel_id=1, source_target_pairs={{0,8},{8,16},{16,24},{24,0},{1,9},{9,17},{17,25},{25,1},{2,10},{10... | collective-permute-start | bytes 638984 | tf_op jit(solution)/shard_map/ppermute | solution.py:398
  10.6 2.3 %collective-permute-start.2 = (bf16[16,16,512]{2,1,0:T(8,128)(2,1)S(1)}, bf16[16,16,512]{2,1,0:T(8,128)(2,1)S(1)}, u32[]{:S(2)}, u32[]{:S(2)}) collective-permute-start(bf16[16,16,512]{2,1,0:T(8,128)(2,1)S(1)} %get-tuple-element.29), channel_id=1, source_target_pairs={{0,1},{1,2},{2,3},{3,4},{4,5},{5,6},{6,7},{7,0},{8,9},{9,10},{10,1... | collective-permute-start | bytes 786440 | tf_op jit(solution)/shard_map/ppermute | solution.py:398
  12.9 0.0 collective-permute-start.3
  12.9 3.6 %collective-permute-done.ylo = bf16[2,104,512]{2,1,0:T(8,128)(2,1)S(1)} collective-permute-done((bf16[2,104,512]{2,1,0:T(8,128)(2,1)S(1)}, bf16[2,104,512]{2,1,0:T(8,128)(2,1)S(1)}, u32[]{:S(2)}, u32[]{:S(2)}) %collective-permute-start) | collective-permute-done | bytes 213024 | tf_op jit(solution)/shard_map/ppermute | solution.py:398
  16.5 1.4 %collective-permute-start.1 = (bf16[2,104,512]{2,1,0:T(8,128)(2,1)S(1)}, bf16[2,104,512]{2,1,0:T(8,128)(2,1)S(1)}, u32[]{:S(2)}, u32[]{:S(2)}) collective-permute-start(bf16[2,104,512]{2,1,0:T(8,128)(2,1)S(1)} %get-tuple-element.28), channel_id=1, source_target_pairs={{8,0},{16,8},{24,16},{0,24},{9,1},{17,9},{25,17},{1,25},{10,2},{18... | collective-permute-start | bytes 638984 | tf_op jit(solution)/shard_map/ppermute | solution.py:401
  17.9 0.5 shard_map.98
  18.4 3.2 %collective-permute-done.1.yhi = bf16[2,104,512]{2,1,0:T(8,128)(2,1)S(1)} collective-permute-done((bf16[2,104,512]{2,1,0:T(8,128)(2,1)S(1)}, bf16[2,104,512]{2,1,0:T(8,128)(2,1)S(1)}, u32[]{:S(2)}, u32[]{:S(2)}) %collective-permute-start.1) | collective-permute-done | bytes 213024 | tf_op jit(solution)/shard_map/ppermute | solution.py:401
  21.5 0.0 collective-permute-start.6
  21.5 0.0 collective-permute-done.2.zlo
  21.5 2.7 %collective-permute-start.7 = (bf16[192,512]{1,0:T(8,128)(2,1)S(1)}, bf16[192,512]{1,0:T(8,128)(2,1)S(1)}, u32[]{:S(2)}, u32[]{:S(2)}) collective-permute-start(bf16[192,512]{1,0:T(8,128)(2,1)S(1)} %get-tuple-element.37), channel_id=1, source_target_pairs={{32,0},{64,32},{96,64},{128,96},{160,128},{192,160},{224,192},{0,2... | collective-permute-start | bytes 589832 | tf_op jit(solution)/shard_map/ppermute | solution.py:401
  24.2 2.0 %shard_map.96 = (bf16[512,384]{1,0:T(8,128)(2,1)S(1)}, bf16[512,128]{1,0:T(8,128)(2,1)S(1)}, bf16[512,128]{1,0:T(8,128)(2,1)S(1)}, f32[16,96,128]{2,1,0:T(8,128)...) custom-call(s32[128,12]{1,0:T(8,128)S(1)} %get-tuple-element.25.ids_ref, ...), custom_call_target="tpu_custom_call" | custom-call | flops 10000000 | bytes 1000000 | tf_op jit(solution)/shard_map/pallas_call | solution.py:436
  26.2 0.0 collective-permute-done.3.zhi
  26.2 0.0 copy-done.2
  26.2 0.0 copy-start.1
  26.2 3.0 %shard_map.97.acc_ref = f32[16,96,512]{2,1,0:T(8,128)S(1)} custom-call(bf16[16,96,512]{2,1,0:T(8,128)(2,1)S(1)} %bitcast.18, bf16[2,104,512]{2,1,0:T(8,128)(2,1)S(1)} %collective-permute-done.ylo, bf16[2,104,512]{2,1,0:T(8,128)(2,1)S(1)} %collective-permute-done.1.yhi, bf16[16,16,512]{2,1,0:T(8,128)(2,1)S(1)} %collective-permute-done.2.zlo, ...), custom_call_target="tpu_custom_call" | custom-call | flops 1000000000 | bytes 6000000 | tf_op jit(solution)/shard_map/pallas_call | solution.py:443
  29.2 0.0 collective-permute-done.4.lo_key.lo_ref
  29.3 0.0 collective-permute-done.5.hi_key.hi_ref
  29.3 0.0 copy-done.1
  29.3 3.0 %shard_map.99.prev_ref = bf16[16,392,128]{2,1,0:T(8,128)(2,1)S(1)} custom-call(f32[16,96,512]{2,1,0:T(8,128)S(1)} %shard_map.97.acc_ref, bf16[584,512]{1,0:T(8,128)(2,1)S(1)} %collective-permute-done.4.lo_key.lo_ref, bf16[584,512]{1,0:T(8,128)(2,1)S(1)} %collective-permute-done.5.hi_key.hi_ref, bf16[584,512]{1,0:T(8,128)(2,1)S(1)} %collective-permute-done.4.lo_key.lo_ref, ...), custom_call_target="tpu_custom_call" | custom-call | flops 1000000000 | bytes 4000000 | tf_op jit(solution)/shard_map/pallas_call | solution.py:448
  32.3 0.0 collective-permute-done.6.lo_ref
  32.3 0.0 collective-permute-done.7.hi_ref
  32.3 1.6 %shard_map.100 = bf16[16,392,128]{2,1,0:T(8,128)(2,1)S(1)} custom-call(f32[16,96,512]{2,1,0:T(8,128)S(1)} %shard_map.97.acc_ref, bf16[584,512]{1,0:T(8,128)(2,1)S(1)} %collective-permute-done.4.lo_key.lo_ref, bf16[584,512]{1,0:T(8,128)(2,1)S(1)} %collective-permute-done.5.hi_key.hi_ref, bf16[192,512]{1,0:T(8,128)(2,1)S(1)} %collective-permute-done.6.lo_ref, ...), custom_call_target="tpu_custom_call" | custom-call | flops 1000000000 | bytes 4000000 | tf_op jit(solution)/shard_map/pallas_call | solution.py:448
  33.9 51.1 %all_to_all.5 = bf16[64,49,2,128]{3,2,1,0:T(2,128)(2,1)S(1)} all-to-all(bf16[64,49,2,128]{3,2,1,0:T(2,128)(2,1)S(1)} %bitcast.19), channel_id=1, replica_groups=mesh['gx'=8,'gy'=4,'gz'=8] {'gx','gz'}, dimensions={0} | all-to-all | bytes 3211264 | tf_op jit(solution)/shard_map/all_to_all | solution.py:460
  85.1 1.8 %shard_map.101 = (bf16[12,128,512]{2,1,0:T(8,128)(2,1)}, s32[12,1,128]{2,1,0:T(1,128)}, s32[1,128]{1,0:T(1,128)}) custom-call(bf16[16,392,128]{2,1,0:T(8,128)(2,1)S(1)} %bitcast.20), custom_call_target="tpu_custom_call" | custom-call | flops 400000000 | bytes 4000000 | tf_op jit(solution)/shard_map/pallas_call | solution.py:461
Async XLA Ops:
  0.6 8.1 %copy-start = (bf16[2,8,8,12,512]{4,2,3,1,0:T(8,128)(2,1)S(1)}, bf16[2,8,8,12,512]{4,2,3,1,0:T(8,128)(2,1)}, u32[]{:S(2)}) copy-start(bf16[2,8,8,12,512]{4,2,3,1,0:T(8,128)(2,1)} %param.7) | copy-start | bytes 4718596
  2.1 27.1 %collective-permute-start.4 = (bf16[584,512]{1,0:T(8,128)(2,1)S(1)}, bf16[584,512]{1,0:T(8,128)(2,1)S(1)}, u32[]{:S(2)}, u32[]{:S(2)}) collective-permute-start(bf16[584,512]{1,0:T(8,128)(2,1)S(1)} %get-tuple-element.34), channel_id=1, source_target_pairs={{0,32},{32,64},{64,96},{96,128},{128,160},{160,192},{192,224},{224... | collective-permute-start | bytes 1794056 | tf_op jit(solution)/shard_map/ppermute | solution.py:398
  4.7 24.6 %collective-permute-start.5 = (bf16[584,512]{1,0:T(8,128)(2,1)S(1)}, bf16[584,512]{1,0:T(8,128)(2,1)S(1)}, u32[]{:S(2)}, u32[]{:S(2)}) collective-permute-start(bf16[584,512]{1,0:T(8,128)(2,1)S(1)} %get-tuple-element.35), channel_id=1, source_target_pairs={{32,0},{64,32},{96,64},{128,96},{160,128},{192,160},{224,192},{0,2... | collective-permute-start | bytes 1794056 | tf_op jit(solution)/shard_map/ppermute | solution.py:401
  8.7 17.5 %copy-start.2 = (f32[8,512]{1,0:T(8,128)S(1)}, f32[8,512]{1,0:T(8,128)}, u32[]{:S(2)}) copy-start(f32[8,512]{1,0:T(8,128)} %constant.4.clone.vel_ref) | copy-start | bytes 49156
  9.2 7.3 %collective-permute-start = (bf16[2,104,512]{2,1,0:T(8,128)(2,1)S(1)}, bf16[2,104,512]{2,1,0:T(8,128)(2,1)S(1)}, u32[]{:S(2)}, u32[]{:S(2)}) collective-permute-start(bf16[2,104,512]{2,1,0:T(8,128)(2,1)S(1)} %get-tuple-element.27), channel_id=1, source_target_pairs={{0,8},{8,16},{16,24},{24,0},{1,9},{9,17},{17,25},{25,1},{2,10},{10... | collective-permute-start | bytes 638984 | tf_op jit(solution)/shard_map/ppermute | solution.py:398
  10.6 11.0 %collective-permute-start.2 = (bf16[16,16,512]{2,1,0:T(8,128)(2,1)S(1)}, bf16[16,16,512]{2,1,0:T(8,128)(2,1)S(1)}, u32[]{:S(2)}, u32[]{:S(2)}) collective-permute-start(bf16[16,16,512]{2,1,0:T(8,128)(2,1)S(1)} %get-tuple-element.29), channel_id=1, source_target_pairs={{0,1},{1,2},{2,3},{3,4},{4,5},{5,6},{6,7},{7,0},{8,9},{9,10},{10,1... | collective-permute-start | bytes 786440 | tf_op jit(solution)/shard_map/ppermute | solution.py:398
  12.9 13.3 %collective-permute-start.3 = (bf16[16,16,512]{2,1,0:T(8,128)(2,1)S(1)}, bf16[16,16,512]{2,1,0:T(8,128)(2,1)S(1)}, u32[]{:S(2)}, u32[]{:S(2)}) collective-permute-start(bf16[16,16,512]{2,1,0:T(8,128)(2,1)S(1)} %get-tuple-element.30), channel_id=1, source_target_pairs={{1,0},{2,1},{3,2},{4,3},{5,4},{6,5},{7,6},{0,7},{9,8},{10,9},{11,1... | collective-permute-start | bytes 786440 | tf_op jit(solution)/shard_map/ppermute | solution.py:401
  16.5 5.1 %collective-permute-start.1 = (bf16[2,104,512]{2,1,0:T(8,128)(2,1)S(1)}, bf16[2,104,512]{2,1,0:T(8,128)(2,1)S(1)}, u32[]{:S(2)}, u32[]{:S(2)}) collective-permute-start(bf16[2,104,512]{2,1,0:T(8,128)(2,1)S(1)} %get-tuple-element.28), channel_id=1, source_target_pairs={{8,0},{16,8},{24,16},{0,24},{9,1},{17,9},{25,17},{1,25},{10,2},{18... | collective-permute-start | bytes 638984 | tf_op jit(solution)/shard_map/ppermute | solution.py:401
  21.5 10.8 %collective-permute-start.6 = (bf16[192,512]{1,0:T(8,128)(2,1)S(1)}, bf16[192,512]{1,0:T(8,128)(2,1)S(1)}, u32[]{:S(2)}, u32[]{:S(2)}) collective-permute-start(bf16[192,512]{1,0:T(8,128)(2,1)S(1)} %get-tuple-element.36), channel_id=1, source_target_pairs={{0,32},{32,64},{64,96},{96,128},{128,160},{160,192},{192,224},{224... | collective-permute-start | bytes 589832 | tf_op jit(solution)/shard_map/ppermute | solution.py:398
  21.5 10.8 %collective-permute-start.7 = (bf16[192,512]{1,0:T(8,128)(2,1)S(1)}, bf16[192,512]{1,0:T(8,128)(2,1)S(1)}, u32[]{:S(2)}, u32[]{:S(2)}) collective-permute-start(bf16[192,512]{1,0:T(8,128)(2,1)S(1)} %get-tuple-element.37), channel_id=1, source_target_pairs={{32,0},{64,32},{96,64},{128,96},{160,128},{192,160},{224,192},{0,2... | collective-permute-start | bytes 589832 | tf_op jit(solution)/shard_map/ppermute | solution.py:401
  26.2 3.1 %copy-start.1 = (bf16[512,128]{1,0:T(8,128)(2,1)S(1)}, bf16[512,128]{1,0:T(8,128)(2,1)}, u32[]{:S(2)}) copy-start(bf16[512,128]{1,0:T(8,128)(2,1)} %constant.5.clone.wts_ref) | copy-start | bytes 393220

commit v6 on v5

--- a/solution.py
+++ b/solution.py
@@ -16,7 +16,7 @@
 EDGE = NV1 // BLK
 VB = BLK**3
 TILES = 16
-PARTS = ((0, 6), (6, 2))
+PARTS = ((0, 5), (5, 3))
 ROWS = MAXB * 8
 LANES = 128
 STEP_COEFF = 0.6
@@ -285,14 +285,14 @@
         per = 1.0 / mass
         u = [(at(1 + d) + at(4 + d)) * per for d in range(3)]
         energy = at(7) + at(8) + at(9) + at(10) + at(11)
-        warm = (energy * per - (u[0] * u[0] + u[1] * u[1] + u[2] * u[2])) / 3.0
+        warm = (energy * per - (u[0] * u[0] + u[1] * u[1] + u[2] * u[2])) * (1.0 / 3.0)
         widen = widen_ref[x * 8 + start : x * 8 + start + count]
         aim = warm * widen.reshape(cells, LANES)[:, :1]
         rate = 1.0 - jnp.exp(-IMPACT_KIND * (mass / VB) * jnp.sqrt(warm))
-        area = 2.0 * math.pi * aim
-        scale = rate * mass / (area * jnp.sqrt(area))
-        sharp = 0.5 * math.log2(math.e) / aim
-        for k, v in enumerate((u[0], u[1], u[2], -sharp, jnp.sqrt(sharp), scale, 1.0 - rate)):
+        narrow = lax.rsqrt(aim)
+        root = math.sqrt(0.5 * math.log2(math.e)) * narrow
+        scale = rate * (mass * (2.0 * math.pi) ** -1.5) * (narrow * narrow * narrow)
+        for k, v in enumerate((u[0], u[1], u[2], -(root * root), root, scale, 1.0 - rate)):
             cell_ref[k, mine] = jnp.broadcast_to(v, (cells, LANES)).reshape(count, 8, LANES)
 
     def collide(t, x, y):

time: 87 us -> 82.8 us (0.952)
  blocking collectives: 51.1 us -> 49 us
  waiting for transfers between devices: 6.74 us -> 5.13 us
    ppermute x4, waiting for transfers between devices: 3.57 us -> 0.01 us  [up(): return lax.ppermute(v, axis, [(i, (i + 1) % n) for i in range(n)])]
    all_to_all x1, blocking collectives: 51.1 us -> 49 us  [advance(): lax.all_to_all(out, ('gx', 'gz'), split_axis=0, concat_axis=0, tiled=True)]
    ppermute x4, waiting for transfers between devices: 3.17 us -> 5.12 us  [down(): return lax.ppermute(v, axis, [((i + 1) % n, i) for i in range(n)])]
  transfers between devices with their start and end apart: 8 -> 8, of which waited for: 2 -> 1; matrix products, arithmetic and copies ran while one was open for 0% -> 0% of each run, Pallas kernels for 10% -> 9%
where the time goes in v6:
time: 82.8 us; the launch traced here: 82.6 us
  blocking collectives  49 us (59%)
  starting transfers between devices  14.2 us (17%)
  Pallas kernels  13.2 us (16%)
  waiting for transfers between devices  5.13 us (6%)
    all_to_all x1, blocking collectives, advance(): lax.all_to_all(out, ('gx', 'gz'), split_axis=0, concat_axis=0, tiled=True)  49 us
    ppermute x4, starting transfers between devices, down(): return lax.ppermute(v, axis, [((i + 1) % n, i) for i in range(n)])  8 us
    ppermute x4, starting transfers between devices, up(): return lax.ppermute(v, axis, [(i, (i + 1) % n) for i in range(n)])  6.16 us
    ppermute x4, waiting for transfers between devices, down(): return lax.ppermute(v, axis, [((i + 1) % n, i) for i in range(n)])  5.12 us
    pallas_call x2, Pallas kernels, advance(): call(functools.partial(final_kernel, part), [((16, 392, LANES), BF16)], s...  4.39 us
    pallas_call x1, Pallas kernels, advance(): call(local_kernel, [((TILES, ROWS, VB), F32)], flops=10 ** 9, moved=6 * 1...  3.05 us
    pallas_call x1, Pallas kernels, advance(): call(route_kernel, [((512, 64 * count), BF16) for _, count in PARTS] + [(...  2 us
    pallas_call x1, Pallas kernels, advance(): call(unpack_kernel, [((MAXB, LANES, VB), BF16), ((MAXB, 1, LANES), jnp.in...  1.75 us
  transfers between devices with their start and end apart: 8, of which 1 were waited for; matrix products, arithmetic and copies ran while one was open for 0% of the time, Pallas kernels for 9%

profile of v6, /device:TPU:1, one launch (start us, length us, event | category | flops | bytes accessed | tf_op | source)
XLA Modules:
  0.0 82.6 jit_solution(7549873529481929872)
XLA Ops:
  0.6 0.0 copy-start
  0.6 1.4 %shard_map.94 = (bf16[488,512]{1,0:T(8,128)(2,1)S(1)}, bf16[488,512]{1,0:T(8,128)(2,1)S(1)}, s32[128,12]{1,0:T(8,128)S(1)}, s32[16,8]{1,0:T(8,128)S(1)}, s32[16,8]{1,0:T(8,128)S(1)}, /*index=5*/bf16[16,8]{1,0:T(8,128)(2,1)S(1)}) custom-call(bf16[1536,512]{1,0:T(8,128)(2,1)} %bitcast.15, s32[128,12]{1,0:T(8,128)} %bitcast.21, s32[16,8]{1,0:T(8,128)} %bitcast.22, ...), custom_call_target="tpu_custom_call" | custom-call | bytes 2000000 | tf_op jit(solution)/shard_map/pallas_call | solution.py:416
  2.1 0.3 copy-done
  2.4 0.0 copy-start.2
  2.4 0.5 shard_map.95
  2.9 2.2 %collective-permute-start = (bf16[2,104,512]{2,1,0:T(8,128)(2,1)S(1)}, bf16[2,104,512]{2,1,0:T(8,128)(2,1)S(1)}, u32[]{:S(2)}, u32[]{:S(2)}) collective-permute-start(bf16[2,104,512]{2,1,0:T(8,128)(2,1)S(1)} %get-tuple-element.27), channel_id=1, source_target_pairs={{0,8},{8,16},{16,24},{24,0},{1,9},{9,17},{17,25},{25,1},{2,10},{10... | collective-permute-start | bytes 638984 | tf_op jit(solution)/shard_map/ppermute | solution.py:398
  5.1 1.6 %collective-permute-start.4 = (bf16[488,512]{1,0:T(8,128)(2,1)S(1)}, bf16[488,512]{1,0:T(8,128)(2,1)S(1)}, u32[]{:S(2)}, u32[]{:S(2)}) collective-permute-start(bf16[488,512]{1,0:T(8,128)(2,1)S(1)} %get-tuple-element.34), channel_id=1, source_target_pairs={{0,32},{32,64},{64,96},{96,128},{128,160},{160,192},{192,224},{224... | collective-permute-start | bytes 1499144 | tf_op jit(solution)/shard_map/ppermute | solution.py:398
  6.7 3.9 %collective-permute-start.5 = (bf16[488,512]{1,0:T(8,128)(2,1)S(1)}, bf16[488,512]{1,0:T(8,128)(2,1)S(1)}, u32[]{:S(2)}, u32[]{:S(2)}) collective-permute-start(bf16[488,512]{1,0:T(8,128)(2,1)S(1)} %get-tuple-element.35), channel_id=1, source_target_pairs={{32,0},{64,32},{96,64},{128,96},{160,128},{192,160},{224,192},{0,2... | collective-permute-start | bytes 1499144 | tf_op jit(solution)/shard_map/ppermute | solution.py:401
  10.7 2.3 %collective-permute-start.2 = (bf16[16,16,512]{2,1,0:T(8,128)(2,1)S(1)}, bf16[16,16,512]{2,1,0:T(8,128)(2,1)S(1)}, u32[]{:S(2)}, u32[]{:S(2)}) collective-permute-start(bf16[16,16,512]{2,1,0:T(8,128)(2,1)S(1)} %get-tuple-element.29), channel_id=1, source_target_pairs={{0,1},{1,2},{2,3},{3,4},{4,5},{5,6},{6,7},{7,0},{8,9},{9,10},{10,1... | collective-permute-start | bytes 786440 | tf_op jit(solution)/shard_map/ppermute | solution.py:398
  13.0 1.4 %collective-permute-start.1 = (bf16[2,104,512]{2,1,0:T(8,128)(2,1)S(1)}, bf16[2,104,512]{2,1,0:T(8,128)(2,1)S(1)}, u32[]{:S(2)}, u32[]{:S(2)}) collective-permute-start(bf16[2,104,512]{2,1,0:T(8,128)(2,1)S(1)} %get-tuple-element.28), channel_id=1, source_target_pairs={{8,0},{16,8},{24,16},{0,24},{9,1},{17,9},{25,17},{1,25},{10,2},{18... | collective-permute-start | bytes 638984 | tf_op jit(solution)/shard_map/ppermute | solution.py:401
  14.4 0.0 collective-permute-done.ylo
  14.4 0.0 collective-permute-start.3
  14.4 0.1 shard_map.98
  14.5 5.1 %collective-permute-done.1.yhi = bf16[2,104,512]{2,1,0:T(8,128)(2,1)S(1)} collective-permute-done((bf16[2,104,512]{2,1,0:T(8,128)(2,1)S(1)}, bf16[2,104,512]{2,1,0:T(8,128)(2,1)S(1)}, u32[]{:S(2)}, u32[]{:S(2)}) %collective-permute-start.1) | collective-permute-done | bytes 213024 | tf_op jit(solution)/shard_map/ppermute | solution.py:401
  19.6 0.0 collective-permute-start.6
  19.6 0.0 collective-permute-done.2.zlo
  19.6 2.7 %collective-permute-start.7 = (bf16[288,512]{1,0:T(8,128)(2,1)S(1)}, bf16[288,512]{1,0:T(8,128)(2,1)S(1)}, u32[]{:S(2)}, u32[]{:S(2)}) collective-permute-start(bf16[288,512]{1,0:T(8,128)(2,1)S(1)} %get-tuple-element.37), channel_id=1, source_target_pairs={{32,0},{64,32},{96,64},{128,96},{160,128},{192,160},{224,192},{0,2... | collective-permute-start | bytes 884744 | tf_op jit(solution)/shard_map/ppermute | solution.py:401
  22.3 2.0 %shard_map.96 = (bf16[512,320]{1,0:T(8,128)(2,1)S(1)}, bf16[512,192]{1,0:T(8,128)(2,1)S(1)}, bf16[512,128]{1,0:T(8,128)(2,1)S(1)}, f32[16,96,128]{2,1,0:T(8,128)...) custom-call(s32[128,12]{1,0:T(8,128)S(1)} %get-tuple-element.25.ids_ref, ...), custom_call_target="tpu_custom_call" | custom-call | flops 10000000 | bytes 1000000 | tf_op jit(solution)/shard_map/pallas_call | solution.py:436
  24.3 0.0 collective-permute-done.3.zhi
  24.3 0.0 copy-done.2
  24.3 0.0 copy-start.1
  24.4 3.1 %shard_map.97.acc_ref = f32[16,96,512]{2,1,0:T(8,128)S(1)} custom-call(bf16[16,96,512]{2,1,0:T(8,128)(2,1)S(1)} %bitcast.18, bf16[2,104,512]{2,1,0:T(8,128)(2,1)S(1)} %collective-permute-done.ylo, bf16[2,104,512]{2,1,0:T(8,128)(2,1)S(1)} %collective-permute-done.1.yhi, bf16[16,16,512]{2,1,0:T(8,128)(2,1)S(1)} %collective-permute-done.2.zlo, ...), custom_call_target="tpu_custom_call" | custom-call | flops 1000000000 | bytes 6000000 | tf_op jit(solution)/shard_map/pallas_call | solution.py:443
  27.4 0.0 collective-permute-done.4.lo_key.lo_ref
  27.4 0.0 collective-permute-done.5.hi_key.hi_ref
  27.4 0.0 copy-done.1
  27.4 2.5 %shard_map.99.prev_ref = bf16[16,392,128]{2,1,0:T(8,128)(2,1)S(1)} custom-call(f32[16,96,512]{2,1,0:T(8,128)S(1)} %shard_map.97.acc_ref, bf16[488,512]{1,0:T(8,128)(2,1)S(1)} %collective-permute-done.4.lo_key.lo_ref, bf16[488,512]{1,0:T(8,128)(2,1)S(1)} %collective-permute-done.5.hi_key.hi_ref, bf16[488,512]{1,0:T(8,128)(2,1)S(1)} %collective-permute-done.4.lo_key.lo_ref, ...), custom_call_target="tpu_custom_call" | custom-call | flops 1000000000 | bytes 4000000 | tf_op jit(solution)/shard_map/pallas_call | solution.py:448
  29.9 0.0 collective-permute-done.6.lo_ref
  29.9 0.0 collective-permute-done.7.hi_ref
  30.0 1.9 %shard_map.100 = bf16[16,392,128]{2,1,0:T(8,128)(2,1)S(1)} custom-call(f32[16,96,512]{2,1,0:T(8,128)S(1)} %shard_map.97.acc_ref, bf16[488,512]{1,0:T(8,128)(2,1)S(1)} %collective-permute-done.4.lo_key.lo_ref, bf16[488,512]{1,0:T(8,128)(2,1)S(1)} %collective-permute-done.5.hi_key.hi_ref, bf16[288,512]{1,0:T(8,128)(2,1)S(1)} %collective-permute-done.6.lo_ref, ...), custom_call_target="tpu_custom_call" | custom-call | flops 1000000000 | bytes 4000000 | tf_op jit(solution)/shard_map/pallas_call | solution.py:448
  31.9 49.0 %all_to_all.5 = bf16[64,49,2,128]{3,2,1,0:T(2,128)(2,1)S(1)} all-to-all(bf16[64,49,2,128]{3,2,1,0:T(2,128)(2,1)S(1)} %bitcast.19), channel_id=1, replica_groups=mesh['gx'=8,'gy'=4,'gz'=8] {'gx','gz'}, dimensions={0} | all-to-all | bytes 3211264 | tf_op jit(solution)/shard_map/all_to_all | solution.py:460
  80.9 1.7 %shard_map.101 = (bf16[12,128,512]{2,1,0:T(8,128)(2,1)}, s32[12,1,128]{2,1,0:T(1,128)}, s32[1,128]{1,0:T(1,128)}) custom-call(bf16[16,392,128]{2,1,0:T(8,128)(2,1)S(1)} %bitcast.20), custom_call_target="tpu_custom_call" | custom-call | flops 400000000 | bytes 4000000 | tf_op jit(solution)/shard_map/pallas_call | solution.py:461
Async XLA Ops:
  0.6 1.8 %copy-start = (bf16[2,8,8,12,512]{4,2,3,1,0:T(8,128)(2,1)S(1)}, bf16[2,8,8,12,512]{4,2,3,1,0:T(8,128)(2,1)}, u32[]{:S(2)}) copy-start(bf16[2,8,8,12,512]{4,2,3,1,0:T(8,128)(2,1)} %param.7) | copy-start | bytes 4718596
  2.4 21.9 %copy-start.2 = (f32[8,512]{1,0:T(8,128)S(1)}, f32[8,512]{1,0:T(8,128)}, u32[]{:S(2)}) copy-start(f32[8,512]{1,0:T(8,128)} %constant.4.clone.vel_ref) | copy-start | bytes 49156
  2.9 11.5 %collective-permute-start = (bf16[2,104,512]{2,1,0:T(8,128)(2,1)S(1)}, bf16[2,104,512]{2,1,0:T(8,128)(2,1)S(1)}, u32[]{:S(2)}, u32[]{:S(2)}) collective-permute-start(bf16[2,104,512]{2,1,0:T(8,128)(2,1)S(1)} %get-tuple-element.27), channel_id=1, source_target_pairs={{0,8},{8,16},{16,24},{24,0},{1,9},{9,17},{17,25},{25,1},{2,10},{10... | collective-permute-start | bytes 638984 | tf_op jit(solution)/shard_map/ppermute | solution.py:398
  5.1 22.3 %collective-permute-start.4 = (bf16[488,512]{1,0:T(8,128)(2,1)S(1)}, bf16[488,512]{1,0:T(8,128)(2,1)S(1)}, u32[]{:S(2)}, u32[]{:S(2)}) collective-permute-start(bf16[488,512]{1,0:T(8,128)(2,1)S(1)} %get-tuple-element.34), channel_id=1, source_target_pairs={{0,32},{32,64},{64,96},{96,128},{128,160},{160,192},{192,224},{224... | collective-permute-start | bytes 1499144 | tf_op jit(solution)/shard_map/ppermute | solution.py:398
  6.7 20.7 %collective-permute-start.5 = (bf16[488,512]{1,0:T(8,128)(2,1)S(1)}, bf16[488,512]{1,0:T(8,128)(2,1)S(1)}, u32[]{:S(2)}, u32[]{:S(2)}) collective-permute-start(bf16[488,512]{1,0:T(8,128)(2,1)S(1)} %get-tuple-element.35), channel_id=1, source_target_pairs={{32,0},{64,32},{96,64},{128,96},{160,128},{192,160},{224,192},{0,2... | collective-permute-start | bytes 1499144 | tf_op jit(solution)/shard_map/ppermute | solution.py:401
  10.7 9.0 %collective-permute-start.2 = (bf16[16,16,512]{2,1,0:T(8,128)(2,1)S(1)}, bf16[16,16,512]{2,1,0:T(8,128)(2,1)S(1)}, u32[]{:S(2)}, u32[]{:S(2)}) collective-permute-start(bf16[16,16,512]{2,1,0:T(8,128)(2,1)S(1)} %get-tuple-element.29), channel_id=1, source_target_pairs={{0,1},{1,2},{2,3},{3,4},{4,5},{5,6},{6,7},{7,0},{8,9},{9,10},{10,1... | collective-permute-start | bytes 786440 | tf_op jit(solution)/shard_map/ppermute | solution.py:398
  13.0 6.6 %collective-permute-start.1 = (bf16[2,104,512]{2,1,0:T(8,128)(2,1)S(1)}, bf16[2,104,512]{2,1,0:T(8,128)(2,1)S(1)}, u32[]{:S(2)}, u32[]{:S(2)}) collective-permute-start(bf16[2,104,512]{2,1,0:T(8,128)(2,1)S(1)} %get-tuple-element.28), channel_id=1, source_target_pairs={{8,0},{16,8},{24,16},{0,24},{9,1},{17,9},{25,17},{1,25},{10,2},{18... | collective-permute-start | bytes 638984 | tf_op jit(solution)/shard_map/ppermute | solution.py:401
  14.4 9.9 %collective-permute-start.3 = (bf16[16,16,512]{2,1,0:T(8,128)(2,1)S(1)}, bf16[16,16,512]{2,1,0:T(8,128)(2,1)S(1)}, u32[]{:S(2)}, u32[]{:S(2)}) collective-permute-start(bf16[16,16,512]{2,1,0:T(8,128)(2,1)S(1)} %get-tuple-element.30), channel_id=1, source_target_pairs={{1,0},{2,1},{3,2},{4,3},{5,4},{6,5},{7,6},{0,7},{9,8},{10,9},{11,1... | collective-permute-start | bytes 786440 | tf_op jit(solution)/shard_map/ppermute | solution.py:401
  19.6 10.3 %collective-permute-start.6 = (bf16[288,512]{1,0:T(8,128)(2,1)S(1)}, bf16[288,512]{1,0:T(8,128)(2,1)S(1)}, u32[]{:S(2)}, u32[]{:S(2)}) collective-permute-start(bf16[288,512]{1,0:T(8,128)(2,1)S(1)} %get-tuple-element.36), channel_id=1, source_target_pairs={{0,32},{32,64},{64,96},{96,128},{128,160},{160,192},{192,224},{224... | collective-permute-start | bytes 884744 | tf_op jit(solution)/shard_map/ppermute | solution.py:398
  19.6 10.3 %collective-permute-start.7 = (bf16[288,512]{1,0:T(8,128)(2,1)S(1)}, bf16[288,512]{1,0:T(8,128)(2,1)S(1)}, u32[]{:S(2)}, u32[]{:S(2)}) collective-permute-start(bf16[288,512]{1,0:T(8,128)(2,1)S(1)} %get-tuple-element.37), channel_id=1, source_target_pairs={{32,0},{64,32},{96,64},{128,96},{160,128},{192,160},{224,192},{0,2... | collective-permute-start | bytes 884744 | tf_op jit(solution)/shard_map/ppermute | solution.py:401
  24.3 3.1 %copy-start.1 = (bf16[512,128]{1,0:T(8,128)(2,1)S(1)}, bf16[512,128]{1,0:T(8,128)(2,1)}, u32[]{:S(2)}) copy-start(bf16[512,128]{1,0:T(8,128)(2,1)} %constant.5.clone.wts_ref) | copy-start | bytes 393220
